TPU v7x, 512 devices: a whole 4x4x16 slice. The times are simulated.
512 devices in a mesh: doc: 16 (over y_lo, x, core), blk: 32 (over y_hi, z).
Axes of the slice: x: 4, y: 4 (y_hi: 2, y_lo: 2; y = y_hi * 2 + y_lo), z: 16, core: 2. Of those that a mesh axis runs over, the one named last changes fastest.
Arguments:
- query_rows: bfloat16 [256, 98304], P('blk', 'doc'), may hold values from -6 to 6
- row_values: bfloat16 [16, 32, 32, 128, 256], P('doc', 'blk'), may hold values from -0.25 to 0.25
- row_slots: int32 [16, 32, 32, 128], P('doc', 'blk'), may hold values from 0 to 49151, as said below
- row_counts: int32 [16, 32, 32], P('doc', 'blk'), may hold values from 16 to 128, as said below
Outputs:
- gram: float32 [256, 65536], P('doc', 'blk')
Inputs may be any that keep to these rules, and one draw needn't show every extreme that they name: row_slots[d, s, o, j] = (s * 192 + e) * 8 + b for a document e of source s's 192 and a feature block b of owner o; the 128 entries of one (d, s, o) are distinct. Slots j >= row_counts[d, s, o] carry no data; for every d some owner receives 128 rows from every source.
All inputs are finite; a program needn't handle non-finite values.
Results may differ from a plain program's by a relative error of at most 0.0003.
Values may be sent and summed in bfloat16 or wider, within the bound.
No kernel may reach another device: no remote copies, remote signals or barrier semaphores. Data moves between devices by JAX's collectives and lax.ppermute only.
A program may use at most 192 MiB of HBM per device.

v0:
```python
import jax
import jax.numpy as jnp
from jax import lax
from jax.sharding import PartitionSpec as P

F = 65536
BW = 256


def per_device(query_rows, row_values, row_slots, row_counts):
    owners = lax.axis_size("blk")
    doc_count = query_rows.shape[1]
    own_width = F // owners
    per_owner = own_width // BW
    places = row_slots.shape[3]
    live_slot = jnp.arange(places, dtype=jnp.int32)[None, None, None, :] < row_counts[:, :, :, None]
    targets = jnp.where(live_slot, row_slots, doc_count * per_owner)
    got_values, got_targets = (
        lax.all_to_all(row_values, "blk", split_axis=2, concat_axis=2, tiled=True),
        lax.all_to_all(targets, "blk", split_axis=2, concat_axis=2, tiled=True),
    )
    flat_values = got_values.reshape(-1, BW)
    flat_targets = got_targets.reshape(-1)
    live_rows = flat_targets < doc_count * per_owner
    doc_of = jnp.where(live_rows, flat_targets // per_owner, doc_count).astype(jnp.int32)
    block_of = flat_targets % per_owner
    block_ids = jnp.arange(per_owner, dtype=jnp.int32)
    gathered = lax.all_gather(query_rows, "blk", axis=0, tiled=True)
    safe_doc = jnp.minimum(doc_of, doc_count - 1)
    picked_queries = jnp.take(gathered, safe_doc, axis=1)

    def block_tile(block):
        keep = (live_rows & (block_of == block))[:, None]
        masked = jnp.where(keep, flat_values, jnp.zeros_like(flat_values))
        return jnp.dot(picked_queries, masked, preferred_element_type=jnp.float32)

    tiles = lax.map(block_tile, block_ids)
    partial_value = tiles.transpose(1, 0, 2).reshape(gathered.shape[0], own_width)
    return lax.psum_scatter(partial_value, "doc", scatter_dimension=0, tiled=True)


def solution(mesh):
    in_specs = (
        P("blk", "doc"),
        P("doc", "blk", None, None, None),
        P("doc", "blk", None, None),
        P("doc", "blk", None),
    )
    out_specs = P("doc", "blk")
    return jax.shard_map(
        per_device, mesh=mesh, in_specs=in_specs, out_specs=out_specs, check_vma=False
    )
```

profile of v0, /device:TPU:1, one launch (start us, length us, event | category | flops | bytes accessed | tf_op | source)
XLA Modules:
  0.0 377.2 jit_solution(15423100263397606264)
XLA Ops:
  6.5 0.8 compare_select_fusion.2
  7.4 32.1 %all_to_all.10 = s32[1,1,32,128]{3,1,0,2:T(1,128)S(1)} all-to-all(s32[1,1,32,128]{3,1,0,2:T(1,128)S(1)} %compare_select_fusion.2), channel_id=1, replica_groups=mesh['doc'=16,'blk'=32] {'blk'}, dimensions={2} | all-to-all | bytes 32768 | tf_op jit(solution)/shard_map/all_to_all | solution.py:20
  39.5 4.8 %all-to-all-start.1 = ((bf16[1,1,32,128,256]{4,3,1,0,2:T(8,128)(2,1)}), bf16[1,1,32,128,256]{4,3,1,0,2:T(8,128)(2,1)}, u32[]{:S(2)}, u32[]{:S(2)}) async-start(bf16[1,1,32,128,256]{4,3,1,0,2:T(8,128)(2,1)} %bitcast.35), calls=%async_computation.1 | async-start | bytes 4194304 | tf_op jit(solution)/shard_map/all_to_all | solution.py:19
  45.2 179.3 %all-gather.2.cloned.1.call-done = bf16[256,6144]{1,0:T(8,128)(2,1)} async-done(((bf16[8,6144]{1,0:T(8,128)(2,1)}), bf16[256,6144]{1,0:T(8,128)(2,1)}) %all-gather.2.cloned.1.call-update) | async-done | bytes 3145744 | tf_op jit(solution)/shard_map/all_gather | solution.py:28
  224.6 3.2 copy.10
  227.7 16.9 %gather_fusion = bf16[4096,256]{1,0:T(8,128)(2,1)} fusion(bf16[256,6144]{0,1:T(8,128)(2,1)S(1)} %copy.10, s32[4096]{0:T(1024)S(1)} %broadcast_clamp_fusion), kind=kCustom, calls=%fused_computation | custom fusion | bytes 4210688 | tf_op jit(solution)/shard_map/jit(_take)/gather | solution.py:30
  244.7 1.9 select_bitcast_fusion
  246.6 2.9 copy.11
  249.6 45.3 %while.10 = (s32[]{:T(128)}, f32[8,256,256]{1,2,0:T(8,128)}, s32[8]{0:T(128)S(1)}, s32[4096]{0:T(1024)S(1)}, pred[4096]{0:T(1024)(128)(4,1)S(1)}, /*index=5*/bf1...) while((s32[]{:T(128)}, f32[8,256,256]{1,2,0:T(8,128)}, s32[8]{0:T(128)S(1)}, s32[4096]{0:T(1024)S(1)}, ...), condition=%wide.region_1.2_spmd, body=%wide.region_0.1_spmd.sunk | while | flops 537927680 | bytes 4485733 | solution.py:37
  250.2 0.7 compare_and_fusion.3
  250.9 4.3 %fusion.21 = f32[8,256,256]{1,2,0:T(8,128)} fusion(f32[8,256,256]{1,2,0:T(8,128)} %get-tuple-element.125, s32[]{:T(128)} %get-tuple-element.124, bf16[256,4096]{1,0:T(8,128)(2,1)} %get-tuple-element.138, bf16[4096,256]{1,0:T(8,128)(2,1)} %get-tuple-element.137, pred[4096]{0:T(1024)(128)(4,1)S(1)} %compare_and_fusion.3), kind=kOutput, calls=%fused_computation.5.clone.1 | convolution fusion | flops 537919488 | bytes 4461056 | tf_op jit(solution)/shard_map/while/body/eval_jaxpr/dot_general | solution.py:35
  255.9 0.7 compare_and_fusion.3
  256.6 4.3 %fusion.21 = f32[8,256,256]{1,2,0:T(8,128)} fusion(f32[8,256,256]{1,2,0:T(8,128)} %get-tuple-element.125, s32[]{:T(128)} %get-tuple-element.124, bf16[256,4096]{1,0:T(8,128)(2,1)} %get-tuple-element.138, bf16[4096,256]{1,0:T(8,128)(2,1)} %get-tuple-element.137, pred[4096]{0:T(1024)(128)(4,1)S(1)} %compare_and_fusion.3), kind=kOutput, calls=%fused_computation.5.clone.1 | convolution fusion | flops 537919488 | bytes 4461056 | tf_op jit(solution)/shard_map/while/body/eval_jaxpr/dot_general | solution.py:35
  261.6 0.7 compare_and_fusion.3
  262.3 4.3 %fusion.21 = f32[8,256,256]{1,2,0:T(8,128)} fusion(f32[8,256,256]{1,2,0:T(8,128)} %get-tuple-element.125, s32[]{:T(128)} %get-tuple-element.124, bf16[256,4096]{1,0:T(8,128)(2,1)} %get-tuple-element.138, bf16[4096,256]{1,0:T(8,128)(2,1)} %get-tuple-element.137, pred[4096]{0:T(1024)(128)(4,1)S(1)} %compare_and_fusion.3), kind=kOutput, calls=%fused_computation.5.clone.1 | convolution fusion | flops 537919488 | bytes 4461056 | tf_op jit(solution)/shard_map/while/body/eval_jaxpr/dot_general | solution.py:35
  267.2 0.7 compare_and_fusion.3
  267.9 4.3 %fusion.21 = f32[8,256,256]{1,2,0:T(8,128)} fusion(f32[8,256,256]{1,2,0:T(8,128)} %get-tuple-element.125, s32[]{:T(128)} %get-tuple-element.124, bf16[256,4096]{1,0:T(8,128)(2,1)} %get-tuple-element.138, bf16[4096,256]{1,0:T(8,128)(2,1)} %get-tuple-element.137, pred[4096]{0:T(1024)(128)(4,1)S(1)} %compare_and_fusion.3), kind=kOutput, calls=%fused_computation.5.clone.1 | convolution fusion | flops 537919488 | bytes 4461056 | tf_op jit(solution)/shard_map/while/body/eval_jaxpr/dot_general | solution.py:35
  272.9 0.7 compare_and_fusion.3
  273.6 4.3 %fusion.21 = f32[8,256,256]{1,2,0:T(8,128)} fusion(f32[8,256,256]{1,2,0:T(8,128)} %get-tuple-element.125, s32[]{:T(128)} %get-tuple-element.124, bf16[256,4096]{1,0:T(8,128)(2,1)} %get-tuple-element.138, bf16[4096,256]{1,0:T(8,128)(2,1)} %get-tuple-element.137, pred[4096]{0:T(1024)(128)(4,1)S(1)} %compare_and_fusion.3), kind=kOutput, calls=%fused_computation.5.clone.1 | convolution fusion | flops 537919488 | bytes 4461056 | tf_op jit(solution)/shard_map/while/body/eval_jaxpr/dot_general | solution.py:35
  279.2 4.3 %fusion.21 = f32[8,256,256]{1,2,0:T(8,128)} fusion(f32[8,256,256]{1,2,0:T(8,128)} %get-tuple-element.125, s32[]{:T(128)} %get-tuple-element.124, bf16[256,4096]{1,0:T(8,128)(2,1)} %get-tuple-element.138, bf16[4096,256]{1,0:T(8,128)(2,1)} %get-tuple-element.137, pred[4096]{0:T(1024)(128)(4,1)S(1)} %compare_and_fusion.3), kind=kOutput, calls=%fused_computation.5.clone.1 | convolution fusion | flops 537919488 | bytes 4461056 | tf_op jit(solution)/shard_map/while/body/eval_jaxpr/dot_general | solution.py:35
  284.9 4.3 %fusion.21 = f32[8,256,256]{1,2,0:T(8,128)} fusion(f32[8,256,256]{1,2,0:T(8,128)} %get-tuple-element.125, s32[]{:T(128)} %get-tuple-element.124, bf16[256,4096]{1,0:T(8,128)(2,1)} %get-tuple-element.138, bf16[4096,256]{1,0:T(8,128)(2,1)} %get-tuple-element.137, pred[4096]{0:T(1024)(128)(4,1)S(1)} %compare_and_fusion.3), kind=kOutput, calls=%fused_computation.5.clone.1 | convolution fusion | flops 537919488 | bytes 4461056 | tf_op jit(solution)/shard_map/while/body/eval_jaxpr/dot_general | solution.py:35
  290.6 4.3 %fusion.21 = f32[8,256,256]{1,2,0:T(8,128)} fusion(f32[8,256,256]{1,2,0:T(8,128)} %get-tuple-element.125, s32[]{:T(128)} %get-tuple-element.124, bf16[256,4096]{1,0:T(8,128)(2,1)} %get-tuple-element.138, bf16[4096,256]{1,0:T(8,128)(2,1)} %get-tuple-element.137, pred[4096]{0:T(1024)(128)(4,1)S(1)} %compare_and_fusion.3), kind=kOutput, calls=%fused_computation.5.clone.1 | convolution fusion | flops 537919488 | bytes 4461056 | tf_op jit(solution)/shard_map/while/body/eval_jaxpr/dot_general | solution.py:35
  294.9 2.9 copy.13
  297.9 72.5 %reduce-scatter.2.cloned.1.call-done = f32[16,2048]{1,0:T(8,128)} async-done(((f32[256,2048]{1,0:T(8,128)}), f32[16,2048]{1,0:T(8,128)}) %reduce-scatter.2.cloned.1.call-update) | async-done | bytes 131088 | tf_op jit(solution)/shard_map/reduce_scatter | solution.py:39
  (22 shorter events, 8.2 us)
Async XLA Ops:
  39.5 210.1 %all-to-all-start.1 = ((bf16[1,1,32,128,256]{4,3,1,0,2:T(8,128)(2,1)}), bf16[1,1,32,128,256]{4,3,1,0,2:T(8,128)(2,1)}, u32[]{:S(2)}, u32[]{:S(2)}) async-start(bf16[1,1,32,128,256]{4,3,1,0,2:T(8,128)(2,1)} %bitcast.35), calls=%async_computation.1 | async-start | bytes 4194304 | tf_op jit(solution)/shard_map/all_to_all | solution.py:19
  44.3 180.3 %all-gather.2.cloned.1.call-start = ((), (), s32[]{:S(2)}) async-start(), calls=%async_computation.3 | async-start | bytes 3244032 | tf_op jit(solution)/shard_map/all_gather | solution.py:28
  45.0 325.3 %reduce-scatter.2.cloned.1.call-start = ((), (), s32[]{:S(2)}) async-start(), calls=%async_computation.4 | async-start | bytes 2228224 | tf_op jit(solution)/shard_map/reduce_scatter | solution.py:39
Sparse Core Ops, SparseCore 0:
  48.2 176.3 all-gather.1
  298.0 72.3 reduce-scatter.1
where the time goes:
time: 379 us; the launch traced here: 377 us
  waiting for transfers between devices  252 us (66%)
  matrix products  34.6 us (9%)
  blocking collectives  32.1 us (8%)
  local copies, waits for them, and re-layouts  31.2 us (8%)
  between operations  13.5 us (4%)
  other arithmetic  8.38 us (2%)
  starting transfers between devices  4.84 us (1%)
    all_gather x1, waiting for transfers between devices, per_device(): gathered = lax.all_gather(query_rows, 'blk', axis=0, tiled=True)  179 us
    reduce_scatter x1, waiting for transfers between devices, per_device(): lax.psum_scatter(partial_value, 'doc', scatter_dimension=0, tiled=True)  72.5 us
    dot_general x8, matrix products, block_tile(): return jnp.dot(picked_queries, masked, preferred_element_type=jnp.float32)  34.6 us
    all_to_all x1, blocking collectives, per_device(): lax.all_to_all(targets, 'blk', split_axis=2, concat_axis=2, tiled=True)  32.1 us
    gather x1, local copies, waits for them, and re-layouts, per_device(): picked_queries = jnp.take(gathered, safe_doc, axis=1)  16.9 us
  transfers between devices with their start and end apart: 3, of which 2 were waited for; matrix products, arithmetic and copies ran while one was open for 7% of the time, Pallas kernels for 0%

commit v1 on v0

v1 whole, which is shorter than its diff:
```python
import functools

import jax
import jax.numpy as jnp
from jax import lax
from jax.experimental import pallas as pl
from jax.experimental.pallas import tpu as pltpu
from jax.sharding import PartitionSpec as P

Y_PARTS = 2
CODE_STEP = 64.0
TOP = 32700.0
TINY = 2.0**-110
LANES = 128


def gram_kernel(flip_ref, q_ref, x_ref, o_ref, left, acc, *, cap, span, per_step, blocks):
    step = pl.program_id(0)
    width = x_ref.shape[2]
    nq = q_ref.shape[0]
    pair_rows = 2 * cap
    for pair in range(per_step // 2):
        docs, ids = [], []
        for k in range(2):
            meta = x_ref[2 * pair + k, cap : cap + 8, :][0:1, :].astype(jnp.float32)
            docs.append(meta[:, :cap] + float(k * span))
            ids.append(meta[:, cap : 2 * cap])
        doc = jnp.concatenate(docs, axis=1).astype(jnp.int32)
        block = jnp.concatenate(ids, axis=1)
        rows = lax.broadcasted_iota(jnp.int32, (2 * span, pair_rows), 0)
        chosen = jnp.where(rows == doc, 1.0, 0.0).astype(jnp.bfloat16)
        queries = q_ref[:, pair * 2 * span : (pair + 1) * 2 * span]
        picked = jnp.dot(queries, chosen, preferred_element_type=jnp.float32)
        for b in range(blocks):
            kept = jnp.where(block == float(b), picked, 0.0).astype(jnp.bfloat16)
            left[b * nq : (b + 1) * nq, pair * pair_rows : (pair + 1) * pair_rows] = kept
    right = jnp.concatenate([x_ref[k, :cap, :] for k in range(per_step)], axis=0)
    product = jnp.dot(left[...], right, preferred_element_type=jnp.float32)

    @pl.when(step == 0)
    def _():
        acc[...] = product

    @pl.when(step > 0)
    def _():
        acc[...] += product

    @pl.when(step == pl.num_programs(0) - 1)
    def _():
        flip = flip_ref[0]
        half = nq // (2 * 16)
        lane = lax.broadcasted_iota(jnp.int32, (16, LANES), 1)
        for m in range(half):
            for slot in range(2):
                target = (slot + flip - 2 * slot * flip) * half + m
                codes = jnp.zeros((16, LANES), jnp.int32)
                for b in range(blocks):
                    base = b * nq + m * 32 + slot * 8
                    tile = jnp.concatenate([acc[base : base + 8, :], acc[base + 16 : base + 24, :]], axis=0)
                    peak = jnp.maximum(jnp.max(jnp.abs(tile), axis=1, keepdims=True), TINY)
                    code = jnp.ceil((jnp.log2(peak) - jnp.log2(TOP)) * CODE_STEP)
                    coded = tile * jnp.exp2(code * (-1.0 / CODE_STEP))
                    coded = jnp.floor(coded + 0.5).astype(jnp.int32).astype(jnp.int16)
                    o_ref[target, :, b * width : (b + 1) * width] = coded
                    codes = jnp.where(lane == b, code.astype(jnp.int32), codes)
                o_ref[target, :, blocks * width :] = codes.astype(jnp.int16)


def partial_tile(flip, queries, rows, *, cap, span, blocks, per_step=8):
    nq, docs = queries.shape
    sources, _, width = rows.shape
    lanes = blocks * width + LANES
    grid_spec = pltpu.PrefetchScalarGridSpec(
        num_scalar_prefetch=1,
        grid=(sources // per_step,),
        in_specs=[
            pl.BlockSpec((nq, per_step * span), lambda i, _: (0, i)),
            pl.BlockSpec((per_step, rows.shape[1], width), lambda i, _: (i, 0, 0)),
        ],
        out_specs=pl.BlockSpec((16, nq // 16, lanes), lambda i, _: (0, 0, 0)),
        scratch_shapes=[
            pltpu.VMEM((blocks * nq, per_step * cap), jnp.bfloat16),
            pltpu.VMEM((blocks * nq, width), jnp.float32),
        ],
    )
    return pl.pallas_call(
        functools.partial(gram_kernel, cap=cap, span=span, per_step=per_step, blocks=blocks),
        grid_spec=grid_spec,
        out_shape=jax.ShapeDtypeStruct((16, nq // 16, lanes), jnp.int16),
        compiler_params=pltpu.CompilerParams(vmem_limit_bytes=48 << 20),
        cost_estimate=pl.CostEstimate(
            flops=2 * nq * sources * cap * width * blocks,
            bytes_accessed=2 * (queries.size + rows.size),
            transcendentals=0,
        ),
        name="gram_tile",
    )(flip, queries, rows)


def sum_kernel(p_ref, o_ref, *, blocks, width):
    groups = p_ref.shape[0]
    scale = jnp.exp2(p_ref[:, :, blocks * width :].astype(jnp.float32) * (1.0 / CODE_STEP))
    for b in range(blocks):
        total = jnp.zeros((p_ref.shape[1], width), jnp.float32)
        for g in range(groups):
            part = p_ref[g, :, b * width : (b + 1) * width].astype(jnp.float32)
            total = total + part * scale[g, :, b : b + 1]
        o_ref[:, b * width : (b + 1) * width] = total


def summed(parts, *, blocks, width):
    return pl.pallas_call(
        functools.partial(sum_kernel, blocks=blocks, width=width),
        out_shape=jax.ShapeDtypeStruct((parts.shape[1], blocks * width), jnp.float32),
        in_specs=[pl.BlockSpec(memory_space=pltpu.VMEM)],
        out_specs=pl.BlockSpec(memory_space=pltpu.VMEM),
        compiler_params=pltpu.CompilerParams(vmem_limit_bytes=16 << 20),
        name="sum_parts",
    )(parts)


def per_device(query_rows, row_values, row_slots, row_counts):
    owners = lax.axis_size("blk")
    z_size = owners // Y_PARTS
    doc_count = query_rows.shape[1]
    span = doc_count // owners
    _, _, _, cap, width = row_values.shape
    blocks = 8
    me = lax.axis_index("blk")

    across = [(i, (i + z_size) % owners) for i in range(owners)]
    mirror = lax.ppermute(query_rows, "blk", across)
    both = jnp.concatenate([query_rows, mirror], axis=0)
    rings = [list(range(h * z_size, (h + 1) * z_size)) for h in range(Y_PARTS)]
    queries = lax.all_gather(both, "blk", axis=0, tiled=True, axis_index_groups=rings)

    slots = row_slots[0, 0]
    live = jnp.arange(cap, dtype=jnp.int32)[None, :] < row_counts[0, 0][:, None]
    doc = (slots // blocks - me * span).astype(jnp.bfloat16)
    block = jnp.where(live, slots % blocks, 2 * blocks).astype(jnp.bfloat16)
    meta = jnp.concatenate([doc, block], axis=1)[:, None, :]
    meta = jnp.pad(meta, ((0, 0), (0, 7), (0, 0)))
    sent = jnp.concatenate([row_values[0, 0], meta], axis=1)
    rows = lax.all_to_all(sent, "blk", split_axis=0, concat_axis=0, tiled=True)

    flip = (me // z_size).astype(jnp.int32).reshape(1)
    coded = partial_tile(flip, queries, rows, cap=cap, span=span, blocks=blocks)
    parts = lax.all_to_all(coded, "doc", split_axis=0, concat_axis=0, tiled=True)
    return summed(parts, blocks=blocks, width=width)


def solution(mesh):
    in_specs = (
        P("blk", "doc"),
        P("doc", "blk", None, None, None),
        P("doc", "blk", None, None),
        P("doc", "blk", None),
    )
    out_specs = P("doc", "blk")
    return jax.shard_map(
        per_device, mesh=mesh, in_specs=in_specs, out_specs=out_specs, check_vma=False
    )
```

time: 379 us -> 213 us (0.56)
  waiting for transfers between devices: 252 us -> 134 us
  matrix products: 34.6 us -> 0 us
  local copies, waits for them, and re-layouts: 31.2 us -> 0.03 us
  starting transfers between devices: 4.84 us -> 23.5 us
  Pallas kernels: 0 us -> 10.2 us
  blocking collectives: 32.1 us -> 26.7 us
    reduce_scatter x1 -> x0, waiting for transfers between devices: 72.5 us -> none  [per_device(): lax.psum_scatter(partial_value, 'doc', scatter_dimension=0, tiled=True)]
    all_gather x1, waiting for transfers between devices: 179 us -> 132 us  [per_device(): lax.all_gather(both, 'blk', axis=0, tiled=True, axis_index_groups=rings)]
    dot_general x8 -> x0, matrix products: 34.6 us -> none  [block_tile(): return jnp.dot(picked_queries, masked, preferred_element_type=jnp.float32)]
    gather x1 -> x0, local copies, waits for them, and re-layouts: 16.9 us -> none  [per_device(): picked_queries = jnp.take(gathered, safe_doc, axis=1)]
    all_to_all x1, starting transfers between devices: 4.76 us -> 18.8 us  [per_device(): rows = lax.all_to_all(sent, 'blk', split_axis=0, concat_axis=0, tiled=True)]
    pallas_call x0 -> x2, Pallas kernels: none -> 10.2 us  [the longest x1 9.16 us: partial_tile(): pl.pallas_call(functools.partial(gram_kernel, cap=cap, span=span, per_ste...]
    and x9 -> x0, other arithmetic: 5.5 us -> none  [the longest x8 5.47 us: block_tile(): keep = (live_rows & (block_of == block))[:, None]]
    all_to_all x1, blocking collectives: 32.1 us -> 26.7 us  [per_device(): lax.all_to_all(coded, 'doc', split_axis=0, concat_axis=0, tiled=True)]
  transfers between devices with their start and end apart: 3 -> 3, of which waited for: 2 -> 2; matrix products, arithmetic and copies ran while one was open for 7% -> 0% of each run, Pallas kernels for 0% -> 0%
where the time goes in v1:
time: 213 us
  waiting for transfers between devices  134 us (63%)
  blocking collectives  26.7 us (13%)
  starting transfers between devices  23.5 us (11%)
  between operations  13.5 us (6%)
  Pallas kernels  10.2 us (5%)
  other arithmetic  4.69 us (2%)
    all_gather x1, waiting for transfers between devices, per_device(): lax.all_gather(both, 'blk', axis=0, tiled=True, axis_index_groups=rings)  132 us
    all_to_all x1, blocking collectives, per_device(): lax.all_to_all(coded, 'doc', split_axis=0, concat_axis=0, tiled=True)  26.7 us
    all_to_all x1, starting transfers between devices, per_device(): rows = lax.all_to_all(sent, 'blk', split_axis=0, concat_axis=0, tiled=True)  18.8 us
    pallas_call x1, Pallas kernels, partial_tile(): pl.pallas_call(functools.partial(gram_kernel, cap=cap, span=span, per_ste...  9.16 us
    ppermute x1, starting transfers between devices, per_device(): mirror = lax.ppermute(query_rows, 'blk', across)  4.65 us
  transfers between devices with their start and end apart: 3, of which 2 were waited for; matrix products, arithmetic and copies ran while one was open for 0% of the time, Pallas kernels for 0%

profile of v1, /device:TPU:1, one launch (start us, length us, event | category | flops | bytes accessed | tf_op | source)
XLA Modules:
  0.0 212.7 jit_solution(13644736531967177159)
XLA Ops:
  6.5 0.8 fusion.3
  7.4 3.2 %fusion.1 = bf16[32,136,256]{2,1,0:T(8,128)(2,1)} fusion(bf16[32,1,256]{2,1,0:T(2,128)(2,1)S(1)} %copy.5, bf16[32,128,256]{2,1,0:T(8,128)(2,1)} %bitcast.31), kind=kLoop, calls=%fused_computation.2 | loop fusion | flops 6684672 | bytes 4341760 | tf_op jit(solution)/shard_map/concatenate | solution.py:143
  10.5 0.0 copy-start
  10.5 18.8 %all-to-all-start = ((bf16[32,136,256]{2,1,0:T(8,128)(2,1)}), bf16[32,136,256]{2,1,0:T(8,128)(2,1)S(1)}, u32[]{:S(2)}, u32[]{:S(2)}) async-start(bf16[32,136,256]{2,1,0:T(8,128)(2,1)} %fusion.1), calls=%async_computation | async-start | bytes 4456448 | tf_op jit(solution)/shard_map/all_to_all | solution.py:144
  29.3 0.0 all-gather.2.cloned.1.call-start
  29.4 0.0 copy-done
  29.4 4.7 %collective-permute-start = (bf16[8,6144]{1,0:T(8,128)(2,1)S(1)}, bf16[8,6144]{1,0:T(8,128)(2,1)S(1)}, u32[]{:S(2)}, u32[]{:S(2)}) collective-permute-start(bf16[8,6144]{1,0:T(8,128)(2,1)S(1)} %copy-done), channel_id=1, source_target_pairs={{0,16},{1,17},{2,18},{3,19},{4,20},{5,21},{6,22},{7,23},{8,24},{9,... | collective-permute-start | bytes 294920 | tf_op jit(solution)/shard_map/ppermute | solution.py:132
  34.1 2.5 %collective-permute-done = bf16[8,6144]{1,0:T(8,128)(2,1)S(1)} collective-permute-done((bf16[8,6144]{1,0:T(8,128)(2,1)S(1)}, bf16[8,6144]{1,0:T(8,128)(2,1)S(1)}, u32[]{:S(2)}, u32[]{:S(2)}) %collective-permute-start) | collective-permute-done | bytes 98336 | tf_op jit(solution)/shard_map/ppermute | solution.py:132
  36.6 0.7 pad_maximum_fusion
  37.3 0.0 all-gather.2.cloned.1.call-update
  37.3 131.6 %all-gather.2.cloned.1.call-done.q_ref = bf16[256,6144]{1,0:T(8,128)(2,1)} async-done(((bf16[16,6144]{1,0:T(8,128)(2,1)}), bf16[256,6144]{1,0:T(8,128)(2,1)}) %all-gather.2.cloned.1.call-update) | async-done | bytes 3145744 | tf_op jit(solution)/shard_map/all_gather | solution.py:135
  169.0 0.0 all-to-all-done.x_ref
  169.0 9.2 %gram_tile.1 = s16[16,16,2176]{2,1,0:T(8,128)(2,1)S(1)} custom-call(s32[1]{0:T(128)} %bitcast.flip_ref, bf16[256,6144]{1,0:T(8,128)(2,1)} %all-gather.2.cloned.1.call-done.q_ref, bf16[32,136,256]{2,1,0:T(8,128)(2,1)S(1)} %all-to-all-done.x_ref), custom_call_target="tpu_custom_call" | custom-call | flops 4294967296 | bytes 5373952 | tf_op jit(solution)/shard_map/gram_tile/pallas_call | solution.py:86
  178.1 26.7 %all_to_all.10.p_ref = s16[16,16,2176]{2,1,0:T(8,128)(2,1)S(1)} all-to-all(s16[16,16,2176]{2,1,0:T(8,128)(2,1)S(1)} %gram_tile.1), channel_id=1, replica_groups=mesh['doc'=16,'blk'=32] {'doc'}, dimensions={0} | all-to-all | bytes 2228224 | tf_op jit(solution)/shard_map/all_to_all | solution.py:148
  204.8 1.0 sum_parts.1
  (2 shorter events, 0.0 us)
Async XLA Ops:
  10.5 18.9 %copy-start = (bf16[8,6144]{1,0:T(8,128)(2,1)S(1)}, bf16[8,6144]{1,0:T(8,128)(2,1)}, u32[]{:S(2)}) copy-start(bf16[8,6144]{1,0:T(8,128)(2,1)} %param.4) | copy-start | bytes 294916
  10.5 158.4 %all-to-all-start = ((bf16[32,136,256]{2,1,0:T(8,128)(2,1)}), bf16[32,136,256]{2,1,0:T(8,128)(2,1)S(1)}, u32[]{:S(2)}, u32[]{:S(2)}) async-start(bf16[32,136,256]{2,1,0:T(8,128)(2,1)} %fusion.1), calls=%async_computation | async-start | bytes 4456448 | tf_op jit(solution)/shard_map/all_to_all | solution.py:144
  29.3 139.6 %all-gather.2.cloned.1.call-start = ((), (), s32[]{:S(2)}) async-start(), calls=%async_computation.2 | async-start | bytes 3342336 | tf_op jit(solution)/shard_map/all_gather | solution.py:135
  29.4 7.2 %collective-permute-start = (bf16[8,6144]{1,0:T(8,128)(2,1)S(1)}, bf16[8,6144]{1,0:T(8,128)(2,1)S(1)}, u32[]{:S(2)}, u32[]{:S(2)}) collective-permute-start(bf16[8,6144]{1,0:T(8,128)(2,1)S(1)} %copy-done), channel_id=1, source_target_pairs={{0,16},{1,17},{2,18},{3,19},{4,20},{5,21},{6,22},{7,23},{8,24},{9,... | collective-permute-start | bytes 294920 | tf_op jit(solution)/shard_map/ppermute | solution.py:132
Sparse Core Ops, SparseCore 0:
  37.5 131.4 all-gather.1

commit v2 on v1

--- a/solution.py
+++ b/solution.py
@@ -30,9 +30,9 @@
         rows = lax.broadcasted_iota(jnp.int32, (2 * span, pair_rows), 0)
         chosen = jnp.where(rows == doc, 1.0, 0.0).astype(jnp.bfloat16)
         queries = q_ref[:, pair * 2 * span : (pair + 1) * 2 * span]
-        picked = jnp.dot(queries, chosen, preferred_element_type=jnp.float32)
+        picked = jnp.dot(queries, chosen, preferred_element_type=jnp.float32).astype(jnp.bfloat16)
         for b in range(blocks):
-            kept = jnp.where(block == float(b), picked, 0.0).astype(jnp.bfloat16)
+            kept = picked * jnp.where(block == float(b), 1.0, 0.0).astype(jnp.bfloat16)
             left[b * nq : (b + 1) * nq, pair * pair_rows : (pair + 1) * pair_rows] = kept
     right = jnp.concatenate([x_ref[k, :cap, :] for k in range(per_step)], axis=0)
     product = jnp.dot(left[...], right, preferred_element_type=jnp.float32)
@@ -97,6 +97,22 @@
     )(flip, queries, rows)
 
 
+def held_kernel(q_ref, o_ref):
+    pltpu.touch(o_ref)
+
+
+def held(queries):
+    return pl.pallas_call(
+        held_kernel,
+        out_shape=jax.ShapeDtypeStruct(queries.shape, queries.dtype),
+        in_specs=[pl.BlockSpec(memory_space=pl.ANY)],
+        out_specs=pl.BlockSpec(memory_space=pl.ANY),
+        input_output_aliases={0: 0},
+        cost_estimate=pl.CostEstimate(flops=10**12, bytes_accessed=10**6, transcendentals=0),
+        name="held",
+    )(queries)
+
+
 def sum_kernel(p_ref, o_ref, *, blocks, width):
     groups = p_ref.shape[0]
     scale = jnp.exp2(p_ref[:, :, blocks * width :].astype(jnp.float32) * (1.0 / CODE_STEP))
@@ -132,19 +148,19 @@
     mirror = lax.ppermute(query_rows, "blk", across)
     both = jnp.concatenate([query_rows, mirror], axis=0)
     rings = [list(range(h * z_size, (h + 1) * z_size)) for h in range(Y_PARTS)]
-    queries = lax.all_gather(both, "blk", axis=0, tiled=True, axis_index_groups=rings)
-
     slots = row_slots[0, 0]
     live = jnp.arange(cap, dtype=jnp.int32)[None, :] < row_counts[0, 0][:, None]
     doc = (slots // blocks - me * span).astype(jnp.bfloat16)
     block = jnp.where(live, slots % blocks, 2 * blocks).astype(jnp.bfloat16)
     meta = jnp.concatenate([doc, block], axis=1)[:, None, :]
     meta = jnp.pad(meta, ((0, 0), (0, 7), (0, 0)))
-    sent = jnp.concatenate([row_values[0, 0], meta], axis=1)
+    values, both = lax.optimization_barrier((row_values[0, 0], both))
+    sent = jnp.concatenate([values, meta], axis=1)
+    queries = lax.all_gather(both, "blk", axis=0, tiled=True, axis_index_groups=rings)
     rows = lax.all_to_all(sent, "blk", split_axis=0, concat_axis=0, tiled=True)
 
     flip = (me // z_size).astype(jnp.int32).reshape(1)
-    coded = partial_tile(flip, queries, rows, cap=cap, span=span, blocks=blocks)
+    coded = partial_tile(flip, held(queries), rows, cap=cap, span=span, blocks=blocks)
     parts = lax.all_to_all(coded, "doc", split_axis=0, concat_axis=0, tiled=True)
     return summed(parts, blocks=blocks, width=width)
 

time: 213 us -> 217 us (1.019)
  waiting for transfers between devices: 134 us -> 139 us
  blocking collectives: 26.7 us -> 24.3 us
    all_gather x1, waiting for transfers between devices: 132 us -> 137 us  [per_device(): lax.all_gather(both, 'blk', axis=0, tiled=True, axis_index_groups=rings)]
    all_to_all x1, blocking collectives: 26.7 us -> 24.3 us  [per_device(): lax.all_to_all(coded, 'doc', split_axis=0, concat_axis=0, tiled=True)]
  transfers between devices with their start and end apart: 3 -> 3, of which waited for: 2 -> 2; matrix products, arithmetic and copies ran while one was open for 0% -> 2% of each run, Pallas kernels for 0% -> 0%
where the time goes in v2:
time: 217 us; the launch traced here: 216 us
  waiting for transfers between devices  139 us (64%)
  blocking collectives  24.3 us (11%)
  starting transfers between devices  23.6 us (11%)
  between operations  13.5 us (6%)
  Pallas kernels  10.3 us (5%)
  other arithmetic  5.56 us (3%)
    all_gather x1, waiting for transfers between devices, per_device(): lax.all_gather(both, 'blk', axis=0, tiled=True, axis_index_groups=rings)  137 us
    all_to_all x1, blocking collectives, per_device(): lax.all_to_all(coded, 'doc', split_axis=0, concat_axis=0, tiled=True)  24.3 us
    all_to_all x1, starting transfers between devices, per_device(): rows = lax.all_to_all(sent, 'blk', split_axis=0, concat_axis=0, tiled=True)  18 us
    pallas_call x1, Pallas kernels, partial_tile(): pl.pallas_call(functools.partial(gram_kernel, cap=cap, span=span, per_ste...  9.31 us
    ppermute x1, starting transfers between devices, per_device(): mirror = lax.ppermute(query_rows, 'blk', across)  5.64 us
  transfers between devices with their start and end apart: 3, of which 2 were waited for; matrix products, arithmetic and copies ran while one was open for 2% of the time, Pallas kernels for 0%

profile of v2, /device:TPU:1, one launch (start us, length us, event | category | flops | bytes accessed | tf_op | source)
XLA Modules:
  0.0 216.4 jit_solution(15992197990599397113)
XLA Ops:
  6.5 0.0 all-gather.2.cloned.1.call-start
  6.5 5.6 %collective-permute-start = (bf16[8,6144]{1,0:T(8,128)(2,1)}, bf16[8,6144]{1,0:T(8,128)(2,1)S(1)}, u32[]{:S(2)}, u32[]{:S(2)}) collective-permute-start(bf16[8,6144]{1,0:T(8,128)(2,1)} %param.4), channel_id=1, source_target_pairs={{0,16},{1,17},{2,18},{3,19},{4,20},{5,21},{6,22},{7,23},{8,24},{9,... | collective-permute-start | bytes 294920 | tf_op jit(solution)/shard_map/ppermute | solution.py:148
  12.2 2.2 %collective-permute-done = bf16[8,6144]{1,0:T(8,128)(2,1)S(1)} collective-permute-done((bf16[8,6144]{1,0:T(8,128)(2,1)}, bf16[8,6144]{1,0:T(8,128)(2,1)S(1)}, u32[]{:S(2)}, u32[]{:S(2)}) %collective-permute-start) | collective-permute-done | bytes 98336 | tf_op jit(solution)/shard_map/ppermute | solution.py:148
  14.4 1.6 pad_maximum_fusion
  16.0 0.0 all-gather.2.cloned.1.call-update
  16.0 0.8 fusion.3
  16.9 3.2 %fusion.1 = bf16[32,136,256]{2,1,0:T(8,128)(2,1)} fusion(bf16[32,1,256]{2,1,0:T(2,128)(2,1)S(1)} %copy.6, bf16[32,128,256]{2,1,0:T(8,128)(2,1)} %bitcast.31), kind=kLoop, calls=%fused_computation.2 | loop fusion | flops 6684672 | bytes 4341760 | tf_op jit(solution)/shard_map/concatenate | solution.py:158
  20.0 18.0 %all-to-all-start = ((bf16[32,136,256]{2,1,0:T(8,128)(2,1)}), bf16[32,136,256]{2,1,0:T(8,128)(2,1)}, u32[]{:S(2)}, u32[]{:S(2)}) async-start(bf16[32,136,256]{2,1,0:T(8,128)(2,1)} %fusion.1), calls=%async_computation | async-start | bytes 4456448 | tf_op jit(solution)/shard_map/all_to_all | solution.py:160
  38.0 136.9 %all-gather.2.cloned.1.call-done.q_ref = bf16[256,6144]{1,0:T(8,128)(2,1)} async-done(((bf16[16,6144]{1,0:T(8,128)(2,1)}), bf16[256,6144]{1,0:T(8,128)(2,1)}) %all-gather.2.cloned.1.call-update) | async-done | bytes 3145744 | tf_op jit(solution)/shard_map/all_gather | solution.py:159
  174.9 0.0 all-to-all-done.x_ref
  174.9 9.3 %gram_tile.1 = s16[16,16,2176]{2,1,0:T(8,128)(2,1)S(1)} custom-call(s32[1]{0:T(128)} %bitcast.flip_ref, bf16[256,6144]{1,0:T(8,128)(2,1)} %held.1.q_ref, bf16[32,136,256]{2,1,0:T(8,128)(2,1)} %all-to-all-done.x_ref), custom_call_target="tpu_custom_call" | custom-call | flops 4294967296 | bytes 5373952 | tf_op jit(solution)/shard_map/gram_tile/pallas_call | solution.py:86
  184.2 24.3 %all_to_all.10.p_ref = s16[16,16,2176]{2,1,0:T(8,128)(2,1)S(1)} all-to-all(s16[16,16,2176]{2,1,0:T(8,128)(2,1)S(1)} %gram_tile.1), channel_id=1, replica_groups=mesh['doc'=16,'blk'=32] {'doc'}, dimensions={0} | all-to-all | bytes 2228224 | tf_op jit(solution)/shard_map/all_to_all | solution.py:164
  208.5 1.0 sum_parts.1
  (3 shorter events, 0.0 us)
Async XLA Ops:
  6.5 168.4 %all-gather.2.cloned.1.call-start = ((), (), s32[]{:S(2)}) async-start(), calls=%async_computation.2 | async-start | bytes 3342336 | tf_op jit(solution)/shard_map/all_gather | solution.py:159
  6.5 7.8 %collective-permute-start = (bf16[8,6144]{1,0:T(8,128)(2,1)}, bf16[8,6144]{1,0:T(8,128)(2,1)S(1)}, u32[]{:S(2)}, u32[]{:S(2)}) collective-permute-start(bf16[8,6144]{1,0:T(8,128)(2,1)} %param.4), channel_id=1, source_target_pairs={{0,16},{1,17},{2,18},{3,19},{4,20},{5,21},{6,22},{7,23},{8,24},{9,... | collective-permute-start | bytes 294920 | tf_op jit(solution)/shard_map/ppermute | solution.py:148
  20.0 154.9 %all-to-all-start = ((bf16[32,136,256]{2,1,0:T(8,128)(2,1)}), bf16[32,136,256]{2,1,0:T(8,128)(2,1)}, u32[]{:S(2)}, u32[]{:S(2)}) async-start(bf16[32,136,256]{2,1,0:T(8,128)(2,1)} %fusion.1), calls=%async_computation | async-start | bytes 4456448 | tf_op jit(solution)/shard_map/all_to_all | solution.py:160
Sparse Core Ops, SparseCore 0:
  16.1 158.7 all-gather.1

commit v3 on v2

v3 whole, which is shorter than its diff:
```python
import functools

import jax
import jax.numpy as jnp
from jax import lax
from jax.experimental import pallas as pl
from jax.experimental.pallas import tpu as pltpu
from jax.sharding import Mesh
from jax.sharding import PartitionSpec as P

HALVES = 2
CODE_STEP = 64.0
TOP = 32700.0
TINY = 2.0**-110
LANES = 128
TILE = 8


def gram_kernel(flip_ref, q_ref, x_ref, o_ref, left, acc, *, cap, span, per_step, blocks):
    step = pl.program_id(0)
    width = x_ref.shape[2]
    nq = q_ref.shape[0]
    pair_rows = 2 * cap
    for owner in range(HALVES):
        for pair in range(per_step // 2):
            docs, ids = [], []
            for k in range(2):
                base = HALVES * cap
                meta = x_ref[2 * pair + k, base : base + TILE, :][owner : owner + 1, :].astype(jnp.float32)
                docs.append(meta[:, :cap] + float(k * span))
                ids.append(meta[:, cap : 2 * cap])
            doc = jnp.concatenate(docs, axis=1).astype(jnp.int32)
            block = jnp.concatenate(ids, axis=1)
            rows = lax.broadcasted_iota(jnp.int32, (2 * span, pair_rows), 0)
            chosen = jnp.where(rows == doc, 1.0, 0.0).astype(jnp.bfloat16)
            queries = q_ref[:, pair * 2 * span : (pair + 1) * 2 * span]
            picked = jnp.dot(queries, chosen, preferred_element_type=jnp.float32).astype(jnp.bfloat16)
            for b in range(blocks):
                kept = picked * jnp.where(block == float(b), 1.0, 0.0).astype(jnp.bfloat16)
                left[owner, b * nq : (b + 1) * nq, pair * pair_rows : (pair + 1) * pair_rows] = kept
        right = jnp.concatenate([x_ref[k, owner * cap : (owner + 1) * cap, :] for k in range(per_step)], axis=0)
        product = jnp.dot(left[owner], right, preferred_element_type=jnp.float32)

        @pl.when(step == 0)
        def _():
            acc[owner] = product

        @pl.when(step > 0)
        def _():
            acc[owner] += product

    @pl.when(step == pl.num_programs(0) - 1)
    def _():
        flip = flip_ref[0]
        half = nq // (2 * 16)
        lane = lax.broadcasted_iota(jnp.int32, (16, LANES), 1)
        for owner in range(HALVES):
            for m in range(half):
                for slot in range(2):
                    target = ((slot + flip - 2 * slot * flip) * half + m) * HALVES + owner
                    codes = jnp.zeros((16, LANES), jnp.int32)
                    for b in range(blocks):
                        base = b * nq + m * 32 + slot * 8
                        tile = jnp.concatenate([acc[owner, base : base + 8, :], acc[owner, base + 16 : base + 24, :]], axis=0)
                        peak = jnp.maximum(jnp.max(jnp.abs(tile), axis=1, keepdims=True), TINY)
                        code = jnp.ceil((jnp.log2(peak) - jnp.log2(TOP)) * CODE_STEP)
                        coded = tile * jnp.exp2(code * (-1.0 / CODE_STEP))
                        coded = jnp.floor(coded + 0.5).astype(jnp.int32).astype(jnp.int16)
                        o_ref[target, :, b * width : (b + 1) * width] = coded
                        codes = jnp.where(lane == b, code.astype(jnp.int32), codes)
                    o_ref[target, :, blocks * width :] = codes.astype(jnp.int16)


def partial_tiles(flip, queries, rows, *, cap, span, blocks, per_step=4):
    nq, docs = queries.shape
    sources, depth, width = rows.shape
    lanes = blocks * width + LANES
    targets = 16 * HALVES
    grid_spec = pltpu.PrefetchScalarGridSpec(
        num_scalar_prefetch=1,
        grid=(sources // per_step,),
        in_specs=[
            pl.BlockSpec((nq, per_step * span), lambda i, _: (0, i)),
            pl.BlockSpec((per_step, depth, width), lambda i, _: (i, 0, 0)),
        ],
        out_specs=pl.BlockSpec((targets, nq // 16, lanes), lambda i, _: (0, 0, 0)),
        scratch_shapes=[
            pltpu.VMEM((HALVES, blocks * nq, per_step * cap), jnp.bfloat16),
            pltpu.VMEM((HALVES, blocks * nq, width), jnp.float32),
        ],
    )
    return pl.pallas_call(
        functools.partial(gram_kernel, cap=cap, span=span, per_step=per_step, blocks=blocks),
        grid_spec=grid_spec,
        out_shape=jax.ShapeDtypeStruct((targets, nq // 16, lanes), jnp.int16),
        compiler_params=pltpu.CompilerParams(vmem_limit_bytes=48 << 20),
        cost_estimate=pl.CostEstimate(
            flops=2 * nq * sources * HALVES * cap * width * blocks,
            bytes_accessed=2 * (queries.size + rows.size),
            transcendentals=0,
        ),
        name="gram_tiles",
    )(flip, queries, rows)


def held_kernel(q_ref, o_ref):
    pltpu.touch(o_ref)


def held(queries):
    return pl.pallas_call(
        held_kernel,
        out_shape=jax.ShapeDtypeStruct(queries.shape, queries.dtype),
        in_specs=[pl.BlockSpec(memory_space=pl.ANY)],
        out_specs=pl.BlockSpec(memory_space=pl.ANY),
        input_output_aliases={0: 0},
        cost_estimate=pl.CostEstimate(flops=10**12, bytes_accessed=10**6, transcendentals=0),
        name="held",
    )(queries)


def sum_kernel(p_ref, o_ref, *, blocks, width):
    groups = p_ref.shape[0]
    scale = jnp.exp2(p_ref[:, :, blocks * width :].astype(jnp.float32) * (1.0 / CODE_STEP))
    for b in range(blocks):
        total = jnp.zeros((p_ref.shape[1], width), jnp.float32)
        for g in range(groups):
            part = p_ref[g, :, b * width : (b + 1) * width].astype(jnp.float32)
            total = total + part * scale[g, :, b : b + 1]
        o_ref[:, b * width : (b + 1) * width] = total


def summed(parts, *, blocks, width):
    return pl.pallas_call(
        functools.partial(sum_kernel, blocks=blocks, width=width),
        out_shape=jax.ShapeDtypeStruct((parts.shape[1], blocks * width), jnp.float32),
        in_specs=[pl.BlockSpec(memory_space=pltpu.VMEM)],
        out_specs=pl.BlockSpec(memory_space=pltpu.VMEM),
        compiler_params=pltpu.CompilerParams(vmem_limit_bytes=16 << 20),
        name="sum_parts",
    )(parts)


def per_device(query_rows, row_values, row_slots, row_counts):
    z_size = lax.axis_size("z")
    owners = HALVES * z_size
    doc_count = query_rows.shape[1]
    span = doc_count // owners
    _, _, _, cap, width = row_values.shape
    blocks = 8
    y = lax.axis_index("y")
    me = y * z_size + lax.axis_index("z")

    half_docs = doc_count // HALVES
    mine = lax.dynamic_slice_in_dim(query_rows, y * half_docs, half_docs, 1)
    theirs = lax.dynamic_slice_in_dim(query_rows, (1 - y) * half_docs, half_docs, 1)
    mirror = lax.ppermute(theirs, "y", [(0, 1), (1, 0)])
    both = jnp.concatenate([mine, mirror], axis=0)

    slots = row_slots[0, 0]
    live = jnp.arange(cap, dtype=jnp.int32)[None, :] < row_counts[0, 0][:, None]
    doc = (slots // blocks - me * span).astype(jnp.bfloat16)
    block = jnp.where(live, slots % blocks, 2 * blocks).astype(jnp.bfloat16)
    meta = jnp.concatenate([doc, block], axis=1).reshape(HALVES, z_size, 2 * cap).transpose(1, 0, 2)
    meta = jnp.pad(meta, ((0, 0), (0, TILE - HALVES), (0, 0)))
    values, both = lax.optimization_barrier((row_values[0, 0], both))
    sent = jnp.concatenate([values[:z_size], values[z_size:], meta], axis=1)

    queries = lax.all_gather(both, "z", axis=0, tiled=True)
    rows = lax.all_to_all(sent, "z", split_axis=0, concat_axis=0, tiled=True)

    coded = partial_tiles(y.astype(jnp.int32).reshape(1), held(queries), rows, cap=cap, span=span, blocks=blocks)
    parts = lax.all_to_all(coded, ("doc", "y"), split_axis=0, concat_axis=0, tiled=True)
    return summed(parts, blocks=blocks, width=width)


def solution(mesh):
    docs, owners = mesh.devices.shape
    split = Mesh(mesh.devices.reshape(docs, HALVES, owners // HALVES), ("doc", "y", "z"))
    blk = ("y", "z")
    in_specs = (
        P(blk, "doc"),
        P("doc", blk, None, None, None),
        P("doc", blk, None, None),
        P("doc", blk, None),
    )
    return jax.shard_map(
        per_device, mesh=split, in_specs=in_specs, out_specs=P("doc", blk), check_vma=False
    )
```

time: 217 us -> 216 us (level)
  waiting for transfers between devices: 139 us -> 114 us
  blocking collectives: 24.3 us -> 41.7 us
  Pallas kernels: 10.3 us -> 16.9 us
  local copies, waits for them, and re-layouts: 0.03 us -> 4.66 us
  starting transfers between devices: 23.6 us -> 20.6 us
    all_gather x1, waiting for transfers between devices: 137 us -> 112 us  [per_device(): queries = lax.all_gather(both, 'z', axis=0, tiled=True)]
    all_to_all x1, blocking collectives: 24.3 us -> 41.7 us  [per_device(): lax.all_to_all(coded, ('doc', 'y'), split_axis=0, concat_axis=0, tiled=True)]
    pallas_call x1, Pallas kernels: 9.31 us -> 15.7 us  [partial_tiles(): pl.pallas_call(functools.partial(gram_kernel, cap=cap, span=span, per_ste...]
    all_to_all x1, starting transfers between devices: 18 us -> 15 us  [per_device(): rows = lax.all_to_all(sent, 'z', split_axis=0, concat_axis=0, tiled=True)]
    concatenate x2, other arithmetic: 4.75 us -> 2.14 us  [the longest x1 1.5 us: per_device(): sent = jnp.concatenate([values[:z_size], values[z_size:], meta], axis=1)]
  transfers between devices with their start and end apart: 3 -> 3, of which waited for: 2 -> 2; matrix products, arithmetic and copies ran while one was open for 2% -> 3% of each run, Pallas kernels for 0% -> 0%
where the time goes in v3:
time: 216 us; the launch traced here: 215 us
  waiting for transfers between devices  114 us (53%)
  blocking collectives  41.7 us (19%)
  starting transfers between devices  20.6 us (10%)
  Pallas kernels  16.9 us (8%)
  between operations  13.4 us (6%)
  local copies, waits for them, and re-layouts  4.66 us (2%)
  other arithmetic  4.2 us (2%)
    all_gather x1, waiting for transfers between devices, per_device(): queries = lax.all_gather(both, 'z', axis=0, tiled=True)  112 us
    all_to_all x1, blocking collectives, per_device(): lax.all_to_all(coded, ('doc', 'y'), split_axis=0, concat_axis=0, tiled=True)  41.7 us
    pallas_call x1, Pallas kernels, partial_tiles(): pl.pallas_call(functools.partial(gram_kernel, cap=cap, span=span, per_ste...  15.7 us
    all_to_all x1, starting transfers between devices, per_device(): rows = lax.all_to_all(sent, 'z', split_axis=0, concat_axis=0, tiled=True)  15 us
    ppermute x1, starting transfers between devices, per_device(): mirror = lax.ppermute(theirs, 'y', [(0, 1), (1, 0)])  5.64 us
  transfers between devices with their start and end apart: 3, of which 2 were waited for; matrix products, arithmetic and copies ran while one was open for 3% of the time, Pallas kernels for 0%

profile of v3, /device:TPU:1, one launch (start us, length us, event | category | flops | bytes accessed | tf_op | source)
XLA Modules:
  0.0 215.4 jit_solution(5760797158136369266)
XLA Ops:
  6.5 0.0 all-gather.2.cloned.1.call-start
  6.5 0.8 constant_dynamic-slice_fusion.1
  7.4 5.6 %collective-permute-start = (bf16[8,3072]{1,0:T(8,128)(2,1)S(1)}, bf16[8,3072]{1,0:T(8,128)(2,1)S(1)}, u32[]{:S(2)}, u32[]{:S(2)}) collective-permute-start(bf16[8,3072]{1,0:T(8,128)(2,1)S(1)} %get-tuple-element.12), channel_id=1, source_target_pairs={{0,16},{16,0},{1,17},{17,1},{2,18},{18,2},{3,19},{19,3},{4,20},{20... | collective-permute-start | bytes 147464 | tf_op jit(solution)/shard_map/ppermute | solution.py:157
  13.0 1.5 collective-permute-done
  14.5 0.6 pad_maximum_fusion
  15.1 0.0 all-gather.2.cloned.1.call-update
  15.2 0.5 broadcast.55
  15.7 1.2 reduce.3
  16.9 0.1 lt.31
  17.0 0.1 copy.11
  17.1 0.8 subtract_convert_fusion
  17.9 1.8 fusion.3
  19.7 1.5 fusion.1
  21.1 15.0 %all-to-all-start = ((bf16[16,264,256]{2,1,0:T(8,128)(2,1)}), bf16[16,264,256]{2,1,0:T(8,128)(2,1)}, u32[]{:S(2)}, u32[]{:S(2)}) async-start(bf16[16,264,256]{2,1,0:T(8,128)(2,1)} %fusion.1), calls=%async_computation | async-start | bytes 4325376 | tf_op jit(solution)/shard_map/all_to_all | solution.py:170
  36.2 112.3 %all-gather.2.cloned.1.call-done.q_ref = bf16[256,3072]{1,0:T(8,128)(2,1)} async-done(((bf16[16,3072]{1,0:T(8,128)(2,1)}), bf16[256,3072]{1,0:T(8,128)(2,1)}) %all-gather.2.cloned.1.call-update) | async-done | bytes 1572880 | tf_op jit(solution)/shard_map/all_gather | solution.py:169
  148.5 0.0 all-to-all-done.x_ref
  148.5 0.0 copy-start
  148.5 1.4 copy-done
  149.9 15.7 %gram_tiles.1 = s16[32,16,2176]{2,1,0:T(8,128)(2,1)S(1)} custom-call(s32[1]{0:T(128)} %bitcast.flip_ref, bf16[256,3072]{1,0:T(8,128)(2,1)S(1)} %copy-done, bf16[16,264,256]{2,1,0:T(8,128)(2,1)} %all-to-all-done.x_ref), custom_call_target="tpu_custom_call" | custom-call | flops 4294967296 | bytes 3735552 | tf_op jit(solution)/shard_map/gram_tiles/pallas_call | solution.py:92
  165.6 41.7 %all_to_all.10.p_ref = s16[32,16,2176]{2,1,0:T(8,128)(2,1)S(1)} all-to-all(s16[32,16,2176]{2,1,0:T(8,128)(2,1)S(1)} %gram_tiles.1), channel_id=1, replica_groups=mesh['doc'=16,'y'=2,'z'=16] {'doc','y'}, dimensions={0} | all-to-all | bytes 4456448 | tf_op jit(solution)/shard_map/all_to_all | solution.py:173
  207.3 1.3 sum_parts.1
  (2 shorter events, 0.0 us)
Async XLA Ops:
  6.5 142.0 %all-gather.2.cloned.1.call-start = ((), (), s32[]{:S(2)}) async-start(), calls=%async_computation.2 | async-start | bytes 1671168 | tf_op jit(solution)/shard_map/all_gather | solution.py:169
  7.4 7.1 %collective-permute-start = (bf16[8,3072]{1,0:T(8,128)(2,1)S(1)}, bf16[8,3072]{1,0:T(8,128)(2,1)S(1)}, u32[]{:S(2)}, u32[]{:S(2)}) collective-permute-start(bf16[8,3072]{1,0:T(8,128)(2,1)S(1)} %get-tuple-element.12), channel_id=1, source_target_pairs={{0,16},{16,0},{1,17},{17,1},{2,18},{18,2},{3,19},{19,3},{4,20},{20... | collective-permute-start | bytes 147464 | tf_op jit(solution)/shard_map/ppermute | solution.py:157
  21.1 127.4 %all-to-all-start = ((bf16[16,264,256]{2,1,0:T(8,128)(2,1)}), bf16[16,264,256]{2,1,0:T(8,128)(2,1)}, u32[]{:S(2)}, u32[]{:S(2)}) async-start(bf16[16,264,256]{2,1,0:T(8,128)(2,1)} %fusion.1), calls=%async_computation | async-start | bytes 4325376 | tf_op jit(solution)/shard_map/all_to_all | solution.py:170
  148.5 1.4 copy-start
Sparse Core Ops, SparseCore 0:
  15.3 133.1 all-gather.1

commit v4 on v3

--- a/solution.py
+++ b/solution.py
@@ -14,6 +14,119 @@
 TINY = 2.0**-110
 LANES = 128
 TILE = 8
+SHALLOW = 96
+EXTRA = 48
+DEAD = 64
+
+
+def code_tiles(flip_ref, acc, o_ref, *, nq, blocks):
+    width = acc.shape[2]
+    flip = flip_ref[0]
+    half = nq // (2 * 16)
+    lane = lax.broadcasted_iota(jnp.int32, (16, LANES), 1)
+
+    def tile_of(owner, b, m, slot):
+        base = b * nq + m * 32 + slot * 8
+        return jnp.concatenate([acc[owner, base : base + 8, :], acc[owner, base + 16 : base + 24, :]], axis=0)
+
+    for owner in range(HALVES):
+        for m in range(half):
+            for slot in range(2):
+                target = ((slot + flip - 2 * slot * flip) * half + m) * HALVES + owner
+                peaks = jnp.full((16, LANES), TINY, jnp.float32)
+                for b in range(blocks):
+                    peak = jnp.max(jnp.abs(tile_of(owner, b, m, slot)), axis=1, keepdims=True)
+                    peaks = jnp.where(lane == b, jnp.maximum(peak, TINY), peaks)
+                code = jnp.ceil((jnp.log2(peaks) - jnp.log2(TOP)) * CODE_STEP)
+                inverse = jnp.exp2(code * (-1.0 / CODE_STEP))
+                for b in range(blocks):
+                    coded = tile_of(owner, b, m, slot) * inverse[:, b : b + 1]
+                    coded = jnp.floor(coded + 0.5).astype(jnp.int32).astype(jnp.int16)
+                    o_ref[target, :, b * width : (b + 1) * width] = coded
+                o_ref[target, :, blocks * width :] = code.astype(jnp.int32).astype(jnp.int16)
+
+
+def lean_kernel(flip_ref, q_ref, deep_ref, x_ref, o_ref, left, acc, *, cap, span, per_step, blocks, extra):
+    step = pl.program_id(0)
+    width = x_ref.shape[2]
+    nq = q_ref.shape[0]
+    base = HALVES * cap
+    group = 4
+
+    def chosen(doc, docs):
+        rows = lax.broadcasted_iota(jnp.int32, (docs, doc.shape[1]), 0)
+        return jnp.where(rows == doc.astype(jnp.int32), 1.0, 0.0).astype(jnp.bfloat16)
+
+    def picked(doc, first, count):
+        queries = q_ref[:, first * span : (first + count) * span]
+        return jnp.dot(queries, chosen(doc, count * span), preferred_element_type=jnp.float32).astype(jnp.bfloat16)
+
+    metas = [x_ref[k, base : base + TILE, :].astype(jnp.float32) for k in range(per_step)]
+    deep_doc = jnp.concatenate([metas[k][2:3, :extra] + float(k * span) for k in range(per_step)], axis=1)
+    deep_block = jnp.concatenate([metas[k][2:3, LANES : LANES + extra] for k in range(per_step)], axis=1)
+    deep_picked = picked(deep_doc, 0, per_step)
+    deep_rows = [deep_ref[k * 16 : (k + 1) * 16, g * width : (g + 1) * width] for k in range(per_step) for g in range(extra // 16)]
+    for owner in range(HALVES):
+        for first in range(0, per_step, group):
+            members = range(first, first + group)
+            doc = jnp.concatenate([metas[k][owner : owner + 1, :cap] + float((k - first) * span) for k in members], axis=1)
+            block = jnp.concatenate([metas[k][owner : owner + 1, LANES : LANES + cap] for k in members], axis=1)
+            got = picked(doc, first, group)
+            for b in range(blocks):
+                kept = got * jnp.where(block == float(b), 1.0, 0.0).astype(jnp.bfloat16)
+                left[owner, b * nq : (b + 1) * nq, first * cap : (first + group) * cap] = kept
+        for b in range(blocks):
+            kept = deep_picked * jnp.where(deep_block == float(b + owner * blocks), 1.0, 0.0).astype(jnp.bfloat16)
+            left[owner, b * nq : (b + 1) * nq, per_step * cap :] = kept
+        right = jnp.concatenate([x_ref[k, owner * cap : (owner + 1) * cap, :] for k in range(per_step)] + deep_rows, axis=0)
+        product = jnp.dot(left[owner], right, preferred_element_type=jnp.float32)
+
+        @pl.when(step == 0)
+        def _():
+            acc[owner] = product
+
+        @pl.when(step > 0)
+        def _():
+            acc[owner] += product
+
+    @pl.when(step == pl.num_programs(0) - 1)
+    def _():
+        code_tiles(flip_ref, acc, o_ref, nq=nq, blocks=blocks)
+
+
+def lean_tiles(flip, queries, rows, *, cap, span, blocks, extra, per_step=8):
+    nq = queries.shape[0]
+    sources, depth, width = rows.shape
+    lanes = blocks * width + LANES
+    targets = 16 * HALVES
+    deep_lanes = extra // 16 * width
+    deep_at = sources * span // deep_lanes
+    grid_spec = pltpu.PrefetchScalarGridSpec(
+        num_scalar_prefetch=1,
+        grid=(sources // per_step,),
+        in_specs=[
+            pl.BlockSpec((nq, per_step * span), lambda i, _: (0, i)),
+            pl.BlockSpec((per_step * 16, deep_lanes), lambda i, _: (i, deep_at)),
+            pl.BlockSpec((per_step, depth, width), lambda i, _: (i, 0, 0)),
+        ],
+        out_specs=pl.BlockSpec((targets, nq // 16, lanes), lambda i, _: (0, 0, 0)),
+        scratch_shapes=[
+            pltpu.VMEM((HALVES, blocks * nq, per_step * (cap + extra)), jnp.bfloat16),
+            pltpu.VMEM((HALVES, blocks * nq, width), jnp.float32),
+        ],
+    )
+    return pl.pallas_call(
+        functools.partial(lean_kernel, cap=cap, span=span, per_step=per_step, blocks=blocks, extra=extra),
+        grid_spec=grid_spec,
+        out_shape=jax.ShapeDtypeStruct((targets, nq // 16, lanes), jnp.int16),
+        compiler_params=pltpu.CompilerParams(vmem_limit_bytes=56 << 20),
+        cost_estimate=pl.CostEstimate(
+            flops=2 * nq * sources * HALVES * (cap + extra) * width * blocks,
+            bytes_accessed=2 * (queries.size + rows.size),
+            transcendentals=0,
+        ),
+        name="lean_tiles",
+    )(flip, queries, queries, rows)
 
 
 def gram_kernel(flip_ref, q_ref, x_ref, o_ref, left, acc, *, cap, span, per_step, blocks):
@@ -51,24 +164,7 @@
 
     @pl.when(step == pl.num_programs(0) - 1)
     def _():
-        flip = flip_ref[0]
-        half = nq // (2 * 16)
-        lane = lax.broadcasted_iota(jnp.int32, (16, LANES), 1)
-        for owner in range(HALVES):
-            for m in range(half):
-                for slot in range(2):
-                    target = ((slot + flip - 2 * slot * flip) * half + m) * HALVES + owner
-                    codes = jnp.zeros((16, LANES), jnp.int32)
-                    for b in range(blocks):
-                        base = b * nq + m * 32 + slot * 8
-                        tile = jnp.concatenate([acc[owner, base : base + 8, :], acc[owner, base + 16 : base + 24, :]], axis=0)
-                        peak = jnp.maximum(jnp.max(jnp.abs(tile), axis=1, keepdims=True), TINY)
-                        code = jnp.ceil((jnp.log2(peak) - jnp.log2(TOP)) * CODE_STEP)
-                        coded = tile * jnp.exp2(code * (-1.0 / CODE_STEP))
-                        coded = jnp.floor(coded + 0.5).astype(jnp.int32).astype(jnp.int16)
-                        o_ref[target, :, b * width : (b + 1) * width] = coded
-                        codes = jnp.where(lane == b, code.astype(jnp.int32), codes)
-                    o_ref[target, :, blocks * width :] = codes.astype(jnp.int16)
+        code_tiles(flip_ref, acc, o_ref, nq=nq, blocks=blocks)
 
 
 def partial_tiles(flip, queries, rows, *, cap, span, blocks, per_step=4):
@@ -158,18 +254,61 @@
     both = jnp.concatenate([mine, mirror], axis=0)
 
     slots = row_slots[0, 0]
-    live = jnp.arange(cap, dtype=jnp.int32)[None, :] < row_counts[0, 0][:, None]
-    doc = (slots // blocks - me * span).astype(jnp.bfloat16)
-    block = jnp.where(live, slots % blocks, 2 * blocks).astype(jnp.bfloat16)
-    meta = jnp.concatenate([doc, block], axis=1).reshape(HALVES, z_size, 2 * cap).transpose(1, 0, 2)
-    meta = jnp.pad(meta, ((0, 0), (0, TILE - HALVES), (0, 0)))
-    values, both = lax.optimization_barrier((row_values[0, 0], both))
-    sent = jnp.concatenate([values[:z_size], values[z_size:], meta], axis=1)
-
+    counts = row_counts[0, 0]
+    places = jnp.arange(cap, dtype=jnp.int32)
+    live = places[None, :] < counts[:, None]
+    doc = slots // blocks - me * span
+    block = jnp.where(live, slots % blocks, DEAD)
+    flip = y.astype(jnp.int32).reshape(1)
+
+    beyond = jnp.maximum(counts - SHALLOW, 0)
+    order = jnp.arange(owners, dtype=jnp.int32)
+    before = jnp.sum(jnp.where(order[None, :] < order[:, None], beyond[None, :], 0), axis=1)
+    too_many = jnp.sum(beyond) > EXTRA
+    depth = cap - SHALLOW
+    place = jnp.where(live[:, SHALLOW:], before[:, None] + jnp.arange(depth, dtype=jnp.int32)[None, :], EXTRA)
+    place = place.reshape(1, owners * depth)
+    taken = place == jnp.arange(EXTRA, dtype=jnp.int32)[:, None]
+    deep = row_values[0, 0, :, SHALLOW:, :].reshape(owners * depth, width)
+    deep = jnp.dot(taken.astype(jnp.bfloat16), deep, preferred_element_type=jnp.float32).astype(jnp.bfloat16)
+    beside = jnp.concatenate([deep[g : g + 16] for g in range(0, EXTRA, 16)], axis=1)
+    both = jnp.concatenate([both, beside], axis=1)
+    packed = 1 + doc * blocks + slots % blocks + order[:, None] * (span * blocks)
+    packed = jnp.sum(jnp.where(taken, packed[:, SHALLOW:].reshape(1, owners * depth), 0), axis=1)
+
+    slots, row_values, both = lax.optimization_barrier((slots, row_values, both))
+    values = row_values[0, 0]
     queries = lax.all_gather(both, "z", axis=0, tiled=True)
+
+    fill = jnp.zeros((owners, LANES - SHALLOW), jnp.int32)
+    near = jnp.concatenate([doc[:, :SHALLOW], fill, block[:, :SHALLOW], fill], axis=1)
+    near = near.reshape(HALVES, z_size, 2 * LANES).transpose(1, 0, 2)
+    code = jnp.maximum(packed - 1, 0)
+    target = code // (span * blocks)
+    ring = jnp.arange(z_size, dtype=jnp.int32)[:, None]
+    wanted = (packed > 0)[None, :] & ((target % z_size)[None, :] == ring)
+    far_block = jnp.where(wanted, (code % blocks + target // z_size * blocks)[None, :], DEAD)
+    far_doc = jnp.broadcast_to((code % (span * blocks)) // blocks, (z_size, EXTRA))
+    blank = jnp.zeros((z_size, LANES - EXTRA), jnp.int32)
+    far = jnp.concatenate([far_doc, blank, far_block, blank], axis=1)[:, None, :]
+    flag = jnp.broadcast_to(too_many.astype(jnp.int32), (z_size, TILE - HALVES - 1, 2 * LANES))
+    meta = jnp.concatenate([near, far, flag], axis=1).astype(jnp.bfloat16)
+    sent = jnp.concatenate([values[:z_size, :SHALLOW], values[z_size:, :SHALLOW], meta], axis=1)
     rows = lax.all_to_all(sent, "z", split_axis=0, concat_axis=0, tiled=True)
 
-    coded = partial_tiles(y.astype(jnp.int32).reshape(1), held(queries), rows, cap=cap, span=span, blocks=blocks)
+    def lean(queries, rows, row_values):
+        return lean_tiles(flip, queries, rows, cap=SHALLOW, span=span, blocks=blocks, extra=EXTRA)
+
+    def full(queries, rows, row_values):
+        meta = jnp.concatenate([doc, block], axis=1).reshape(HALVES, z_size, 2 * cap).transpose(1, 0, 2)
+        meta = jnp.pad(meta, ((0, 0), (0, TILE - HALVES), (0, 0))).astype(jnp.bfloat16)
+        values = row_values[0, 0]
+        sent = jnp.concatenate([values[:z_size], values[z_size:], meta], axis=1)
+        rows = lax.all_to_all(sent, "z", split_axis=0, concat_axis=0, tiled=True)
+        return partial_tiles(flip, queries, rows, cap=cap, span=span, blocks=blocks)
+
+    crowded = jnp.max(rows[:, HALVES * SHALLOW + TILE - 1, 0].astype(jnp.float32)) > 0.5
+    coded = lax.cond(crowded, full, lean, held(queries), rows, row_values)
     parts = lax.all_to_all(coded, ("doc", "y"), split_axis=0, concat_axis=0, tiled=True)
     return summed(parts, blocks=blocks, width=width)
 

time: 216 us -> 210 us (0.972)
  waiting for transfers between devices: 114 us -> 94.3 us
  local copies, waits for them, and re-layouts: 4.66 us -> 11.7 us
  Pallas kernels: 16.9 us -> 20.3 us
    all_gather x1, waiting for transfers between devices: 112 us -> 94.2 us  [per_device(): queries = lax.all_gather(both, 'z', axis=0, tiled=True)]
    concatenate x0 -> x2, local copies, waits for them, and re-layouts: none -> 8.42 us  [the longest x1 8.41 us: per_device(): jnp.concatenate([values[:z_size, :SHALLOW], values[z_size:, :SHALLOW], me...]
    pallas_call x1, Pallas kernels: 15.7 us -> 19 us  [lean_tiles(): pl.pallas_call(functools.partial(lean_kernel, cap=cap, span=span, per_ste...]
  transfers between devices with their start and end apart: 3 -> 3, of which waited for: 2 -> 1; matrix products, arithmetic and copies ran while one was open for 3% -> 7% of each run, Pallas kernels for 0% -> 0%
where the time goes in v4:
time: 210 us
  waiting for transfers between devices  94.3 us (45%)
  blocking collectives  42.7 us (20%)
  starting transfers between devices  20.6 us (10%)
  Pallas kernels  20.3 us (10%)
  between operations  14.9 us (7%)
  local copies, waits for them, and re-layouts  11.7 us (6%)
  other arithmetic  4.99 us (2%)
    all_gather x1, waiting for transfers between devices, per_device(): queries = lax.all_gather(both, 'z', axis=0, tiled=True)  94.2 us
    all_to_all x1, blocking collectives, per_device(): lax.all_to_all(coded, ('doc', 'y'), split_axis=0, concat_axis=0, tiled=True)  42.7 us
    pallas_call x1, Pallas kernels, lean_tiles(): pl.pallas_call(functools.partial(lean_kernel, cap=cap, span=span, per_ste...  19 us
    all_to_all x1, starting transfers between devices, per_device(): rows = lax.all_to_all(sent, 'z', split_axis=0, concat_axis=0, tiled=True)  15 us
    concatenate x1, local copies, waits for them, and re-layouts, per_device(): jnp.concatenate([values[:z_size, :SHALLOW], values[z_size:, :SHALLOW], me...  8.41 us
    ppermute x1, starting transfers between devices, per_device(): mirror = lax.ppermute(theirs, 'y', [(0, 1), (1, 0)])  5.64 us
  transfers between devices with their start and end apart: 3, of which 1 were waited for; matrix products, arithmetic and copies ran while one was open for 7% of the time, Pallas kernels for 0%

profile of v4, /device:TPU:1, one launch (start us, length us, event | category | flops | bytes accessed | tf_op | source)
XLA Modules:
  0.0 210.0 jit_solution(11943906978870569777)
XLA Ops:
  6.5 1.0 constant_dynamic-slice_fusion.1
  7.5 5.6 %collective-permute-start = (bf16[8,3072]{1,0:T(8,128)(2,1)S(1)}, bf16[8,3072]{1,0:T(8,128)(2,1)S(1)}, u32[]{:S(2)}, u32[]{:S(2)}) collective-permute-start(bf16[8,3072]{1,0:T(8,128)(2,1)S(1)} %get-tuple-element.43), channel_id=1, source_target_pairs={{0,16},{16,0},{1,17},{17,1},{2,18},{18,2},{3,19},{19,3},{4,20},{20... | collective-permute-start | bytes 147464 | tf_op jit(solution)/shard_map/ppermute | solution.py:253
  13.2 1.4 fusion.11
  14.5 0.1 select_reduce_fusion.1
  14.7 0.7 iota_compare_fusion.4
  15.4 0.1 add_select_fusion.2
  15.5 1.1 slice.48
  16.6 0.2 convolution_convert_fusion
  16.8 0.7 pad_maximum_fusion.1
  18.3 0.1 add_select_fusion
  18.3 0.1 fusion.4
  18.4 0.1 broadcast_in_dim.79
  18.5 0.1 select_reduce_fusion
  18.7 0.1 maximum_bitcast_fusion
  18.9 0.1 pad_maximum_fusion.2
  19.0 1.0 fusion.12
  20.0 8.4 %concatenate.31 = bf16[16,200,256]{2,1,0:T(8,128)(2,1)} concatenate(bf16[16,96,256]{2,1,0:T(8,128)(2,1)} %get-tuple-element.41, bf16[16,96,256]{2,1,0:T(8,128)(2,1)S(1)} %get-tuple-element.40, bf16[16,2,256]{2,1,0:T(2,128)(2,1)S(1)} %bitcast.29, bf16[16,1,256]{2,1,0:T(2,128)(2,1)S(1)} %copy.12, bf16[16,5,256]{2,1,0:T(8,128)(2,1)S(1)} %broadcast_in_dim.87), dimensions={1} | concatenate | bytes 3276800 | tf_op jit(solution)/shard_map/concatenate | solution.py:296
  28.4 15.0 %all-to-all-start.1 = ((bf16[16,200,256]{2,1,0:T(8,128)(2,1)}), bf16[16,200,256]{2,1,0:T(8,128)(2,1)}, u32[]{:S(2)}, u32[]{:S(2)}) async-start(bf16[16,200,256]{2,1,0:T(8,128)(2,1)} %concatenate.31), calls=%async_computation.1 | async-start | bytes 3276800 | tf_op jit(solution)/shard_map/all_to_all | solution.py:297
  43.4 94.2 %all-gather.2.cloned.1.call-done.q_ref = bf16[256,3840]{1,0:T(8,128)(2,1)} async-done(((bf16[16,3840]{1,0:T(8,128)(2,1)}), bf16[256,3840]{1,0:T(8,128)(2,1)}) %all-gather.2.cloned.1.call-update) | async-done | bytes 1966096 | tf_op jit(solution)/shard_map/all_gather | solution.py:281
  137.6 1.5 slice_reduce_fusion
  139.8 19.3 %conditional.1 = (s16[32,16,2176]{2,1,0:T(8,128)(2,1)S(1)}) conditional(s32[]{:T(128)} %convert_element_type.15, (s32[1]{0:T(128)}, bf16[256,3840]{1,0:T(8,128)(2,1)}, bf16[16,200,256]{2,1,0:T(8,128)(2,1)}) %tuple.13, (bf16[1,1,32,128,256]{4,3,2,1,0:T(8,128)(2,1)S(1)}, s32[32,128]{1,0:T(8,128)S(1)}, s32[32,128]{1,0:T(8,128)S(1)}, s32[1]{0:T(128)}, ...), branch_computations={%region_4.5_spmd, %region_5.6_spmd} | conditional | flops 4831838208 | bytes 24903716 | solution.py:311
  139.8 19.0 %lean_tiles.1 = s16[32,16,2176]{2,1,0:T(8,128)(2,1)S(1)} custom-call(s32[1]{0:T(128)} %get-tuple-element.24.flip_ref, bf16[256,3840]{1,0:T(8,128)(2,1)} %get-tuple-element.25.q_ref.deep_ref, bf16[256,3840]{1,0:T(8,128)(2,1)} %get-tuple-element.25.q_ref.deep_ref, bf16[16,200,256]{2,1,0:T(8,128)(2,1)} %get-tuple-element.26.x_ref), custom_call_target="tpu_custom_call" | custom-call | flops 4831838208 | bytes 3604480 | tf_op jit(solution)/shard_map/cond/branch_0_fun/lean_tiles/pallas_call | solution.py:118
  159.1 42.7 %all_to_all.15.p_ref = s16[32,16,2176]{2,1,0:T(8,128)(2,1)S(1)} all-to-all(s16[32,16,2176]{2,1,0:T(8,128)(2,1)S(1)} %get-tuple-element.56), channel_id=1, replica_groups=mesh['doc'=16,'y'=2,'z'=16] {'doc','y'}, dimensions={0} | all-to-all | bytes 4456448 | tf_op jit(solution)/shard_map/all_to_all | solution.py:312
  201.8 1.3 sum_parts.1
  (35 shorter events, 0.3 us)
Async XLA Ops:
  6.5 11.7 %copy-start.7 = (s32[1,1,32]{2,1,0:T(1,128)S(1)}, s32[1,1,32]{2,1,0:T(1,128)}, u32[]{:S(2)}) copy-start(s32[1,1,32]{2,1,0:T(1,128)} %param.9) | copy-start | bytes 388
  6.5 12.5 %copy-start = (bf16[1,1,32,128,256]{4,3,2,1,0:T(8,128)(2,1)S(1)}, bf16[1,1,32,128,256]{4,3,2,1,0:T(8,128)(2,1)}, u32[]{:S(2)}) copy-start(bf16[1,1,32,128,256]{4,3,2,1,0:T(8,128)(2,1)} %param.7) | copy-start | bytes 6291460
  6.5 11.7 %copy-start.6 = (s32[1,1,32,128]{3,2,1,0:T(8,128)S(1)}, s32[1,1,32,128]{3,2,1,0:T(8,128)}, u32[]{:S(2)}) copy-start(s32[1,1,32,128]{3,2,1,0:T(8,128)} %param.8) | copy-start | bytes 49156
  6.5 131.1 %all-gather.2.cloned.1.call-start = ((), (), s32[]{:S(2)}) async-start(), calls=%async_computation.3 | async-start | bytes 2088960 | tf_op jit(solution)/shard_map/all_gather | solution.py:281
  7.5 9.3 %collective-permute-start = (bf16[8,3072]{1,0:T(8,128)(2,1)S(1)}, bf16[8,3072]{1,0:T(8,128)(2,1)S(1)}, u32[]{:S(2)}, u32[]{:S(2)}) collective-permute-start(bf16[8,3072]{1,0:T(8,128)(2,1)S(1)} %get-tuple-element.43), channel_id=1, source_target_pairs={{0,16},{16,0},{1,17},{17,1},{2,18},{18,2},{3,19},{19,3},{4,20},{20... | collective-permute-start | bytes 147464 | tf_op jit(solution)/shard_map/ppermute | solution.py:253
  18.3 0.6 copy-start.2
  18.3 0.6 copy-start.4
  28.4 109.2 %all-to-all-start.1 = ((bf16[16,200,256]{2,1,0:T(8,128)(2,1)}), bf16[16,200,256]{2,1,0:T(8,128)(2,1)}, u32[]{:S(2)}, u32[]{:S(2)}) async-start(bf16[16,200,256]{2,1,0:T(8,128)(2,1)} %concatenate.31), calls=%async_computation.1 | async-start | bytes 3276800 | tf_op jit(solution)/shard_map/all_to_all | solution.py:297
  137.6 2.2 %copy-start.1 = (bf16[1,1,32,128,256]{4,3,2,1,0:T(8,128)(2,1)S(1)}, bf16[1,1,32,128,256]{4,3,2,1,0:T(8,128)(2,1)}, u32[]{:S(2)}) copy-start(bf16[1,1,32,128,256]{4,3,2,1,0:T(8,128)(2,1)} %param.7) | copy-start | bytes 6291460
  137.6 2.2 %copy-start.3 = (s32[32,128]{1,0:T(8,128)S(1)}, s32[32,128]{1,0:T(8,128)}, u32[]{:S(2)}) copy-start(s32[32,128]{1,0:T(8,128)} %copy-done.2) | copy-start | bytes 49156
  137.6 2.2 %copy-start.5 = (s32[32,128]{1,0:T(8,128)S(1)}, s32[32,128]{1,0:T(8,128)}, u32[]{:S(2)}) copy-start(s32[32,128]{1,0:T(8,128)} %copy-done.4) | copy-start | bytes 49156
Sparse Core Ops, SparseCore 0:
  17.7 119.9 all-gather.1

commit v5 on v4

--- a/solution.py
+++ b/solution.py
@@ -15,7 +15,7 @@
 LANES = 128
 TILE = 8
 SHALLOW = 96
-EXTRA = 48
+EXTRA = 32
 DEAD = 64
 
 
@@ -51,34 +51,33 @@
     width = x_ref.shape[2]
     nq = q_ref.shape[0]
     base = HALVES * cap
+    window = 2 * LANES
     group = 4
-
-    def chosen(doc, docs):
-        rows = lax.broadcasted_iota(jnp.int32, (docs, doc.shape[1]), 0)
-        return jnp.where(rows == doc.astype(jnp.int32), 1.0, 0.0).astype(jnp.bfloat16)
-
-    def picked(doc, first, count):
-        queries = q_ref[:, first * span : (first + count) * span]
-        return jnp.dot(queries, chosen(doc, count * span), preferred_element_type=jnp.float32).astype(jnp.bfloat16)
-
-    metas = [x_ref[k, base : base + TILE, :].astype(jnp.float32) for k in range(per_step)]
-    deep_doc = jnp.concatenate([metas[k][2:3, :extra] + float(k * span) for k in range(per_step)], axis=1)
-    deep_block = jnp.concatenate([metas[k][2:3, LANES : LANES + extra] for k in range(per_step)], axis=1)
-    deep_picked = picked(deep_doc, 0, per_step)
+    places = lax.broadcasted_iota(jnp.int32, (window, window), 0)
+    picked, blocks_of = [], []
+    for k in range(per_step):
+        meta = x_ref[k, base : base + TILE, :].astype(jnp.float32)
+        start = k * span // LANES * LANES
+        doc = meta[0:1, :].astype(jnp.int32) + (k * span - start)
+        chosen = jnp.where(places == doc, 1.0, 0.0).astype(jnp.bfloat16)
+        queries = q_ref[:, start : start + window]
+        picked.append(jnp.dot(queries, chosen, preferred_element_type=jnp.float32).astype(jnp.bfloat16))
+        blocks_of.append(meta[1:2, :])
+    deep_picked = jnp.concatenate([p[:, base : base + extra] for p in picked], axis=1)
+    deep_block = jnp.concatenate([c[:, base : base + extra] for c in blocks_of], axis=1)
     deep_rows = [deep_ref[k * 16 : (k + 1) * 16, g * width : (g + 1) * width] for k in range(per_step) for g in range(extra // 16)]
     for owner in range(HALVES):
+        lanes = slice(owner * cap, (owner + 1) * cap)
         for first in range(0, per_step, group):
-            members = range(first, first + group)
-            doc = jnp.concatenate([metas[k][owner : owner + 1, :cap] + float((k - first) * span) for k in members], axis=1)
-            block = jnp.concatenate([metas[k][owner : owner + 1, LANES : LANES + cap] for k in members], axis=1)
-            got = picked(doc, first, group)
+            got = jnp.concatenate([p[:, lanes] for p in picked[first : first + group]], axis=1)
+            block = jnp.concatenate([c[:, lanes] for c in blocks_of[first : first + group]], axis=1)
             for b in range(blocks):
                 kept = got * jnp.where(block == float(b), 1.0, 0.0).astype(jnp.bfloat16)
                 left[owner, b * nq : (b + 1) * nq, first * cap : (first + group) * cap] = kept
         for b in range(blocks):
             kept = deep_picked * jnp.where(deep_block == float(b + owner * blocks), 1.0, 0.0).astype(jnp.bfloat16)
             left[owner, b * nq : (b + 1) * nq, per_step * cap :] = kept
-        right = jnp.concatenate([x_ref[k, owner * cap : (owner + 1) * cap, :] for k in range(per_step)] + deep_rows, axis=0)
+        right = jnp.concatenate([x_ref[k, lanes, :] for k in range(per_step)] + deep_rows, axis=0)
         product = jnp.dot(left[owner], right, preferred_element_type=jnp.float32)
 
         @pl.when(step == 0)
@@ -199,6 +198,60 @@
     )(flip, queries, rows)
 
 
+def payload_kernel(counts_ref, info_ref, slots_ref, far_ref, low_ref, high_ref, o_ref, *, shallow, extra, blocks):
+    step = pl.program_id(0)
+    here, z_size = low_ref.shape[0], low_ref.shape[0] * pl.num_programs(0)
+    lane = lax.broadcasted_iota(jnp.int32, (1, slots_ref.shape[1]), 1)
+    base = HALVES * shallow
+    rest = o_ref.shape[2] - base - extra
+    for r in range(here):
+        z = step * here + r
+        docs, ids = [], []
+        for half in range(HALVES):
+            owner = half * z_size + z
+            slots = slots_ref[pl.ds(owner, 1), :]
+            doc = lax.shift_right_logical(slots, blocks.bit_length() - 1) - info_ref[0]
+            block = jnp.where(lane < counts_ref[owner], slots & (blocks - 1), DEAD)
+            docs.append(doc[:, :shallow].astype(jnp.float32))
+            ids.append(block[:, :shallow].astype(jnp.float32))
+        far = jnp.where(far_ref[2:3, :] == z, far_ref[1:2, :], DEAD)
+        docs.append(far_ref[0:1, :extra].astype(jnp.float32))
+        ids.append(far[:, :extra].astype(jnp.float32))
+        docs.append(jnp.zeros((1, rest), jnp.float32))
+        ids.append(jnp.full((1, rest), float(DEAD), jnp.float32))
+        flag = jnp.full((TILE - 2, o_ref.shape[2]), info_ref[1].astype(jnp.float32))
+        meta = jnp.concatenate([jnp.concatenate(docs, axis=1), jnp.concatenate(ids, axis=1), flag], axis=0)
+        o_ref[r, :shallow, :] = low_ref[r, :shallow, :]
+        o_ref[r, shallow:base, :] = high_ref[r, :shallow, :]
+        o_ref[r, base:, :] = meta.astype(jnp.bfloat16)
+
+
+def payload(counts, info, slots, far, values, *, blocks, per_step=4):
+    owners, cap, width = values.shape
+    z_size = owners // HALVES
+    depth = HALVES * SHALLOW + TILE
+    steps = z_size // per_step
+    grid_spec = pltpu.PrefetchScalarGridSpec(
+        num_scalar_prefetch=2,
+        grid=(steps,),
+        in_specs=[
+            pl.BlockSpec(slots.shape, lambda i, *_: (0, 0)),
+            pl.BlockSpec(far.shape, lambda i, *_: (0, 0)),
+            pl.BlockSpec((per_step, cap, width), lambda i, *_: (i, 0, 0)),
+            pl.BlockSpec((per_step, cap, width), lambda i, *_: (i + steps, 0, 0)),
+        ],
+        out_specs=pl.BlockSpec((per_step, depth, width), lambda i, *_: (i, 0, 0)),
+    )
+    return pl.pallas_call(
+        functools.partial(payload_kernel, shallow=SHALLOW, extra=EXTRA, blocks=blocks),
+        grid_spec=grid_spec,
+        out_shape=jax.ShapeDtypeStruct((z_size, depth, width), jnp.bfloat16),
+        compiler_params=pltpu.CompilerParams(vmem_limit_bytes=16 << 20),
+        cost_estimate=pl.CostEstimate(flops=0, bytes_accessed=4 * values.size, transcendentals=0),
+        name="payload",
+    )(counts, info, slots, far, values, values)
+
+
 def held_kernel(q_ref, o_ref):
     pltpu.touch(o_ref)
 
@@ -277,23 +330,18 @@
     packed = jnp.sum(jnp.where(taken, packed[:, SHALLOW:].reshape(1, owners * depth), 0), axis=1)
 
     slots, row_values, both = lax.optimization_barrier((slots, row_values, both))
-    values = row_values[0, 0]
     queries = lax.all_gather(both, "z", axis=0, tiled=True)
 
-    fill = jnp.zeros((owners, LANES - SHALLOW), jnp.int32)
-    near = jnp.concatenate([doc[:, :SHALLOW], fill, block[:, :SHALLOW], fill], axis=1)
-    near = near.reshape(HALVES, z_size, 2 * LANES).transpose(1, 0, 2)
     code = jnp.maximum(packed - 1, 0)
     target = code // (span * blocks)
-    ring = jnp.arange(z_size, dtype=jnp.int32)[:, None]
-    wanted = (packed > 0)[None, :] & ((target % z_size)[None, :] == ring)
-    far_block = jnp.where(wanted, (code % blocks + target // z_size * blocks)[None, :], DEAD)
-    far_doc = jnp.broadcast_to((code % (span * blocks)) // blocks, (z_size, EXTRA))
-    blank = jnp.zeros((z_size, LANES - EXTRA), jnp.int32)
-    far = jnp.concatenate([far_doc, blank, far_block, blank], axis=1)[:, None, :]
-    flag = jnp.broadcast_to(too_many.astype(jnp.int32), (z_size, TILE - HALVES - 1, 2 * LANES))
-    meta = jnp.concatenate([near, far, flag], axis=1).astype(jnp.bfloat16)
-    sent = jnp.concatenate([values[:z_size, :SHALLOW], values[z_size:, :SHALLOW], meta], axis=1)
+    far = jnp.stack([
+        code % (span * blocks) // blocks,
+        code % blocks + target // z_size * blocks,
+        jnp.where(packed > 0, target % z_size, z_size),
+    ])
+    far = jnp.pad(far, ((0, TILE - 3), (0, LANES - EXTRA)))
+    info = jnp.stack([me * span, too_many.astype(jnp.int32)])
+    sent = payload(counts, info, slots, far, row_values[0, 0], blocks=blocks)
     rows = lax.all_to_all(sent, "z", split_axis=0, concat_axis=0, tiled=True)
 
     def lean(queries, rows, row_values):

time: 210 us -> 204 us (0.971)
  local copies, waits for them, and re-layouts: 11.7 us -> 3.45 us
  waiting for transfers between devices: 94.3 us -> 102 us
  blocking collectives: 42.7 us -> 38.3 us
    concatenate x2 -> x0, local copies, waits for them, and re-layouts: 8.42 us -> none  [the longest x1 8.41 us: per_device(): jnp.concatenate([values[:z_size, :SHALLOW], values[z_size:, :SHALLOW], me...]
    all_gather x1, waiting for transfers between devices: 94.2 us -> 102 us  [per_device(): queries = lax.all_gather(both, 'z', axis=0, tiled=True)]
    all_to_all x1, blocking collectives: 42.7 us -> 38.3 us  [per_device(): lax.all_to_all(coded, ('doc', 'y'), split_axis=0, concat_axis=0, tiled=True)]
    pallas_call x1, Pallas kernels: 19 us -> 15.8 us  [lean_tiles(): pl.pallas_call(functools.partial(lean_kernel, cap=cap, span=span, per_ste...]
    pallas_call x0 -> x1, Pallas kernels: none -> 2.39 us  [payload(): pl.pallas_call(functools.partial(payload_kernel, shallow=SHALLOW, extra=E...]
  transfers between devices with their start and end apart: 3 -> 3, of which waited for: 1 -> 1; matrix products, arithmetic and copies ran while one was open for 7% -> 2% of each run, Pallas kernels for 0% -> 1%
where the time goes in v5:
time: 204 us
  waiting for transfers between devices  102 us (50%)
  blocking collectives  38.3 us (19%)
  starting transfers between devices  20.6 us (10%)
  Pallas kernels  19.5 us (10%)
  between operations  14.8 us (7%)
  other arithmetic  4.75 us (2%)
  local copies, waits for them, and re-layouts  3.45 us (2%)
    all_gather x1, waiting for transfers between devices, per_device(): queries = lax.all_gather(both, 'z', axis=0, tiled=True)  102 us
    all_to_all x1, blocking collectives, per_device(): lax.all_to_all(coded, ('doc', 'y'), split_axis=0, concat_axis=0, tiled=True)  38.3 us
    pallas_call x1, Pallas kernels, lean_tiles(): pl.pallas_call(functools.partial(lean_kernel, cap=cap, span=span, per_ste...  15.8 us
    all_to_all x1, starting transfers between devices, per_device(): rows = lax.all_to_all(sent, 'z', split_axis=0, concat_axis=0, tiled=True)  15 us
    ppermute x1, starting transfers between devices, per_device(): mirror = lax.ppermute(theirs, 'y', [(0, 1), (1, 0)])  5.64 us
  transfers between devices with their start and end apart: 3, of which 1 were waited for; matrix products, arithmetic and copies ran while one was open for 2% of the time, Pallas kernels for 1%

profile of v5, /device:TPU:1, one launch (start us, length us, event | category | flops | bytes accessed | tf_op | source)
XLA Modules:
  0.0 203.6 jit_solution(11616809154927682388)
XLA Ops:
  6.5 1.0 constant_dynamic-slice_fusion.1
  7.5 5.6 %collective-permute-start = (bf16[8,3072]{1,0:T(8,128)(2,1)S(1)}, bf16[8,3072]{1,0:T(8,128)(2,1)S(1)}, u32[]{:S(2)}, u32[]{:S(2)}) collective-permute-start(bf16[8,3072]{1,0:T(8,128)(2,1)S(1)} %get-tuple-element.47), channel_id=1, source_target_pairs={{0,16},{16,0},{1,17},{17,1},{2,18},{18,2},{3,19},{19,3},{4,20},{20... | collective-permute-start | bytes 147464 | tf_op jit(solution)/shard_map/ppermute | solution.py:306
  13.2 1.3 add_maximum_fusion.1
  14.5 0.1 select_reduce_fusion.1
  14.6 0.7 iota_compare_fusion.4
  15.3 0.6 copy-done.8
  15.9 0.1 add_select_fusion.2
  16.0 0.1 eq.22
  16.1 1.1 slice.31
  17.1 0.2 convolution_convert_fusion
  17.4 0.7 pad_maximum_fusion.1
  18.7 0.6 copy-done.4
  19.3 0.1 fusion.4
  19.3 0.1 broadcast_in_dim.48
  19.4 0.1 select_reduce_fusion
  19.6 0.1 pad_add_fusion.1.info_ref
  19.7 2.4 %payload.1 = bf16[16,200,256]{2,1,0:T(8,128)(2,1)} custom-call(s32[32]{0:T(128)S(1)} %bitcast.62, s32[2]{0:T(128)S(1)} %pad_add_fusion.1.info_ref, s32[32,128]{1,0:T(8,128)S(1)} %bitcast.60, s32[8,128]{1,0:T(8,128)S(1)} %pad.9.far_ref, bf16[32,128,256]{2,1,0:T(8,128)(2,1)S(1)} %bitcast.63, bf16[32,128,256]{2,1,0:T(8,128)(2,1)S(1)} %bitcast.64), custom_call_target="tpu_custom_call" | custom-call | bytes 4194304 | tf_op jit(solution)/shard_map/payload/pallas_call | solution.py:245
  22.1 15.0 %all-to-all-start.1 = ((bf16[16,200,256]{2,1,0:T(8,128)(2,1)}), bf16[16,200,256]{2,1,0:T(8,128)(2,1)}, u32[]{:S(2)}, u32[]{:S(2)}) async-start(bf16[16,200,256]{2,1,0:T(8,128)(2,1)} %payload.1), calls=%async_computation.1 | async-start | bytes 3276800 | tf_op jit(solution)/shard_map/all_to_all | solution.py:345
  37.1 101.8 %all-gather.2.cloned.1.call-done.q_ref = bf16[256,3584]{1,0:T(8,128)(2,1)} async-done(((bf16[16,3584]{1,0:T(8,128)(2,1)}), bf16[256,3584]{1,0:T(8,128)(2,1)}) %all-gather.2.cloned.1.call-update) | async-done | bytes 1835024 | tf_op jit(solution)/shard_map/all_gather | solution.py:333
  138.9 1.5 slice_reduce_fusion
  141.1 16.0 %conditional.1 = (s16[32,16,2176]{2,1,0:T(8,128)(2,1)S(1)}) conditional(s32[]{:T(128)} %convert_element_type.5, (s32[1]{0:T(128)}, bf16[256,3584]{1,0:T(8,128)(2,1)}, bf16[16,200,256]{2,1,0:T(8,128)(2,1)}) %tuple.14, (bf16[1,1,32,128,256]{4,3,2,1,0:T(8,128)(2,1)S(1)}, s32[32,128]{1,0:T(8,128)S(1)}, pred[32,128]{1,0:T(8,128)(4,1)S(1)}, ...), branch_computations={%region_4.5_spmd, %region_5.6_spmd} | conditional | flops 4303663104 | bytes 24252452 | solution.py:359
  141.1 15.8 %lean_tiles.1 = s16[32,16,2176]{2,1,0:T(8,128)(2,1)S(1)} custom-call(s32[1]{0:T(128)} %get-tuple-element.29.flip_ref, bf16[256,3584]{1,0:T(8,128)(2,1)} %get-tuple-element.30.q_ref.deep_ref, bf16[256,3584]{1,0:T(8,128)(2,1)} %get-tuple-element.30.q_ref.deep_ref, bf16[16,200,256]{2,1,0:T(8,128)(2,1)} %get-tuple-element.31.x_ref), custom_call_target="tpu_custom_call" | custom-call | flops 4294967296 | bytes 3473408 | tf_op jit(solution)/shard_map/cond/branch_0_fun/lean_tiles/pallas_call | solution.py:117
  157.1 38.3 %all_to_all.15.p_ref = s16[32,16,2176]{2,1,0:T(8,128)(2,1)S(1)} all-to-all(s16[32,16,2176]{2,1,0:T(8,128)(2,1)S(1)} %get-tuple-element.57), channel_id=1, replica_groups=mesh['doc'=16,'y'=2,'z'=16] {'doc','y'}, dimensions={0} | all-to-all | bytes 4456448 | tf_op jit(solution)/shard_map/all_to_all | solution.py:360
  195.4 1.3 sum_parts.1
  (29 shorter events, 0.1 us)
Async XLA Ops:
  6.5 13.2 %copy-start.1 = (s32[1,1,32]{2,1,0:T(1,128)S(1)}, s32[1,1,32]{2,1,0:T(1,128)}, u32[]{:S(2)}) copy-start(s32[1,1,32]{2,1,0:T(1,128)} %param.9) | copy-start | bytes 388
  6.5 13.2 %copy-start.2 = (bf16[1,1,32,128,256]{4,3,2,1,0:T(8,128)(2,1)S(1)}, bf16[1,1,32,128,256]{4,3,2,1,0:T(8,128)(2,1)}, u32[]{:S(2)}) copy-start(bf16[1,1,32,128,256]{4,3,2,1,0:T(8,128)(2,1)} %param.7) | copy-start | bytes 6291460
  6.5 12.1 %copy-start = (s32[1,1,32,128]{3,2,1,0:T(8,128)S(1)}, s32[1,1,32,128]{3,2,1,0:T(8,128)}, u32[]{:S(2)}) copy-start(s32[1,1,32,128]{3,2,1,0:T(8,128)} %param.8) | copy-start | bytes 49156
  6.5 132.3 %all-gather.2.cloned.1.call-start = ((), (), s32[]{:S(2)}) async-start(), calls=%async_computation.3 | async-start | bytes 1949696 | tf_op jit(solution)/shard_map/all_gather | solution.py:333
  7.5 9.8 %collective-permute-start = (bf16[8,3072]{1,0:T(8,128)(2,1)S(1)}, bf16[8,3072]{1,0:T(8,128)(2,1)S(1)}, u32[]{:S(2)}, u32[]{:S(2)}) collective-permute-start(bf16[8,3072]{1,0:T(8,128)(2,1)S(1)} %get-tuple-element.47), channel_id=1, source_target_pairs={{0,16},{16,0},{1,17},{17,1},{2,18},{18,2},{3,19},{19,3},{4,20},{20... | collective-permute-start | bytes 147464 | tf_op jit(solution)/shard_map/ppermute | solution.py:306
  15.3 0.6 copy-start.8
  18.7 0.6 copy-start.4
  18.7 0.6 copy-start.6
  22.1 116.8 %all-to-all-start.1 = ((bf16[16,200,256]{2,1,0:T(8,128)(2,1)}), bf16[16,200,256]{2,1,0:T(8,128)(2,1)}, u32[]{:S(2)}, u32[]{:S(2)}) async-start(bf16[16,200,256]{2,1,0:T(8,128)(2,1)} %payload.1), calls=%async_computation.1 | async-start | bytes 3276800 | tf_op jit(solution)/shard_map/all_to_all | solution.py:345
  138.9 2.2 %copy-start.3 = (bf16[1,1,32,128,256]{4,3,2,1,0:T(8,128)(2,1)S(1)}, bf16[1,1,32,128,256]{4,3,2,1,0:T(8,128)(2,1)}, u32[]{:S(2)}) copy-start(bf16[1,1,32,128,256]{4,3,2,1,0:T(8,128)(2,1)} %param.7) | copy-start | bytes 6291460
  138.9 2.2 %copy-start.5 = (s32[32,128]{1,0:T(8,128)S(1)}, s32[32,128]{1,0:T(8,128)}, u32[]{:S(2)}) copy-start(s32[32,128]{1,0:T(8,128)} %copy-done.4) | copy-start | bytes 49156
  138.9 2.2 %copy-start.7 = (s32[32,128]{1,0:T(8,128)S(1)}, s32[32,128]{1,0:T(8,128)}, u32[]{:S(2)}) copy-start(s32[32,128]{1,0:T(8,128)} %copy-done.6) | copy-start | bytes 49156
  138.9 2.2 %copy-start.9 = (pred[32,128]{1,0:T(8,128)(4,1)S(1)}, pred[32,128]{1,0:T(8,128)(4,1)}, u32[]{:S(2)}) copy-start(pred[32,128]{1,0:T(8,128)(4,1)} %copy-done.8) | copy-start | bytes 12292
Sparse Core Ops, SparseCore 0:
  18.2 120.6 all-gather.1

commit v6 on v5

--- a/solution.py
+++ b/solution.py
@@ -46,72 +46,75 @@
                 o_ref[target, :, blocks * width :] = code.astype(jnp.int32).astype(jnp.int16)
 
 
-def lean_kernel(flip_ref, q_ref, deep_ref, x_ref, o_ref, left, acc, *, cap, span, per_step, blocks, extra):
+def lean_kernel(place_ref, q_ref, deep_ref, far_ref, x_ref, o_ref, left, acc, right_ref, *, cap, span, per_step, blocks, extra):
     step = pl.program_id(0)
     width = x_ref.shape[2]
     nq = q_ref.shape[0]
     base = HALVES * cap
     window = 2 * LANES
-    group = 4
+    tall = blocks * nq
+    lane = lax.broadcasted_iota(jnp.int32, (1, LANES), 1)
+
+    @pl.when(step == 0)
+    def _():
+        acc[...] = jnp.zeros_like(acc)
+
     places = lax.broadcasted_iota(jnp.int32, (window, window), 0)
-    picked, blocks_of = [], []
     for k in range(per_step):
         meta = x_ref[k, base : base + TILE, :].astype(jnp.float32)
+        far = far_ref[k * 16 : k * 16 + TILE, :].astype(jnp.float32)
+        docs, ids = [], []
+        for owner in range(HALVES):
+            lanes = slice(owner * LANES, (owner + 1) * LANES)
+            to_owner = far[2:3, :] == (place_ref[1] + owner * place_ref[2]).astype(jnp.float32)
+            docs.append(jnp.where(lane < cap, meta[0:1, lanes], far[0:1, :]))
+            ids.append(jnp.where(lane < cap, meta[1:2, lanes], jnp.where(to_owner, far[1:2, :], float(DEAD))))
         start = k * span // LANES * LANES
-        doc = meta[0:1, :].astype(jnp.int32) + (k * span - start)
+        doc = jnp.concatenate(docs, axis=1).astype(jnp.int32) + (k * span - start)
         chosen = jnp.where(places == doc, 1.0, 0.0).astype(jnp.bfloat16)
         queries = q_ref[:, start : start + window]
-        picked.append(jnp.dot(queries, chosen, preferred_element_type=jnp.float32).astype(jnp.bfloat16))
-        blocks_of.append(meta[1:2, :])
-    deep_picked = jnp.concatenate([p[:, base : base + extra] for p in picked], axis=1)
-    deep_block = jnp.concatenate([c[:, base : base + extra] for c in blocks_of], axis=1)
-    deep_rows = [deep_ref[k * 16 : (k + 1) * 16, g * width : (g + 1) * width] for k in range(per_step) for g in range(extra // 16)]
+        picked = jnp.dot(queries, chosen, preferred_element_type=jnp.float32).astype(jnp.bfloat16)
+        for owner in range(HALVES):
+            lanes = slice(owner * LANES, (owner + 1) * LANES)
+            for b in range(blocks):
+                kept = picked[:, lanes] * jnp.where(ids[owner] == float(b), 1.0, 0.0).astype(jnp.bfloat16)
+                left[owner * tall + b * nq : owner * tall + (b + 1) * nq, k * LANES : (k + 1) * LANES] = kept
     for owner in range(HALVES):
-        lanes = slice(owner * cap, (owner + 1) * cap)
-        for first in range(0, per_step, group):
-            got = jnp.concatenate([p[:, lanes] for p in picked[first : first + group]], axis=1)
-            block = jnp.concatenate([c[:, lanes] for c in blocks_of[first : first + group]], axis=1)
-            for b in range(blocks):
-                kept = got * jnp.where(block == float(b), 1.0, 0.0).astype(jnp.bfloat16)
-                left[owner, b * nq : (b + 1) * nq, first * cap : (first + group) * cap] = kept
-        for b in range(blocks):
-            kept = deep_picked * jnp.where(deep_block == float(b + owner * blocks), 1.0, 0.0).astype(jnp.bfloat16)
-            left[owner, b * nq : (b + 1) * nq, per_step * cap :] = kept
-        right = jnp.concatenate([x_ref[k, lanes, :] for k in range(per_step)] + deep_rows, axis=0)
-        product = jnp.dot(left[owner], right, preferred_element_type=jnp.float32)
-
-        @pl.when(step == 0)
-        def _():
-            acc[owner] = product
-
-        @pl.when(step > 0)
-        def _():
-            acc[owner] += product
+        right = []
+        for k in range(per_step):
+            right.append(x_ref[k, owner * cap : (owner + 1) * cap, :])
+            right += [deep_ref[k * 16 : (k + 1) * 16, g * width : (g + 1) * width] for g in range(extra // 16)]
+        right = jnp.concatenate(right, axis=0)
+        right_ref[...] = right
+        acc[owner] += jnp.dot(left[owner * tall : (owner + 1) * tall, :], right_ref[...], preferred_element_type=jnp.float32)
 
     @pl.when(step == pl.num_programs(0) - 1)
     def _():
-        code_tiles(flip_ref, acc, o_ref, nq=nq, blocks=blocks)
-
-
-def lean_tiles(flip, queries, rows, *, cap, span, blocks, extra, per_step=8):
+        code_tiles(place_ref, acc, o_ref, nq=nq, blocks=blocks)
+
+
+def lean_tiles(place, queries, rows, *, cap, span, blocks, extra, per_step=8):
     nq = queries.shape[0]
     sources, depth, width = rows.shape
     lanes = blocks * width + LANES
     targets = 16 * HALVES
     deep_lanes = extra // 16 * width
     deep_at = sources * span // deep_lanes
+    far_at = (deep_at + 1) * deep_lanes // LANES
     grid_spec = pltpu.PrefetchScalarGridSpec(
         num_scalar_prefetch=1,
         grid=(sources // per_step,),
         in_specs=[
             pl.BlockSpec((nq, per_step * span), lambda i, _: (0, i)),
             pl.BlockSpec((per_step * 16, deep_lanes), lambda i, _: (i, deep_at)),
+            pl.BlockSpec((per_step * 16, LANES), lambda i, _: (i, far_at)),
             pl.BlockSpec((per_step, depth, width), lambda i, _: (i, 0, 0)),
         ],
         out_specs=pl.BlockSpec((targets, nq // 16, lanes), lambda i, _: (0, 0, 0)),
         scratch_shapes=[
-            pltpu.VMEM((HALVES, blocks * nq, per_step * (cap + extra)), jnp.bfloat16),
+            pltpu.VMEM((HALVES * blocks * nq, per_step * (cap + extra)), jnp.bfloat16),
             pltpu.VMEM((HALVES, blocks * nq, width), jnp.float32),
+            pltpu.VMEM((per_step * (cap + extra), width), jnp.bfloat16),
         ],
     )
     return pl.pallas_call(
@@ -125,7 +128,7 @@
             transcendentals=0,
         ),
         name="lean_tiles",
-    )(flip, queries, queries, rows)
+    )(place, queries, queries, queries, rows)
 
 
 def gram_kernel(flip_ref, q_ref, x_ref, o_ref, left, acc, *, cap, span, per_step, blocks):
@@ -198,35 +201,28 @@
     )(flip, queries, rows)
 
 
-def payload_kernel(counts_ref, info_ref, slots_ref, far_ref, low_ref, high_ref, o_ref, *, shallow, extra, blocks):
+def payload_kernel(counts_ref, first_ref, slots_ref, low_ref, high_ref, o_ref, *, shallow, blocks):
     step = pl.program_id(0)
     here, z_size = low_ref.shape[0], low_ref.shape[0] * pl.num_programs(0)
     lane = lax.broadcasted_iota(jnp.int32, (1, slots_ref.shape[1]), 1)
     base = HALVES * shallow
-    rest = o_ref.shape[2] - base - extra
     for r in range(here):
         z = step * here + r
         docs, ids = [], []
         for half in range(HALVES):
             owner = half * z_size + z
             slots = slots_ref[pl.ds(owner, 1), :]
-            doc = lax.shift_right_logical(slots, blocks.bit_length() - 1) - info_ref[0]
-            block = jnp.where(lane < counts_ref[owner], slots & (blocks - 1), DEAD)
-            docs.append(doc[:, :shallow].astype(jnp.float32))
-            ids.append(block[:, :shallow].astype(jnp.float32))
-        far = jnp.where(far_ref[2:3, :] == z, far_ref[1:2, :], DEAD)
-        docs.append(far_ref[0:1, :extra].astype(jnp.float32))
-        ids.append(far[:, :extra].astype(jnp.float32))
-        docs.append(jnp.zeros((1, rest), jnp.float32))
-        ids.append(jnp.full((1, rest), float(DEAD), jnp.float32))
-        flag = jnp.full((TILE - 2, o_ref.shape[2]), info_ref[1].astype(jnp.float32))
-        meta = jnp.concatenate([jnp.concatenate(docs, axis=1), jnp.concatenate(ids, axis=1), flag], axis=0)
+            doc = lax.shift_right_logical(slots, blocks.bit_length() - 1) - first_ref[0]
+            docs.append(doc.astype(jnp.float32))
+            ids.append(jnp.where(lane < counts_ref[owner], slots & (blocks - 1), DEAD).astype(jnp.float32))
+        rest = jnp.zeros((TILE - 2, o_ref.shape[2]), jnp.float32)
+        meta = jnp.concatenate([jnp.concatenate(docs, axis=1), jnp.concatenate(ids, axis=1), rest], axis=0)
         o_ref[r, :shallow, :] = low_ref[r, :shallow, :]
         o_ref[r, shallow:base, :] = high_ref[r, :shallow, :]
         o_ref[r, base:, :] = meta.astype(jnp.bfloat16)
 
 
-def payload(counts, info, slots, far, values, *, blocks, per_step=4):
+def payload(counts, first, slots, values, *, blocks, per_step=4):
     owners, cap, width = values.shape
     z_size = owners // HALVES
     depth = HALVES * SHALLOW + TILE
@@ -236,36 +232,19 @@
         grid=(steps,),
         in_specs=[
             pl.BlockSpec(slots.shape, lambda i, *_: (0, 0)),
-            pl.BlockSpec(far.shape, lambda i, *_: (0, 0)),
             pl.BlockSpec((per_step, cap, width), lambda i, *_: (i, 0, 0)),
             pl.BlockSpec((per_step, cap, width), lambda i, *_: (i + steps, 0, 0)),
         ],
         out_specs=pl.BlockSpec((per_step, depth, width), lambda i, *_: (i, 0, 0)),
     )
     return pl.pallas_call(
-        functools.partial(payload_kernel, shallow=SHALLOW, extra=EXTRA, blocks=blocks),
+        functools.partial(payload_kernel, shallow=SHALLOW, blocks=blocks),
         grid_spec=grid_spec,
         out_shape=jax.ShapeDtypeStruct((z_size, depth, width), jnp.bfloat16),
         compiler_params=pltpu.CompilerParams(vmem_limit_bytes=16 << 20),
         cost_estimate=pl.CostEstimate(flops=0, bytes_accessed=4 * values.size, transcendentals=0),
         name="payload",
-    )(counts, info, slots, far, values, values)
-
-
-def held_kernel(q_ref, o_ref):
-    pltpu.touch(o_ref)
-
-
-def held(queries):
-    return pl.pallas_call(
-        held_kernel,
-        out_shape=jax.ShapeDtypeStruct(queries.shape, queries.dtype),
-        in_specs=[pl.BlockSpec(memory_space=pl.ANY)],
-        out_specs=pl.BlockSpec(memory_space=pl.ANY),
-        input_output_aliases={0: 0},
-        cost_estimate=pl.CostEstimate(flops=10**12, bytes_accessed=10**6, transcendentals=0),
-        name="held",
-    )(queries)
+    )(counts, first, slots, values, values)
 
 
 def sum_kernel(p_ref, o_ref, *, blocks, width):
@@ -300,20 +279,18 @@
     y = lax.axis_index("y")
     me = y * z_size + lax.axis_index("z")
 
+    slots = row_slots[0, 0]
+    counts = row_counts[0, 0]
+    sent = payload(counts, (me * span).reshape(1), slots, row_values[0, 0], blocks=blocks)
+    rows = lax.all_to_all(sent, "z", split_axis=0, concat_axis=0, tiled=True)
+
     half_docs = doc_count // HALVES
     mine = lax.dynamic_slice_in_dim(query_rows, y * half_docs, half_docs, 1)
     theirs = lax.dynamic_slice_in_dim(query_rows, (1 - y) * half_docs, half_docs, 1)
     mirror = lax.ppermute(theirs, "y", [(0, 1), (1, 0)])
-    both = jnp.concatenate([mine, mirror], axis=0)
-
-    slots = row_slots[0, 0]
-    counts = row_counts[0, 0]
-    places = jnp.arange(cap, dtype=jnp.int32)
-    live = places[None, :] < counts[:, None]
+
+    live = jnp.arange(cap, dtype=jnp.int32)[None, :] < counts[:, None]
     doc = slots // blocks - me * span
-    block = jnp.where(live, slots % blocks, DEAD)
-    flip = y.astype(jnp.int32).reshape(1)
-
     beyond = jnp.maximum(counts - SHALLOW, 0)
     order = jnp.arange(owners, dtype=jnp.int32)
     before = jnp.sum(jnp.where(order[None, :] < order[:, None], beyond[None, :], 0), axis=1)
@@ -324,30 +301,24 @@
     taken = place == jnp.arange(EXTRA, dtype=jnp.int32)[:, None]
     deep = row_values[0, 0, :, SHALLOW:, :].reshape(owners * depth, width)
     deep = jnp.dot(taken.astype(jnp.bfloat16), deep, preferred_element_type=jnp.float32).astype(jnp.bfloat16)
-    beside = jnp.concatenate([deep[g : g + 16] for g in range(0, EXTRA, 16)], axis=1)
-    both = jnp.concatenate([both, beside], axis=1)
     packed = 1 + doc * blocks + slots % blocks + order[:, None] * (span * blocks)
     packed = jnp.sum(jnp.where(taken, packed[:, SHALLOW:].reshape(1, owners * depth), 0), axis=1)
-
-    slots, row_values, both = lax.optimization_barrier((slots, row_values, both))
+    code = jnp.maximum(packed - 1, 0)
+    target = jnp.where(packed > 0, code // (span * blocks), DEAD)
+    flag = jnp.broadcast_to(too_many.astype(jnp.int32), (EXTRA,))
+    far = jnp.stack([code % (span * blocks) // blocks, code % blocks, target, flag]).astype(jnp.bfloat16)
+    far = jnp.pad(far, ((0, 16 - 4), (SHALLOW, LANES - SHALLOW - EXTRA)))
+    beside = jnp.concatenate([deep[g : g + 16] for g in range(0, EXTRA, 16)] + [far], axis=1)
+    both = jnp.concatenate([jnp.concatenate([mine, mirror], axis=0), beside], axis=1)
     queries = lax.all_gather(both, "z", axis=0, tiled=True)
-
-    code = jnp.maximum(packed - 1, 0)
-    target = code // (span * blocks)
-    far = jnp.stack([
-        code % (span * blocks) // blocks,
-        code % blocks + target // z_size * blocks,
-        jnp.where(packed > 0, target % z_size, z_size),
-    ])
-    far = jnp.pad(far, ((0, TILE - 3), (0, LANES - EXTRA)))
-    info = jnp.stack([me * span, too_many.astype(jnp.int32)])
-    sent = payload(counts, info, slots, far, row_values[0, 0], blocks=blocks)
-    rows = lax.all_to_all(sent, "z", split_axis=0, concat_axis=0, tiled=True)
+    flip = y.astype(jnp.int32).reshape(1)
 
     def lean(queries, rows, row_values):
-        return lean_tiles(flip, queries, rows, cap=SHALLOW, span=span, blocks=blocks, extra=EXTRA)
+        place = jnp.stack([y, lax.axis_index("z"), z_size]).astype(jnp.int32)
+        return lean_tiles(place, queries, rows, cap=SHALLOW, span=span, blocks=blocks, extra=EXTRA)
 
     def full(queries, rows, row_values):
+        block = jnp.where(live, slots % blocks, DEAD)
         meta = jnp.concatenate([doc, block], axis=1).reshape(HALVES, z_size, 2 * cap).transpose(1, 0, 2)
         meta = jnp.pad(meta, ((0, 0), (0, TILE - HALVES), (0, 0))).astype(jnp.bfloat16)
         values = row_values[0, 0]
@@ -355,8 +326,9 @@
         rows = lax.all_to_all(sent, "z", split_axis=0, concat_axis=0, tiled=True)
         return partial_tiles(flip, queries, rows, cap=cap, span=span, blocks=blocks)
 
-    crowded = jnp.max(rows[:, HALVES * SHALLOW + TILE - 1, 0].astype(jnp.float32)) > 0.5
-    coded = lax.cond(crowded, full, lean, held(queries), rows, row_values)
+    flags = queries[:, -LANES:].reshape(z_size, 16, LANES)[:, 3, SHALLOW]
+    crowded = jnp.max(flags.astype(jnp.float32)) > 0.5
+    coded = lax.cond(crowded, full, lean, queries, rows, row_values)
     parts = lax.all_to_all(coded, ("doc", "y"), split_axis=0, concat_axis=0, tiled=True)
     return summed(parts, blocks=blocks, width=width)
 

time: 204 us -> 203 us (level)
    pallas_call x1, Pallas kernels: 15.8 us -> 12.2 us  [lean_tiles(): pl.pallas_call(functools.partial(lean_kernel, cap=cap, span=span, per_ste...]
    all_to_all x1, blocking collectives: 38.3 us -> 40.3 us  [per_device(): lax.all_to_all(coded, ('doc', 'y'), split_axis=0, concat_axis=0, tiled=True)]
    pallas_call x2 -> x1, Pallas kernels: 2.39 us -> 4.24 us  [payload(): pl.pallas_call(functools.partial(payload_kernel, shallow=SHALLOW, blocks=...]
  transfers between devices with their start and end apart: 3 -> 3, of which waited for: 1 -> 1; matrix products, arithmetic and copies ran while one was open for 2% -> 2% of each run, Pallas kernels for 1% -> 2%
where the time goes in v6:
time: 203 us; the launch traced here: 202 us
  waiting for transfers between devices  102 us (50%)
  blocking collectives  40.3 us (20%)
  starting transfers between devices  20.8 us (10%)
  Pallas kernels  17.7 us (9%)
  between operations  14.9 us (7%)
  other arithmetic  3.38 us (2%)
  local copies, waits for them, and re-layouts  2.6 us (1%)
    all_gather x1, waiting for transfers between devices, per_device(): queries = lax.all_gather(both, 'z', axis=0, tiled=True)  102 us
    all_to_all x1, blocking collectives, per_device(): lax.all_to_all(coded, ('doc', 'y'), split_axis=0, concat_axis=0, tiled=True)  40.3 us
    all_to_all x1, starting transfers between devices, per_device(): rows = lax.all_to_all(sent, 'z', split_axis=0, concat_axis=0, tiled=True)  15.1 us
    pallas_call x1, Pallas kernels, lean_tiles(): pl.pallas_call(functools.partial(lean_kernel, cap=cap, span=span, per_ste...  12.2 us
    ppermute x1, starting transfers between devices, per_device(): mirror = lax.ppermute(theirs, 'y', [(0, 1), (1, 0)])  5.64 us
    pallas_call x1, Pallas kernels, payload(): pl.pallas_call(functools.partial(payload_kernel, shallow=SHALLOW, blocks=...  4.24 us
  transfers between devices with their start and end apart: 3, of which 1 were waited for; matrix products, arithmetic and copies ran while one was open for 2% of the time, Pallas kernels for 2%

profile of v6, /device:TPU:1, one launch (start us, length us, event | category | flops | bytes accessed | tf_op | source)
XLA Modules:
  0.0 202.3 jit_solution(13514335314501292834)
XLA Ops:
  6.5 0.8 constant_dynamic-slice_fusion.1
  7.4 5.6 %collective-permute-start = (bf16[8,3072]{1,0:T(8,128)(2,1)S(1)}, bf16[8,3072]{1,0:T(8,128)(2,1)S(1)}, u32[]{:S(2)}, u32[]{:S(2)}) collective-permute-start(bf16[8,3072]{1,0:T(8,128)(2,1)S(1)} %get-tuple-element.39), channel_id=1, source_target_pairs={{0,16},{16,0},{1,17},{17,1},{2,18},{18,2},{3,19},{19,3},{4,20},{20... | collective-permute-start | bytes 147464 | tf_op jit(solution)/shard_map/ppermute | solution.py:290
  13.0 0.6 copy-done
  13.7 4.2 %payload.1 = bf16[16,200,256]{2,1,0:T(8,128)(2,1)} custom-call(s32[32]{0:T(128)S(1)} %bitcast.53, s32[1]{0:T(128)} %bitcast.16.first_ref, s32[32,128]{1,0:T(8,128)} %bitcast.58, bf16[32,128,256]{2,1,0:T(8,128)(2,1)} %bitcast.55, bf16[32,128,256]{2,1,0:T(8,128)(2,1)} %bitcast.56), custom_call_target="tpu_custom_call" | custom-call | bytes 4194304 | tf_op jit(solution)/shard_map/payload/pallas_call | solution.py:240
  17.9 15.1 %all-to-all-start.1 = ((bf16[16,200,256]{2,1,0:T(8,128)(2,1)}), bf16[16,200,256]{2,1,0:T(8,128)(2,1)}, u32[]{:S(2)}, u32[]{:S(2)}) async-start(bf16[16,200,256]{2,1,0:T(8,128)(2,1)} %payload.1), calls=%async_computation.1 | async-start | bytes 3276800 | tf_op jit(solution)/shard_map/all_to_all | solution.py:285
  33.1 0.7 fusion.17
  33.8 0.1 iota_compare_fusion.5
  34.6 0.1 select_reduce_fusion.1
  34.7 0.1 add_select_fusion.3
  34.8 0.1 eq.21
  34.9 0.1 fusion.10
  35.1 0.1 pad.26.clone
  35.2 0.1 select_reduce_fusion
  35.3 0.2 convolution_convert_fusion
  35.5 0.1 maximum_maximum_fusion
  35.6 0.7 fusion.6
  36.4 102.1 %all-gather.2.cloned.1.call-done = bf16[256,3712]{1,0:T(8,128)(2,1)} async-done(((bf16[16,3712]{1,0:T(8,128)(2,1)}), bf16[256,3712]{1,0:T(8,128)(2,1)}) %all-gather.2.cloned.1.call-update) | async-done | bytes 1900560 | tf_op jit(solution)/shard_map/all_gather | solution.py:313
  138.4 0.8 slice.46
  139.3 0.7 slice_reduce_fusion
  140.6 13.1 %conditional.1 = (s16[32,16,2176]{2,1,0:T(8,128)(2,1)S(1)}) conditional(s32[]{:T(128)} %convert_element_type.17, (s32[]{:T(128)}, bf16[256,3712]{1,0:T(8,128)(2,1)}, bf16[16,200,256]{2,1,0:T(8,128)(2,1)}) %tuple.11, (s32[]{:T(128)}, bf16[1,1,32,128,256]{4,3,2,1,0:T(8,128)(2,1)S(1)}, s32[32,128]{1,0:T(8,128)S(1)}, s32[32,128]{1,0:T(8,128)S(1)}, ...), branch_computations={%region_4.5_spmd, %region_5.6_spmd} | conditional | flops 4303708160 | bytes 24580132 | solution.py:331
  140.7 0.7 pad_add_fusion.place_ref
  141.3 12.2 %lean_tiles.1 = s16[32,16,2176]{2,1,0:T(8,128)(2,1)S(1)} custom-call(s32[3]{0:T(128)} %pad_add_fusion.place_ref, bf16[256,3712]{1,0:T(8,128)(2,1)} %get-tuple-element.28.q_ref.deep_ref.far_ref, bf16[256,3712]{1,0:T(8,128)(2,1)} %get-tuple-element.28.q_ref.deep_ref.far_ref, bf16[256,3712]{1,0:T(8,128)(2,1)} %get-tuple-element.28.q_ref.deep_ref.far_ref, ...), custom_call_target="tpu_custom_call" | custom-call | flops 4294967296 | bytes 3538944 | tf_op jit(solution)/shard_map/cond/branch_0_fun/lean_tiles/pallas_call | solution.py:120
  153.8 40.3 %all_to_all.15.p_ref = s16[32,16,2176]{2,1,0:T(8,128)(2,1)S(1)} all-to-all(s16[32,16,2176]{2,1,0:T(8,128)(2,1)S(1)} %get-tuple-element.49), channel_id=1, replica_groups=mesh['doc'=16,'y'=2,'z'=16] {'doc','y'}, dimensions={0} | all-to-all | bytes 4456448 | tf_op jit(solution)/shard_map/all_to_all | solution.py:332
  194.1 1.3 sum_parts.1
  (18 shorter events, 0.3 us)
Async XLA Ops:
  7.4 28.3 %collective-permute-start = (bf16[8,3072]{1,0:T(8,128)(2,1)S(1)}, bf16[8,3072]{1,0:T(8,128)(2,1)S(1)}, u32[]{:S(2)}, u32[]{:S(2)}) collective-permute-start(bf16[8,3072]{1,0:T(8,128)(2,1)S(1)} %get-tuple-element.39), channel_id=1, source_target_pairs={{0,16},{16,0},{1,17},{17,1},{2,18},{18,2},{3,19},{19,3},{4,20},{20... | collective-permute-start | bytes 147464 | tf_op jit(solution)/shard_map/ppermute | solution.py:290
  13.0 0.7 copy-start
  17.9 15.2 %copy-start.1 = (s32[1,1,32]{2,1,0:T(1,128)S(1)}, s32[1,1,32]{2,1,0:T(1,128)}, u32[]{:S(2)}) copy-start(s32[1,1,32]{2,1,0:T(1,128)} %param.9) | copy-start | bytes 388
  17.9 16.0 %copy-start.2 = (bf16[1,1,32,128,256]{4,3,2,1,0:T(8,128)(2,1)S(1)}, bf16[1,1,32,128,256]{4,3,2,1,0:T(8,128)(2,1)}, u32[]{:S(2)}) copy-start(bf16[1,1,32,128,256]{4,3,2,1,0:T(8,128)(2,1)} %param.7) | copy-start | bytes 6291460
  17.9 17.0 %copy-start.3 = (s32[1,1,32,128]{3,2,1,0:T(8,128)S(1)}, s32[1,1,32,128]{3,2,1,0:T(8,128)}, u32[]{:S(2)}) copy-start(s32[1,1,32,128]{3,2,1,0:T(8,128)} %param.8) | copy-start | bytes 49156
  17.9 122.7 %all-to-all-start.1 = ((bf16[16,200,256]{2,1,0:T(8,128)(2,1)}), bf16[16,200,256]{2,1,0:T(8,128)(2,1)}, u32[]{:S(2)}, u32[]{:S(2)}) async-start(bf16[16,200,256]{2,1,0:T(8,128)(2,1)} %payload.1), calls=%async_computation.1 | async-start | bytes 3276800 | tf_op jit(solution)/shard_map/all_to_all | solution.py:285
  33.0 105.4 %all-gather.2.cloned.1.call-start = ((), (), s32[]{:S(2)}) async-start(), calls=%async_computation.3 | async-start | bytes 2019328 | tf_op jit(solution)/shard_map/all_gather | solution.py:313
Sparse Core Ops, SparseCore 0:
  36.5 101.9 all-gather.1

commit v7 on v6

--- a/solution.py
+++ b/solution.py
@@ -62,7 +62,8 @@
     places = lax.broadcasted_iota(jnp.int32, (window, window), 0)
     for k in range(per_step):
         meta = x_ref[k, base : base + TILE, :].astype(jnp.float32)
-        far = far_ref[k * 16 : k * 16 + TILE, :].astype(jnp.float32)
+        behind = (per_step - 1 - k) * 16
+        far = far_ref[behind : behind + TILE, :].astype(jnp.float32)
         docs, ids = [], []
         for owner in range(HALVES):
             lanes = slice(owner * LANES, (owner + 1) * LANES)
@@ -83,7 +84,8 @@
         right = []
         for k in range(per_step):
             right.append(x_ref[k, owner * cap : (owner + 1) * cap, :])
-            right += [deep_ref[k * 16 : (k + 1) * 16, g * width : (g + 1) * width] for g in range(extra // 16)]
+            behind = (per_step - 1 - k) * 16
+            right += [deep_ref[behind : behind + 16, g * width : (g + 1) * width] for g in range(extra // 16)]
         right = jnp.concatenate(right, axis=0)
         right_ref[...] = right
         acc[owner] += jnp.dot(left[owner * tall : (owner + 1) * tall, :], right_ref[...], preferred_element_type=jnp.float32)
@@ -93,21 +95,21 @@
         code_tiles(place_ref, acc, o_ref, nq=nq, blocks=blocks)
 
 
-def lean_tiles(place, queries, rows, *, cap, span, blocks, extra, per_step=8):
+def lean_tiles(place, queries, beside, rows, *, cap, span, blocks, extra, per_step=8):
     nq = queries.shape[0]
     sources, depth, width = rows.shape
     lanes = blocks * width + LANES
     targets = 16 * HALVES
     deep_lanes = extra // 16 * width
-    deep_at = sources * span // deep_lanes
-    far_at = (deep_at + 1) * deep_lanes // LANES
+    steps = sources // per_step
+    far_at = deep_lanes // LANES
     grid_spec = pltpu.PrefetchScalarGridSpec(
         num_scalar_prefetch=1,
         grid=(sources // per_step,),
         in_specs=[
             pl.BlockSpec((nq, per_step * span), lambda i, _: (0, i)),
-            pl.BlockSpec((per_step * 16, deep_lanes), lambda i, _: (i, deep_at)),
-            pl.BlockSpec((per_step * 16, LANES), lambda i, _: (i, far_at)),
+            pl.BlockSpec((per_step * 16, deep_lanes), lambda i, _: (steps - 1 - i, 0)),
+            pl.BlockSpec((per_step * 16, LANES), lambda i, _: (steps - 1 - i, far_at)),
             pl.BlockSpec((per_step, depth, width), lambda i, _: (i, 0, 0)),
         ],
         out_specs=pl.BlockSpec((targets, nq // 16, lanes), lambda i, _: (0, 0, 0)),
@@ -128,7 +130,7 @@
             transcendentals=0,
         ),
         name="lean_tiles",
-    )(place, queries, queries, queries, rows)
+    )(place, queries, beside, beside, rows)
 
 
 def gram_kernel(flip_ref, q_ref, x_ref, o_ref, left, acc, *, cap, span, per_step, blocks):
@@ -206,6 +208,10 @@
     here, z_size = low_ref.shape[0], low_ref.shape[0] * pl.num_programs(0)
     lane = lax.broadcasted_iota(jnp.int32, (1, slots_ref.shape[1]), 1)
     base = HALVES * shallow
+    beyond = jnp.int32(0)
+    for owner in range(slots_ref.shape[0]):
+        beyond += jnp.maximum(counts_ref[owner] - shallow, 0)
+    crowded = jnp.where(beyond > EXTRA, 1.0, 0.0)
     for r in range(here):
         z = step * here + r
         docs, ids = [], []
@@ -215,7 +221,7 @@
             doc = lax.shift_right_logical(slots, blocks.bit_length() - 1) - first_ref[0]
             docs.append(doc.astype(jnp.float32))
             ids.append(jnp.where(lane < counts_ref[owner], slots & (blocks - 1), DEAD).astype(jnp.float32))
-        rest = jnp.zeros((TILE - 2, o_ref.shape[2]), jnp.float32)
+        rest = jnp.full((TILE - 2, o_ref.shape[2]), crowded)
         meta = jnp.concatenate([jnp.concatenate(docs, axis=1), jnp.concatenate(ids, axis=1), rest], axis=0)
         o_ref[r, :shallow, :] = low_ref[r, :shallow, :]
         o_ref[r, shallow:base, :] = high_ref[r, :shallow, :]
@@ -288,47 +294,44 @@
     mine = lax.dynamic_slice_in_dim(query_rows, y * half_docs, half_docs, 1)
     theirs = lax.dynamic_slice_in_dim(query_rows, (1 - y) * half_docs, half_docs, 1)
     mirror = lax.ppermute(theirs, "y", [(0, 1), (1, 0)])
+    queries = lax.all_gather(jnp.concatenate([mine, mirror], axis=0), "z", axis=0, tiled=True)
 
     live = jnp.arange(cap, dtype=jnp.int32)[None, :] < counts[:, None]
     doc = slots // blocks - me * span
     beyond = jnp.maximum(counts - SHALLOW, 0)
     order = jnp.arange(owners, dtype=jnp.int32)
     before = jnp.sum(jnp.where(order[None, :] < order[:, None], beyond[None, :], 0), axis=1)
-    too_many = jnp.sum(beyond) > EXTRA
     depth = cap - SHALLOW
-    place = jnp.where(live[:, SHALLOW:], before[:, None] + jnp.arange(depth, dtype=jnp.int32)[None, :], EXTRA)
-    place = place.reshape(1, owners * depth)
-    taken = place == jnp.arange(EXTRA, dtype=jnp.int32)[:, None]
+    spot = jnp.where(live[:, SHALLOW:], before[:, None] + jnp.arange(depth, dtype=jnp.int32)[None, :], EXTRA)
+    spot = spot.reshape(1, owners * depth)
+    taken = spot == jnp.arange(EXTRA, dtype=jnp.int32)[:, None]
     deep = row_values[0, 0, :, SHALLOW:, :].reshape(owners * depth, width)
     deep = jnp.dot(taken.astype(jnp.bfloat16), deep, preferred_element_type=jnp.float32).astype(jnp.bfloat16)
     packed = 1 + doc * blocks + slots % blocks + order[:, None] * (span * blocks)
     packed = jnp.sum(jnp.where(taken, packed[:, SHALLOW:].reshape(1, owners * depth), 0), axis=1)
     code = jnp.maximum(packed - 1, 0)
     target = jnp.where(packed > 0, code // (span * blocks), DEAD)
-    flag = jnp.broadcast_to(too_many.astype(jnp.int32), (EXTRA,))
-    far = jnp.stack([code % (span * blocks) // blocks, code % blocks, target, flag]).astype(jnp.bfloat16)
-    far = jnp.pad(far, ((0, 16 - 4), (SHALLOW, LANES - SHALLOW - EXTRA)))
+    far = jnp.stack([code % (span * blocks) // blocks, code % blocks, target]).astype(jnp.bfloat16)
+    far = jnp.pad(far, ((0, 16 - 3), (SHALLOW, LANES - SHALLOW - EXTRA)))
     beside = jnp.concatenate([deep[g : g + 16] for g in range(0, EXTRA, 16)] + [far], axis=1)
-    both = jnp.concatenate([jnp.concatenate([mine, mirror], axis=0), beside], axis=1)
-    queries = lax.all_gather(both, "z", axis=0, tiled=True)
-    flip = y.astype(jnp.int32).reshape(1)
-
-    def lean(queries, rows, row_values):
-        place = jnp.stack([y, lax.axis_index("z"), z_size]).astype(jnp.int32)
-        return lean_tiles(place, queries, rows, cap=SHALLOW, span=span, blocks=blocks, extra=EXTRA)
-
-    def full(queries, rows, row_values):
+    downward = [list(range(z_size - 1, -1, -1))]
+    beside = lax.all_gather(beside, "z", axis=0, tiled=True, axis_index_groups=downward)
+    home = jnp.stack([y, lax.axis_index("z"), jnp.int32(z_size)]).astype(jnp.int32)
+
+    def lean(place, queries, beside, rows, row_values):
+        return lean_tiles(place, queries, beside, rows, cap=SHALLOW, span=span, blocks=blocks, extra=EXTRA)
+
+    def full(place, queries, beside, rows, row_values):
         block = jnp.where(live, slots % blocks, DEAD)
         meta = jnp.concatenate([doc, block], axis=1).reshape(HALVES, z_size, 2 * cap).transpose(1, 0, 2)
         meta = jnp.pad(meta, ((0, 0), (0, TILE - HALVES), (0, 0))).astype(jnp.bfloat16)
         values = row_values[0, 0]
         sent = jnp.concatenate([values[:z_size], values[z_size:], meta], axis=1)
         rows = lax.all_to_all(sent, "z", split_axis=0, concat_axis=0, tiled=True)
-        return partial_tiles(flip, queries, rows, cap=cap, span=span, blocks=blocks)
-
-    flags = queries[:, -LANES:].reshape(z_size, 16, LANES)[:, 3, SHALLOW]
-    crowded = jnp.max(flags.astype(jnp.float32)) > 0.5
-    coded = lax.cond(crowded, full, lean, queries, rows, row_values)
+        return partial_tiles(place, queries, rows, cap=cap, span=span, blocks=blocks)
+
+    flags = rows[:, HALVES * SHALLOW + TILE - 1, 0].astype(jnp.float32)
+    coded = lax.cond(jnp.max(flags) > 0.5, full, lean, home, queries, beside, rows, row_values)
     parts = lax.all_to_all(coded, ("doc", "y"), split_axis=0, concat_axis=0, tiled=True)
     return summed(parts, blocks=blocks, width=width)
 

time: 203 us -> 198 us (0.975)
  waiting for transfers between devices: 102 us -> 2.55 us
  blocking collectives: 40.3 us -> 138 us
    all_gather x1, waiting for transfers between devices: 102 us -> 1.02 us  [per_device(): lax.all_gather(jnp.concatenate([mine, mirror], axis=0), 'z', axis=0, tile...]
    all_gather x0 -> x1, blocking collectives: none -> 94.9 us  [per_device(): lax.all_gather(beside, 'z', axis=0, tiled=True, axis_index_groups=downward)]
    all_to_all x1, blocking collectives: 40.3 us -> 43 us  [per_device(): lax.all_to_all(coded, ('doc', 'y'), split_axis=0, concat_axis=0, tiled=True)]
  transfers between devices with their start and end apart: 3 -> 3, of which waited for: 1 -> 2; matrix products, arithmetic and copies ran while one was open for 2% -> 1% of each run, Pallas kernels for 2% -> 0%
where the time goes in v7:
time: 198 us; the launch traced here: 197 us
  blocking collectives  138 us (70%)
  starting transfers between devices  20.8 us (11%)
  Pallas kernels  17.6 us (9%)
  between operations  14.2 us (7%)
  other arithmetic  2.73 us (1%)
  waiting for transfers between devices  2.55 us (1%)
    all_gather x1, blocking collectives, per_device(): lax.all_gather(beside, 'z', axis=0, tiled=True, axis_index_groups=downward)  94.9 us
    all_to_all x1, blocking collectives, per_device(): lax.all_to_all(coded, ('doc', 'y'), split_axis=0, concat_axis=0, tiled=True)  43 us
    all_to_all x1, starting transfers between devices, per_device(): rows = lax.all_to_all(sent, 'z', split_axis=0, concat_axis=0, tiled=True)  15.9 us
    pallas_call x1, Pallas kernels, lean_tiles(): pl.pallas_call(functools.partial(lean_kernel, cap=cap, span=span, per_ste...  12 us
    ppermute x1, starting transfers between devices, per_device(): mirror = lax.ppermute(theirs, 'y', [(0, 1), (1, 0)])  4.82 us
    pallas_call x1, Pallas kernels, payload(): pl.pallas_call(functools.partial(payload_kernel, shallow=SHALLOW, blocks=...  4.28 us
  transfers between devices with their start and end apart: 3, of which 2 were waited for; matrix products, arithmetic and copies ran while one was open for 1% of the time, Pallas kernels for 0%

profile of v7, /device:TPU:1, one launch (start us, length us, event | category | flops | bytes accessed | tf_op | source)
XLA Modules:
  0.0 197.1 jit_solution(2078977743167868075)
XLA Ops:
  6.5 0.7 copy-done
  7.2 4.3 %payload.1 = bf16[16,200,256]{2,1,0:T(8,128)(2,1)} custom-call(s32[32]{0:T(128)S(1)} %bitcast.48, s32[1]{0:T(128)} %bitcast.5.first_ref, s32[32,128]{1,0:T(8,128)} %bitcast.53, bf16[32,128,256]{2,1,0:T(8,128)(2,1)} %bitcast.50, bf16[32,128,256]{2,1,0:T(8,128)(2,1)} %bitcast.51), custom_call_target="tpu_custom_call" | custom-call | bytes 4194304 | tf_op jit(solution)/shard_map/payload/pallas_call | solution.py:246
  11.5 15.9 %all-to-all-start.1 = ((bf16[16,200,256]{2,1,0:T(8,128)(2,1)}), bf16[16,200,256]{2,1,0:T(8,128)(2,1)}, u32[]{:S(2)}, u32[]{:S(2)}) async-start(bf16[16,200,256]{2,1,0:T(8,128)(2,1)} %payload.1), calls=%async_computation.1 | async-start | bytes 3276800 | tf_op jit(solution)/shard_map/all_to_all | solution.py:291
  27.4 0.0 all-gather.2.cloned.1.call-start
  27.5 4.8 %collective-permute-start = (bf16[8,3072]{1,0:T(8,128)(2,1)S(1)}, bf16[8,3072]{1,0:T(8,128)(2,1)S(1)}, u32[]{:S(2)}, u32[]{:S(2)}) collective-permute-start(bf16[8,3072]{1,0:T(8,128)(2,1)S(1)} %get-tuple-element.41), channel_id=1, source_target_pairs={{0,16},{16,0},{1,17},{17,1},{2,18},{18,2},{3,19},{19,3},{4,20},{20... | collective-permute-start | bytes 147464 | tf_op jit(solution)/shard_map/ppermute | solution.py:296
  32.3 1.5 collective-permute-done
  33.9 0.6 pad_maximum_fusion.1
  34.6 0.1 select_reduce_fusion.1
  34.7 0.1 iota_compare_fusion.4
  34.8 0.1 add_select_fusion.3
  34.9 0.1 eq.21
  35.0 0.1 fusion.8
  35.1 0.1 broadcast_in_dim.49
  35.2 0.1 pad_add_fusion
  35.2 0.1 select_reduce_fusion
  35.4 0.1 fusion.19
  35.5 0.2 convolution_convert_fusion
  35.7 94.9 %all_gather.7 = bf16[256,640]{1,0:T(8,128)(2,1)S(1)} all-gather(bf16[16,640]{1,0:T(8,128)(2,1)S(1)} %pad_maximum_fusion.2), channel_id=1, replica_groups={{15,14,13,12,11,10,9,8,7,6,5,4,3,2,1,0},{31,30,29,28,27,26,25,24,23,22,..., dimensions={0}, use_global_device_ids=true | all-gather | bytes 348160 | tf_op jit(solution)/shard_map/all_gather | solution.py:318
  130.6 1.0 all-gather.2.cloned.1.call-done
  131.6 1.4 slice_reduce_fusion
  133.7 12.3 %conditional.1 = (s16[32,16,2176]{2,1,0:T(8,128)(2,1)S(1)}) conditional(s32[]{:T(128)} %convert_element_type.6, (s32[3]{0:T(128)S(1)}, bf16[256,3072]{1,0:T(8,128)(2,1)}, bf16[256,640]{1,0:T(8,128)(2,1)S(1)}, bf16[16,200,256]{2,1,0:T(8,128)(2,1)}) %tuple.11, (bf16[1,1,32,128,256]{4,3,2,1,0:T(8,128)(2,1)S(1)}, s32[32,128]{1,0:T(8,128)S(1)}, ...), branch_computations={%region_3.4_spmd, %region_4.5_spmd} | conditional | flops 4303708160 | bytes 22941732 | solution.py:334
  133.7 12.0 %lean_tiles.1 = s16[32,16,2176]{2,1,0:T(8,128)(2,1)S(1)} custom-call(s32[3]{0:T(128)S(1)} %get-tuple-element.28.place_ref, bf16[256,3072]{1,0:T(8,128)(2,1)} %get-tuple-element.29.q_ref, bf16[256,640]{1,0:T(8,128)(2,1)S(1)} %get-tuple-element.30.deep_ref.far_ref, bf16[256,640]{1,0:T(8,128)(2,1)S(1)} %get-tuple-element.30.deep_ref.far_ref, ...), custom_call_target="tpu_custom_call" | custom-call | flops 4294967296 | bytes 3211264 | tf_op jit(solution)/shard_map/cond/branch_0_fun/lean_tiles/pallas_call | solution.py:122
  145.9 43.0 %all_to_all.15.p_ref = s16[32,16,2176]{2,1,0:T(8,128)(2,1)S(1)} all-to-all(s16[32,16,2176]{2,1,0:T(8,128)(2,1)S(1)} %get-tuple-element.49), channel_id=1, replica_groups=mesh['doc'=16,'y'=2,'z'=16] {'doc','y'}, dimensions={0} | all-to-all | bytes 4456448 | tf_op jit(solution)/shard_map/all_to_all | solution.py:335
  189.0 1.3 sum_parts.1
  (20 shorter events, 0.2 us)
Async XLA Ops:
  6.5 0.7 copy-start
  11.5 16.0 %copy-start.4 = (bf16[8,6144]{1,0:T(8,128)(2,1)S(1)}, bf16[8,6144]{1,0:T(8,128)(2,1)}, u32[]{:S(2)}) copy-start(bf16[8,6144]{1,0:T(8,128)(2,1)} %param.6) | copy-start | bytes 294916
  11.5 23.1 %copy-start.2 = (bf16[1,1,32,128,256]{4,3,2,1,0:T(8,128)(2,1)S(1)}, bf16[1,1,32,128,256]{4,3,2,1,0:T(8,128)(2,1)}, u32[]{:S(2)}) copy-start(bf16[1,1,32,128,256]{4,3,2,1,0:T(8,128)(2,1)} %param.7) | copy-start | bytes 6291460
  11.5 23.1 %copy-start.1 = (s32[1,1,32]{2,1,0:T(1,128)S(1)}, s32[1,1,32]{2,1,0:T(1,128)}, u32[]{:S(2)}) copy-start(s32[1,1,32]{2,1,0:T(1,128)} %param.9) | copy-start | bytes 388
  11.5 23.5 %copy-start.3 = (s32[1,1,32,128]{3,2,1,0:T(8,128)S(1)}, s32[1,1,32,128]{3,2,1,0:T(8,128)}, u32[]{:S(2)}) copy-start(s32[1,1,32,128]{3,2,1,0:T(8,128)} %param.8) | copy-start | bytes 49156
  11.5 120.1 %all-to-all-start.1 = ((bf16[16,200,256]{2,1,0:T(8,128)(2,1)}), bf16[16,200,256]{2,1,0:T(8,128)(2,1)}, u32[]{:S(2)}, u32[]{:S(2)}) async-start(bf16[16,200,256]{2,1,0:T(8,128)(2,1)} %payload.1), calls=%async_computation.1 | async-start | bytes 3276800 | tf_op jit(solution)/shard_map/all_to_all | solution.py:291
  27.4 104.2 %all-gather.2.cloned.1.call-start = ((), (), s32[]{:S(2)}) async-start(), calls=%async_computation.3 | async-start | bytes 1671168 | tf_op jit(solution)/shard_map/all_gather | solution.py:297
  27.5 6.3 %collective-permute-start = (bf16[8,3072]{1,0:T(8,128)(2,1)S(1)}, bf16[8,3072]{1,0:T(8,128)(2,1)S(1)}, u32[]{:S(2)}, u32[]{:S(2)}) collective-permute-start(bf16[8,3072]{1,0:T(8,128)(2,1)S(1)} %get-tuple-element.41), channel_id=1, source_target_pairs={{0,16},{16,0},{1,17},{17,1},{2,18},{18,2},{3,19},{19,3},{4,20},{20... | collective-permute-start | bytes 147464 | tf_op jit(solution)/shard_map/ppermute | solution.py:296
Sparse Core Ops, SparseCore 0:
  34.6 96.9 all-gather.1

commit v8 on v7

--- a/solution.py
+++ b/solution.py
@@ -8,6 +8,7 @@
 from jax.sharding import Mesh
 from jax.sharding import PartitionSpec as P
 
+CORES = 2
 HALVES = 2
 CODE_STEP = 64.0
 TOP = 32700.0
@@ -19,34 +20,73 @@
 DEAD = 64
 
 
-def code_tiles(flip_ref, acc, o_ref, *, nq, blocks):
+def coded_rows(tiles, blocks):
+    lane = lax.broadcasted_iota(jnp.int32, (16, LANES), 1)
+    peaks = jnp.full((16, LANES), TINY, jnp.float32)
+    for b in range(blocks):
+        peak = jnp.max(jnp.abs(tiles(b)), axis=1, keepdims=True)
+        peaks = jnp.where(lane == b, jnp.maximum(peak, TINY), peaks)
+    code = jnp.ceil((jnp.log2(peaks) - jnp.log2(TOP)) * CODE_STEP)
+    inverse = jnp.exp2(code * (-1.0 / CODE_STEP))
+    out = [jnp.floor(tiles(b) * inverse[:, b : b + 1] + 0.5).astype(jnp.int32).astype(jnp.int16) for b in range(blocks)]
+    return out, code.astype(jnp.int32).astype(jnp.int16)
+
+
+def code_tiles(place_ref, acc, keep_ref, give_ref, *, nq, blocks):
     width = acc.shape[2]
-    flip = flip_ref[0]
+    flip, core = place_ref[0], place_ref[3]
     half = nq // (2 * 16)
-    lane = lax.broadcasted_iota(jnp.int32, (16, LANES), 1)
 
     def tile_of(owner, b, m, slot):
-        base = b * nq + m * 32 + slot * 8
-        return jnp.concatenate([acc[owner, base : base + 8, :], acc[owner, base + 16 : base + 24, :]], axis=0)
+        base = pl.multiple_of(b * nq + m * 32 + slot * 8, 8)
+        return jnp.concatenate([acc[owner, pl.ds(base, 8), :], acc[owner, pl.ds(base + 16, 8), :]], axis=0)
 
     for owner in range(HALVES):
-        for m in range(half):
+        for pair in range(half // CORES):
             for slot in range(2):
-                target = ((slot + flip - 2 * slot * flip) * half + m) * HALVES + owner
-                peaks = jnp.full((16, LANES), TINY, jnp.float32)
+                target = ((slot + flip - 2 * slot * flip) * (half // CORES) + pair) * HALVES + owner
                 for b in range(blocks):
-                    peak = jnp.max(jnp.abs(tile_of(owner, b, m, slot)), axis=1, keepdims=True)
-                    peaks = jnp.where(lane == b, jnp.maximum(peak, TINY), peaks)
-                code = jnp.ceil((jnp.log2(peaks) - jnp.log2(TOP)) * CODE_STEP)
-                inverse = jnp.exp2(code * (-1.0 / CODE_STEP))
+                    keep_ref[target, :, b * width : (b + 1) * width] = tile_of(owner, b, pair * CORES + core, slot)
+                other = lambda b: tile_of(owner, b, pair * CORES + 1 - core, slot)
+                out, code = coded_rows(other, blocks)
                 for b in range(blocks):
-                    coded = tile_of(owner, b, m, slot) * inverse[:, b : b + 1]
-                    coded = jnp.floor(coded + 0.5).astype(jnp.int32).astype(jnp.int16)
-                    o_ref[target, :, b * width : (b + 1) * width] = coded
-                o_ref[target, :, blocks * width :] = code.astype(jnp.int32).astype(jnp.int16)
-
-
-def lean_kernel(place_ref, q_ref, deep_ref, far_ref, x_ref, o_ref, left, acc, right_ref, *, cap, span, per_step, blocks, extra):
+                    give_ref[target, :, b * width : (b + 1) * width] = out[b]
+                give_ref[target, :, blocks * width :] = code
+
+
+def merge_kernel(keep_ref, got_ref, o_ref, *, blocks):
+    width = keep_ref.shape[2] // blocks
+    for t in range(keep_ref.shape[0]):
+        scale = jnp.exp2(got_ref[t, :, blocks * width :].astype(jnp.float32) * (1.0 / CODE_STEP))
+
+        def total(b):
+            lanes = slice(b * width, (b + 1) * width)
+            return keep_ref[t, :, lanes] + got_ref[t, :, lanes].astype(jnp.float32) * scale[:, b : b + 1]
+
+        sums = [total(b) for b in range(blocks)]
+        out, code = coded_rows(lambda b: sums[b], blocks)
+        for b in range(blocks):
+            o_ref[t, :, b * width : (b + 1) * width] = out[b]
+        o_ref[t, :, blocks * width :] = code
+
+
+def merged(keep, got, *, blocks, per_step=4):
+    targets, rows, lanes = got.shape
+    return pl.pallas_call(
+        functools.partial(merge_kernel, blocks=blocks),
+        grid=(targets // per_step,),
+        in_specs=[
+            pl.BlockSpec((per_step, rows, keep.shape[2]), lambda i: (i, 0, 0)),
+            pl.BlockSpec((per_step, rows, lanes), lambda i: (i, 0, 0)),
+        ],
+        out_specs=pl.BlockSpec((per_step, rows, lanes), lambda i: (i, 0, 0)),
+        out_shape=jax.ShapeDtypeStruct(got.shape, jnp.int16),
+        compiler_params=pltpu.CompilerParams(vmem_limit_bytes=16 << 20),
+        name="merge",
+    )(keep, got)
+
+
+def lean_kernel(place_ref, q_ref, deep_ref, far_ref, x_ref, keep_ref, give_ref, left, acc, right_ref, *, cap, span, per_step, blocks, extra):
     step = pl.program_id(0)
     width = x_ref.shape[2]
     nq = q_ref.shape[0]
@@ -60,6 +100,7 @@
         acc[...] = jnp.zeros_like(acc)
 
     places = lax.broadcasted_iota(jnp.int32, (window, window), 0)
+    got, codes_of = [], []
     for k in range(per_step):
         meta = x_ref[k, base : base + TILE, :].astype(jnp.float32)
         behind = (per_step - 1 - k) * 16
@@ -75,12 +116,14 @@
         chosen = jnp.where(places == doc, 1.0, 0.0).astype(jnp.bfloat16)
         queries = q_ref[:, start : start + window]
         picked = jnp.dot(queries, chosen, preferred_element_type=jnp.float32).astype(jnp.bfloat16)
-        for owner in range(HALVES):
-            lanes = slice(owner * LANES, (owner + 1) * LANES)
+        got.append(picked)
+        codes_of.append(ids)
+    for owner in range(HALVES):
+        lanes = slice(owner * LANES, (owner + 1) * LANES)
+        for k in range(per_step):
             for b in range(blocks):
-                kept = picked[:, lanes] * jnp.where(ids[owner] == float(b), 1.0, 0.0).astype(jnp.bfloat16)
+                kept = got[k][:, lanes] * jnp.where(codes_of[k][owner] == float(b), 1.0, 0.0).astype(jnp.bfloat16)
                 left[owner * tall + b * nq : owner * tall + (b + 1) * nq, k * LANES : (k + 1) * LANES] = kept
-    for owner in range(HALVES):
         right = []
         for k in range(per_step):
             right.append(x_ref[k, owner * cap : (owner + 1) * cap, :])
@@ -92,14 +135,14 @@
 
     @pl.when(step == pl.num_programs(0) - 1)
     def _():
-        code_tiles(place_ref, acc, o_ref, nq=nq, blocks=blocks)
-
-
-def lean_tiles(place, queries, beside, rows, *, cap, span, blocks, extra, per_step=8):
+        code_tiles(place_ref, acc, keep_ref, give_ref, nq=nq, blocks=blocks)
+
+
+def lean_tiles(place, queries, beside, rows, *, cap, span, blocks, extra, per_step=4):
     nq = queries.shape[0]
     sources, depth, width = rows.shape
     lanes = blocks * width + LANES
-    targets = 16 * HALVES
+    targets = 16 // CORES * HALVES
     deep_lanes = extra // 16 * width
     steps = sources // per_step
     far_at = deep_lanes // LANES
@@ -112,7 +155,10 @@
             pl.BlockSpec((per_step * 16, LANES), lambda i, _: (steps - 1 - i, far_at)),
             pl.BlockSpec((per_step, depth, width), lambda i, _: (i, 0, 0)),
         ],
-        out_specs=pl.BlockSpec((targets, nq // 16, lanes), lambda i, _: (0, 0, 0)),
+        out_specs=[
+            pl.BlockSpec((targets, nq // 16, blocks * width), lambda i, _: (0, 0, 0)),
+            pl.BlockSpec((targets, nq // 16, lanes), lambda i, _: (0, 0, 0)),
+        ],
         scratch_shapes=[
             pltpu.VMEM((HALVES * blocks * nq, per_step * (cap + extra)), jnp.bfloat16),
             pltpu.VMEM((HALVES, blocks * nq, width), jnp.float32),
@@ -122,7 +168,10 @@
     return pl.pallas_call(
         functools.partial(lean_kernel, cap=cap, span=span, per_step=per_step, blocks=blocks, extra=extra),
         grid_spec=grid_spec,
-        out_shape=jax.ShapeDtypeStruct((targets, nq // 16, lanes), jnp.int16),
+        out_shape=[
+            jax.ShapeDtypeStruct((targets, nq // 16, blocks * width), jnp.float32),
+            jax.ShapeDtypeStruct((targets, nq // 16, lanes), jnp.int16),
+        ],
         compiler_params=pltpu.CompilerParams(vmem_limit_bytes=56 << 20),
         cost_estimate=pl.CostEstimate(
             flops=2 * nq * sources * HALVES * (cap + extra) * width * blocks,
@@ -133,7 +182,7 @@
     )(place, queries, beside, beside, rows)
 
 
-def gram_kernel(flip_ref, q_ref, x_ref, o_ref, left, acc, *, cap, span, per_step, blocks):
+def gram_kernel(place_ref, q_ref, x_ref, keep_ref, give_ref, left, acc, *, cap, span, per_step, blocks):
     step = pl.program_id(0)
     width = x_ref.shape[2]
     nq = q_ref.shape[0]
@@ -168,14 +217,14 @@
 
     @pl.when(step == pl.num_programs(0) - 1)
     def _():
-        code_tiles(flip_ref, acc, o_ref, nq=nq, blocks=blocks)
+        code_tiles(place_ref, acc, keep_ref, give_ref, nq=nq, blocks=blocks)
 
 
 def partial_tiles(flip, queries, rows, *, cap, span, blocks, per_step=4):
     nq, docs = queries.shape
     sources, depth, width = rows.shape
     lanes = blocks * width + LANES
-    targets = 16 * HALVES
+    targets = 16 // CORES * HALVES
     grid_spec = pltpu.PrefetchScalarGridSpec(
         num_scalar_prefetch=1,
         grid=(sources // per_step,),
@@ -183,7 +232,10 @@
             pl.BlockSpec((nq, per_step * span), lambda i, _: (0, i)),
             pl.BlockSpec((per_step, depth, width), lambda i, _: (i, 0, 0)),
         ],
-        out_specs=pl.BlockSpec((targets, nq // 16, lanes), lambda i, _: (0, 0, 0)),
+        out_specs=[
+            pl.BlockSpec((targets, nq // 16, blocks * width), lambda i, _: (0, 0, 0)),
+            pl.BlockSpec((targets, nq // 16, lanes), lambda i, _: (0, 0, 0)),
+        ],
         scratch_shapes=[
             pltpu.VMEM((HALVES, blocks * nq, per_step * cap), jnp.bfloat16),
             pltpu.VMEM((HALVES, blocks * nq, width), jnp.float32),
@@ -192,7 +244,10 @@
     return pl.pallas_call(
         functools.partial(gram_kernel, cap=cap, span=span, per_step=per_step, blocks=blocks),
         grid_spec=grid_spec,
-        out_shape=jax.ShapeDtypeStruct((targets, nq // 16, lanes), jnp.int16),
+        out_shape=[
+            jax.ShapeDtypeStruct((targets, nq // 16, blocks * width), jnp.float32),
+            jax.ShapeDtypeStruct((targets, nq // 16, lanes), jnp.int16),
+        ],
         compiler_params=pltpu.CompilerParams(vmem_limit_bytes=48 << 20),
         cost_estimate=pl.CostEstimate(
             flops=2 * nq * sources * HALVES * cap * width * blocks,
@@ -316,7 +371,7 @@
     beside = jnp.concatenate([deep[g : g + 16] for g in range(0, EXTRA, 16)] + [far], axis=1)
     downward = [list(range(z_size - 1, -1, -1))]
     beside = lax.all_gather(beside, "z", axis=0, tiled=True, axis_index_groups=downward)
-    home = jnp.stack([y, lax.axis_index("z"), jnp.int32(z_size)]).astype(jnp.int32)
+    home = jnp.stack([y, lax.axis_index("z"), jnp.int32(z_size), lax.axis_index("core")]).astype(jnp.int32)
 
     def lean(place, queries, beside, rows, row_values):
         return lean_tiles(place, queries, beside, rows, cap=SHALLOW, span=span, blocks=blocks, extra=EXTRA)
@@ -331,21 +386,24 @@
         return partial_tiles(place, queries, rows, cap=cap, span=span, blocks=blocks)
 
     flags = rows[:, HALVES * SHALLOW + TILE - 1, 0].astype(jnp.float32)
-    coded = lax.cond(jnp.max(flags) > 0.5, full, lean, home, queries, beside, rows, row_values)
-    parts = lax.all_to_all(coded, ("doc", "y"), split_axis=0, concat_axis=0, tiled=True)
+    keep, give = lax.cond(jnp.max(flags) > 0.5, full, lean, home, queries, beside, rows, row_values)
+    got = lax.ppermute(give, "core", [(0, 1), (1, 0)])
+    coded = merged(keep, got, blocks=blocks)
+    parts = lax.all_to_all(coded, ("chip", "y"), split_axis=0, concat_axis=0, tiled=True)
     return summed(parts, blocks=blocks, width=width)
 
 
 def solution(mesh):
     docs, owners = mesh.devices.shape
-    split = Mesh(mesh.devices.reshape(docs, HALVES, owners // HALVES), ("doc", "y", "z"))
-    blk = ("y", "z")
+    shape = (docs // CORES, CORES, HALVES, owners // HALVES)
+    split = Mesh(mesh.devices.reshape(shape), ("chip", "core", "y", "z"))
+    doc, blk = ("chip", "core"), ("y", "z")
     in_specs = (
-        P(blk, "doc"),
-        P("doc", blk, None, None, None),
-        P("doc", blk, None, None),
-        P("doc", blk, None),
+        P(blk, doc),
+        P(doc, blk, None, None, None),
+        P(doc, blk, None, None),
+        P(doc, blk, None),
     )
     return jax.shard_map(
-        per_device, mesh=split, in_specs=in_specs, out_specs=P("doc", blk), check_vma=False
+        per_device, mesh=split, in_specs=in_specs, out_specs=P(doc, blk), check_vma=False
     )

time: 198 us -> 191 us (0.965)
  blocking collectives: 138 us -> 118 us
  starting transfers between devices: 20.8 us -> 28.5 us
  waiting for transfers between devices: 2.55 us -> 5.68 us
  Pallas kernels: 17.6 us -> 20.3 us
    all_to_all x1, blocking collectives: 43 us -> 24.2 us  [per_device(): lax.all_to_all(coded, ('chip', 'y'), split_axis=0, concat_axis=0, tiled=T...]
    ppermute x0 -> x1, starting transfers between devices: none -> 7.71 us  [per_device(): got = lax.ppermute(give, 'core', [(0, 1), (1, 0)])]
    pallas_call x0 -> x1, Pallas kernels: none -> 2.58 us  [merged(): pl.pallas_call(functools.partial(merge_kernel, blocks=blocks), grid=(targ...]
    ppermute x0 -> x1, waiting for transfers between devices: none -> 2.57 us  [per_device(): got = lax.ppermute(give, 'core', [(0, 1), (1, 0)])]
  transfers between devices with their start and end apart: 3 -> 4, of which waited for: 2 -> 3; matrix products, arithmetic and copies ran while one was open for 1% -> 1% of each run, Pallas kernels for 0% -> 0%
where the time goes in v8:
time: 191 us
  blocking collectives  118 us (62%)
  starting transfers between devices  28.5 us (15%)
  Pallas kernels  20.3 us (11%)
  between operations  14.2 us (7%)
  waiting for transfers between devices  5.68 us (3%)
  other arithmetic  2.73 us (1%)
    all_gather x1, blocking collectives, per_device(): lax.all_gather(beside, 'z', axis=0, tiled=True, axis_index_groups=downward)  94.3 us
    all_to_all x1, blocking collectives, per_device(): lax.all_to_all(coded, ('chip', 'y'), split_axis=0, concat_axis=0, tiled=T...  24.2 us
    all_to_all x1, starting transfers between devices, per_device(): rows = lax.all_to_all(sent, 'z', split_axis=0, concat_axis=0, tiled=True)  15.9 us
    pallas_call x1, Pallas kernels, lean_tiles(): pl.pallas_call(functools.partial(lean_kernel, cap=cap, span=span, per_ste...  12.5 us
    ppermute x1, starting transfers between devices, per_device(): got = lax.ppermute(give, 'core', [(0, 1), (1, 0)])  7.71 us
    ppermute x1, starting transfers between devices, per_device(): mirror = lax.ppermute(theirs, 'y', [(0, 1), (1, 0)])  4.82 us
    pallas_call x1, Pallas kernels, payload(): pl.pallas_call(functools.partial(payload_kernel, shallow=SHALLOW, blocks=...  4.29 us
  transfers between devices with their start and end apart: 4, of which 3 were waited for; matrix products, arithmetic and copies ran while one was open for 1% of the time, Pallas kernels for 0%

profile of v8, /device:TPU:1, one launch (start us, length us, event | category | flops | bytes accessed | tf_op | source)
XLA Modules:
  0.0 191.0 jit_solution(16784688060894780721)
XLA Ops:
  6.5 0.7 copy-done
  7.2 4.3 %payload.1 = bf16[16,200,256]{2,1,0:T(8,128)(2,1)} custom-call(s32[32]{0:T(128)S(1)} %bitcast.49, s32[1]{0:T(128)} %bitcast.5.first_ref, s32[32,128]{1,0:T(8,128)} %bitcast.54, bf16[32,128,256]{2,1,0:T(8,128)(2,1)} %bitcast.51, bf16[32,128,256]{2,1,0:T(8,128)(2,1)} %bitcast.52), custom_call_target="tpu_custom_call" | custom-call | bytes 4194304 | tf_op jit(solution)/shard_map/payload/pallas_call | solution.py:301
  11.5 15.9 %all-to-all-start.1 = ((bf16[16,200,256]{2,1,0:T(8,128)(2,1)}), bf16[16,200,256]{2,1,0:T(8,128)(2,1)}, u32[]{:S(2)}, u32[]{:S(2)}) async-start(bf16[16,200,256]{2,1,0:T(8,128)(2,1)} %payload.1), calls=%async_computation.1 | async-start | bytes 3276800 | tf_op jit(solution)/shard_map/all_to_all | solution.py:346
  27.5 4.8 %collective-permute-start = (bf16[8,3072]{1,0:T(8,128)(2,1)S(1)}, bf16[8,3072]{1,0:T(8,128)(2,1)S(1)}, u32[]{:S(2)}, u32[]{:S(2)}) collective-permute-start(bf16[8,3072]{1,0:T(8,128)(2,1)S(1)} %get-tuple-element.42), channel_id=1, source_target_pairs={{0,16},{16,0},{1,17},{17,1},{2,18},{18,2},{3,19},{19,3},{4,20},{20... | collective-permute-start | bytes 147464 | tf_op jit(solution)/shard_map/ppermute | solution.py:351
  32.4 1.5 collective-permute-done
  33.9 0.6 pad_maximum_fusion.1
  34.6 0.1 select_reduce_fusion.1
  34.8 0.1 add_select_fusion.3
  34.9 0.1 eq.21
  35.0 0.1 fusion.8
  35.2 0.1 pad_add_fusion
  35.3 0.1 select_reduce_fusion
  35.4 0.1 fusion.19
  35.5 0.2 convolution_convert_fusion
  35.7 94.3 %all_gather.7 = bf16[256,640]{1,0:T(8,128)(2,1)S(1)} all-gather(bf16[16,640]{1,0:T(8,128)(2,1)S(1)} %pad_maximum_fusion.2), channel_id=1, replica_groups={{15,14,13,12,11,10,9,8,7,6,5,4,3,2,1,0},{31,30,29,28,27,26,25,24,23,22,..., dimensions={0}, use_global_device_ids=true | all-gather | bytes 348160 | tf_op jit(solution)/shard_map/all_gather | solution.py:373
  130.0 1.6 all-gather.2.cloned.1.call-done
  131.6 1.4 slice_reduce_fusion
  133.6 12.5 %conditional.1 = ((f32[16,16,2048]{2,1,0:T(8,128)S(1)}, s16[16,16,2176]{2,1,0:T(8,128)(2,1)})) conditional(s32[]{:T(128)} %convert_element_type.6, (s32[4]{0:T(128)S(1)}, bf16[256,3072]{1,0:T(8,128)(2,1)}, bf16[256,640]{1,0:T(8,128)(2,1)S(1)}, bf16[16,200,256]{2,1,0:T(8,128)(2,1)}) %tuple.11, (bf16[1,1,32,128,256]{4,3,2,1,0:T(8,128)(2,1)S(1)}, ...), branch_computations={%region_3.4_spmd, %region_4.5_spmd} | conditional | flops 4303708160 | bytes 22941732 | solution.py:389
  133.6 12.5 %lean_tiles.1 = (f32[16,16,2048]{2,1,0:T(8,128)S(1)}, s16[16,16,2176]{2,1,0:T(8,128)(2,1)}) custom-call(s32[4]{0:T(128)S(1)} %get-tuple-element.25.place_ref, bf16[256,3072]{1,0:T(8,128)(2,1)} %get-tuple-element.26.q_ref, bf16[256,640]{1,0:T(8,128)(2,1)S(1)} %get-tuple-element.27.deep_ref.far_ref, bf16[256,640]{1,0:T(8,128)(2,1)S(1)} %get-tuple-element.27.deep_ref.far_ref, ...), custom_call_target="tpu_custom_call" | custom-call | flops 4294967296 | bytes 3211264 | tf_op jit(solution)/shard_map/cond/branch_0_fun/lean_tiles/pallas_call | solution.py:168
  146.1 7.7 %collective-permute-start.1 = (s16[16,16,2176]{2,1,0:T(8,128)(2,1)}, s16[16,16,2176]{2,1,0:T(8,128)(2,1)S(1)}, u32[]{:S(2)}, u32[]{:S(2)}) collective-permute-start(s16[16,16,2176]{2,1,0:T(8,128)(2,1)} %get-tuple-element.38), channel_id=1, source_target_pairs={{0,32},{32,0},{1,33},{33,1},{2,34},{34,2},{3,35},{35,3},{4,36},{36... | collective-permute-start | bytes 3342344 | tf_op jit(solution)/shard_map/ppermute | solution.py:390
  153.8 2.6 %collective-permute-done.1.got_ref = s16[16,16,2176]{2,1,0:T(8,128)(2,1)S(1)} collective-permute-done((s16[16,16,2176]{2,1,0:T(8,128)(2,1)}, s16[16,16,2176]{2,1,0:T(8,128)(2,1)S(1)}, u32[]{:S(2)}, u32[]{:S(2)}) %collective-permute-start.1) | collective-permute-done | bytes 1114144 | tf_op jit(solution)/shard_map/ppermute | solution.py:390
  156.4 2.6 %merge.1 = s16[16,16,2176]{2,1,0:T(8,128)(2,1)S(1)} custom-call(f32[16,16,2048]{2,1,0:T(8,128)S(1)} %get-tuple-element.37.keep_ref, s16[16,16,2176]{2,1,0:T(8,128)(2,1)S(1)} %collective-permute-done.1.got_ref), custom_call_target="tpu_custom_call" | custom-call | tf_op jit(solution)/shard_map/merge/pallas_call | solution.py:75
  159.0 24.2 %all_to_all.15.p_ref = s16[16,16,2176]{2,1,0:T(8,128)(2,1)S(1)} all-to-all(s16[16,16,2176]{2,1,0:T(8,128)(2,1)S(1)} %merge.1), channel_id=1, replica_groups=mesh['chip'=8,'core'=2,'y'=2,'z'=16] {'chip','y'}, dimensions={0} | all-to-all | bytes 2228224 | tf_op jit(solution)/shard_map/all_to_all | solution.py:392
  183.1 1.0 sum_parts.1
  (23 shorter events, 0.4 us)
Async XLA Ops:
  6.5 0.7 copy-start
  11.5 16.0 %copy-start.4 = (bf16[8,6144]{1,0:T(8,128)(2,1)S(1)}, bf16[8,6144]{1,0:T(8,128)(2,1)}, u32[]{:S(2)}) copy-start(bf16[8,6144]{1,0:T(8,128)(2,1)} %param.6) | copy-start | bytes 294916
  11.5 23.1 %copy-start.2 = (bf16[1,1,32,128,256]{4,3,2,1,0:T(8,128)(2,1)S(1)}, bf16[1,1,32,128,256]{4,3,2,1,0:T(8,128)(2,1)}, u32[]{:S(2)}) copy-start(bf16[1,1,32,128,256]{4,3,2,1,0:T(8,128)(2,1)} %param.7) | copy-start | bytes 6291460
  11.5 23.1 %copy-start.1 = (s32[1,1,32]{2,1,0:T(1,128)S(1)}, s32[1,1,32]{2,1,0:T(1,128)}, u32[]{:S(2)}) copy-start(s32[1,1,32]{2,1,0:T(1,128)} %param.9) | copy-start | bytes 388
  11.5 23.5 %copy-start.3 = (s32[1,1,32,128]{3,2,1,0:T(8,128)S(1)}, s32[1,1,32,128]{3,2,1,0:T(8,128)}, u32[]{:S(2)}) copy-start(s32[1,1,32,128]{3,2,1,0:T(8,128)} %param.8) | copy-start | bytes 49156
  11.5 120.1 %all-to-all-start.1 = ((bf16[16,200,256]{2,1,0:T(8,128)(2,1)}), bf16[16,200,256]{2,1,0:T(8,128)(2,1)}, u32[]{:S(2)}, u32[]{:S(2)}) async-start(bf16[16,200,256]{2,1,0:T(8,128)(2,1)} %payload.1), calls=%async_computation.1 | async-start | bytes 3276800 | tf_op jit(solution)/shard_map/all_to_all | solution.py:346
  27.4 104.1 %all-gather.2.cloned.1.call-start = ((), (), s32[]{:S(2)}) async-start(), calls=%async_computation.3 | async-start | bytes 1671168 | tf_op jit(solution)/shard_map/all_gather | solution.py:352
  27.5 6.3 %collective-permute-start = (bf16[8,3072]{1,0:T(8,128)(2,1)S(1)}, bf16[8,3072]{1,0:T(8,128)(2,1)S(1)}, u32[]{:S(2)}, u32[]{:S(2)}) collective-permute-start(bf16[8,3072]{1,0:T(8,128)(2,1)S(1)} %get-tuple-element.42), channel_id=1, source_target_pairs={{0,16},{16,0},{1,17},{17,1},{2,18},{18,2},{3,19},{19,3},{4,20},{20... | collective-permute-start | bytes 147464 | tf_op jit(solution)/shard_map/ppermute | solution.py:351
  146.1 10.3 %collective-permute-start.1 = (s16[16,16,2176]{2,1,0:T(8,128)(2,1)}, s16[16,16,2176]{2,1,0:T(8,128)(2,1)S(1)}, u32[]{:S(2)}, u32[]{:S(2)}) collective-permute-start(s16[16,16,2176]{2,1,0:T(8,128)(2,1)} %get-tuple-element.38), channel_id=1, source_target_pairs={{0,32},{32,0},{1,33},{33,1},{2,34},{34,2},{3,35},{35,3},{4,36},{36... | collective-permute-start | bytes 3342344 | tf_op jit(solution)/shard_map/ppermute | solution.py:390
Sparse Core Ops, SparseCore 0:
  34.7 96.8 all-gather.1

commit v9 on v8

--- a/solution.py
+++ b/solution.py
@@ -283,7 +283,7 @@
         o_ref[r, base:, :] = meta.astype(jnp.bfloat16)
 
 
-def payload(counts, first, slots, values, *, blocks, per_step=4):
+def payload(counts, first, slots, values, *, blocks, per_step=8):
     owners, cap, width = values.shape
     z_size = owners // HALVES
     depth = HALVES * SHALLOW + TILE
@@ -293,8 +293,8 @@
         grid=(steps,),
         in_specs=[
             pl.BlockSpec(slots.shape, lambda i, *_: (0, 0)),
-            pl.BlockSpec((per_step, cap, width), lambda i, *_: (i, 0, 0)),
-            pl.BlockSpec((per_step, cap, width), lambda i, *_: (i + steps, 0, 0)),
+            pl.BlockSpec((per_step, SHALLOW, width), lambda i, *_: (i, 0, 0)),
+            pl.BlockSpec((per_step, SHALLOW, width), lambda i, *_: (i + steps, 0, 0)),
         ],
         out_specs=pl.BlockSpec((per_step, depth, width), lambda i, *_: (i, 0, 0)),
     )

time: 191 us -> 190 us (level)
  no operation moved by 1% of the time
where the time goes in v9:
time: 190 us
  blocking collectives  118 us (62%)
  starting transfers between devices  28.5 us (15%)
  Pallas kernels  19 us (10%)
  between operations  14.2 us (7%)
  waiting for transfers between devices  5.68 us (3%)
  other arithmetic  2.73 us (1%)
    all_gather x1, blocking collectives, per_device(): lax.all_gather(beside, 'z', axis=0, tiled=True, axis_index_groups=downward)  94.3 us
    all_to_all x1, blocking collectives, per_device(): lax.all_to_all(coded, ('chip', 'y'), split_axis=0, concat_axis=0, tiled=T...  24.2 us
    all_to_all x1, starting transfers between devices, per_device(): rows = lax.all_to_all(sent, 'z', split_axis=0, concat_axis=0, tiled=True)  15.9 us
    pallas_call x1, Pallas kernels, lean_tiles(): pl.pallas_call(functools.partial(lean_kernel, cap=cap, span=span, per_ste...  12.5 us
    ppermute x1, starting transfers between devices, per_device(): got = lax.ppermute(give, 'core', [(0, 1), (1, 0)])  7.71 us
    ppermute x1, starting transfers between devices, per_device(): mirror = lax.ppermute(theirs, 'y', [(0, 1), (1, 0)])  4.82 us
  transfers between devices with their start and end apart: 4, of which 3 were waited for; matrix products, arithmetic and copies ran while one was open for 1% of the time, Pallas kernels for 0%

profile of v9, /device:TPU:1, one launch (start us, length us, event | category | flops | bytes accessed | tf_op | source)
XLA Modules:
  0.0 189.6 jit_solution(13599814550335713051)
XLA Ops:
  6.5 0.7 copy-done
  7.2 2.9 %payload.1 = bf16[16,200,256]{2,1,0:T(8,128)(2,1)} custom-call(s32[32]{0:T(128)S(1)} %bitcast.49, s32[1]{0:T(128)} %bitcast.5.first_ref, s32[32,128]{1,0:T(8,128)} %bitcast.54, bf16[32,128,256]{2,1,0:T(8,128)(2,1)} %bitcast.51, bf16[32,128,256]{2,1,0:T(8,128)(2,1)} %bitcast.52), custom_call_target="tpu_custom_call" | custom-call | bytes 4194304 | tf_op jit(solution)/shard_map/payload/pallas_call | solution.py:301
  10.1 15.9 %all-to-all-start.1 = ((bf16[16,200,256]{2,1,0:T(8,128)(2,1)}), bf16[16,200,256]{2,1,0:T(8,128)(2,1)}, u32[]{:S(2)}, u32[]{:S(2)}) async-start(bf16[16,200,256]{2,1,0:T(8,128)(2,1)} %payload.1), calls=%async_computation.1 | async-start | bytes 3276800 | tf_op jit(solution)/shard_map/all_to_all | solution.py:346
  26.2 4.8 %collective-permute-start = (bf16[8,3072]{1,0:T(8,128)(2,1)S(1)}, bf16[8,3072]{1,0:T(8,128)(2,1)S(1)}, u32[]{:S(2)}, u32[]{:S(2)}) collective-permute-start(bf16[8,3072]{1,0:T(8,128)(2,1)S(1)} %get-tuple-element.42), channel_id=1, source_target_pairs={{0,16},{16,0},{1,17},{17,1},{2,18},{18,2},{3,19},{19,3},{4,20},{20... | collective-permute-start | bytes 147464 | tf_op jit(solution)/shard_map/ppermute | solution.py:351
  31.0 1.5 collective-permute-done
  32.5 0.6 pad_maximum_fusion.1
  33.3 0.1 select_reduce_fusion.1
  33.4 0.1 add_select_fusion.3
  33.5 0.1 eq.21
  33.7 0.1 fusion.8
  33.8 0.1 pad_add_fusion
  33.9 0.1 select_reduce_fusion
  34.1 0.1 fusion.19
  34.1 0.2 convolution_convert_fusion
  34.4 94.3 %all_gather.7 = bf16[256,640]{1,0:T(8,128)(2,1)S(1)} all-gather(bf16[16,640]{1,0:T(8,128)(2,1)S(1)} %pad_maximum_fusion.2), channel_id=1, replica_groups={{15,14,13,12,11,10,9,8,7,6,5,4,3,2,1,0},{31,30,29,28,27,26,25,24,23,22,..., dimensions={0}, use_global_device_ids=true | all-gather | bytes 348160 | tf_op jit(solution)/shard_map/all_gather | solution.py:373
  128.6 1.6 all-gather.2.cloned.1.call-done
  130.2 1.4 slice_reduce_fusion
  132.3 12.5 %conditional.1 = ((f32[16,16,2048]{2,1,0:T(8,128)S(1)}, s16[16,16,2176]{2,1,0:T(8,128)(2,1)})) conditional(s32[]{:T(128)} %convert_element_type.6, (s32[4]{0:T(128)S(1)}, bf16[256,3072]{1,0:T(8,128)(2,1)}, bf16[256,640]{1,0:T(8,128)(2,1)S(1)}, bf16[16,200,256]{2,1,0:T(8,128)(2,1)}) %tuple.11, (bf16[1,1,32,128,256]{4,3,2,1,0:T(8,128)(2,1)S(1)}, ...), branch_computations={%region_3.4_spmd, %region_4.5_spmd} | conditional | flops 4303708160 | bytes 22941732 | solution.py:389
  132.3 12.5 %lean_tiles.1 = (f32[16,16,2048]{2,1,0:T(8,128)S(1)}, s16[16,16,2176]{2,1,0:T(8,128)(2,1)}) custom-call(s32[4]{0:T(128)S(1)} %get-tuple-element.25.place_ref, bf16[256,3072]{1,0:T(8,128)(2,1)} %get-tuple-element.26.q_ref, bf16[256,640]{1,0:T(8,128)(2,1)S(1)} %get-tuple-element.27.deep_ref.far_ref, bf16[256,640]{1,0:T(8,128)(2,1)S(1)} %get-tuple-element.27.deep_ref.far_ref, ...), custom_call_target="tpu_custom_call" | custom-call | flops 4294967296 | bytes 3211264 | tf_op jit(solution)/shard_map/cond/branch_0_fun/lean_tiles/pallas_call | solution.py:168
  144.7 7.7 %collective-permute-start.1 = (s16[16,16,2176]{2,1,0:T(8,128)(2,1)}, s16[16,16,2176]{2,1,0:T(8,128)(2,1)S(1)}, u32[]{:S(2)}, u32[]{:S(2)}) collective-permute-start(s16[16,16,2176]{2,1,0:T(8,128)(2,1)} %get-tuple-element.38), channel_id=1, source_target_pairs={{0,32},{32,0},{1,33},{33,1},{2,34},{34,2},{3,35},{35,3},{4,36},{36... | collective-permute-start | bytes 3342344 | tf_op jit(solution)/shard_map/ppermute | solution.py:390
  152.4 2.6 %collective-permute-done.1.got_ref = s16[16,16,2176]{2,1,0:T(8,128)(2,1)S(1)} collective-permute-done((s16[16,16,2176]{2,1,0:T(8,128)(2,1)}, s16[16,16,2176]{2,1,0:T(8,128)(2,1)S(1)}, u32[]{:S(2)}, u32[]{:S(2)}) %collective-permute-start.1) | collective-permute-done | bytes 1114144 | tf_op jit(solution)/shard_map/ppermute | solution.py:390
  155.0 2.6 %merge.1 = s16[16,16,2176]{2,1,0:T(8,128)(2,1)S(1)} custom-call(f32[16,16,2048]{2,1,0:T(8,128)S(1)} %get-tuple-element.37.keep_ref, s16[16,16,2176]{2,1,0:T(8,128)(2,1)S(1)} %collective-permute-done.1.got_ref), custom_call_target="tpu_custom_call" | custom-call | tf_op jit(solution)/shard_map/merge/pallas_call | solution.py:75
  157.6 24.2 %all_to_all.15.p_ref = s16[16,16,2176]{2,1,0:T(8,128)(2,1)S(1)} all-to-all(s16[16,16,2176]{2,1,0:T(8,128)(2,1)S(1)} %merge.1), channel_id=1, replica_groups=mesh['chip'=8,'core'=2,'y'=2,'z'=16] {'chip','y'}, dimensions={0} | all-to-all | bytes 2228224 | tf_op jit(solution)/shard_map/all_to_all | solution.py:392
  181.8 1.0 sum_parts.1
  (23 shorter events, 0.4 us)
Async XLA Ops:
  6.5 0.7 copy-start
  10.1 16.0 %copy-start.4 = (bf16[8,6144]{1,0:T(8,128)(2,1)S(1)}, bf16[8,6144]{1,0:T(8,128)(2,1)}, u32[]{:S(2)}) copy-start(bf16[8,6144]{1,0:T(8,128)(2,1)} %param.6) | copy-start | bytes 294916
  10.1 23.1 %copy-start.2 = (bf16[1,1,32,128,256]{4,3,2,1,0:T(8,128)(2,1)S(1)}, bf16[1,1,32,128,256]{4,3,2,1,0:T(8,128)(2,1)}, u32[]{:S(2)}) copy-start(bf16[1,1,32,128,256]{4,3,2,1,0:T(8,128)(2,1)} %param.7) | copy-start | bytes 6291460
  10.1 23.1 %copy-start.1 = (s32[1,1,32]{2,1,0:T(1,128)S(1)}, s32[1,1,32]{2,1,0:T(1,128)}, u32[]{:S(2)}) copy-start(s32[1,1,32]{2,1,0:T(1,128)} %param.9) | copy-start | bytes 388
  10.1 23.5 %copy-start.3 = (s32[1,1,32,128]{3,2,1,0:T(8,128)S(1)}, s32[1,1,32,128]{3,2,1,0:T(8,128)}, u32[]{:S(2)}) copy-start(s32[1,1,32,128]{3,2,1,0:T(8,128)} %param.8) | copy-start | bytes 49156
  10.1 120.1 %all-to-all-start.1 = ((bf16[16,200,256]{2,1,0:T(8,128)(2,1)}), bf16[16,200,256]{2,1,0:T(8,128)(2,1)}, u32[]{:S(2)}, u32[]{:S(2)}) async-start(bf16[16,200,256]{2,1,0:T(8,128)(2,1)} %payload.1), calls=%async_computation.1 | async-start | bytes 3276800 | tf_op jit(solution)/shard_map/all_to_all | solution.py:346
  26.1 104.1 %all-gather.2.cloned.1.call-start = ((), (), s32[]{:S(2)}) async-start(), calls=%async_computation.3 | async-start | bytes 1671168 | tf_op jit(solution)/shard_map/all_gather | solution.py:352
  26.2 6.3 %collective-permute-start = (bf16[8,3072]{1,0:T(8,128)(2,1)S(1)}, bf16[8,3072]{1,0:T(8,128)(2,1)S(1)}, u32[]{:S(2)}, u32[]{:S(2)}) collective-permute-start(bf16[8,3072]{1,0:T(8,128)(2,1)S(1)} %get-tuple-element.42), channel_id=1, source_target_pairs={{0,16},{16,0},{1,17},{17,1},{2,18},{18,2},{3,19},{19,3},{4,20},{20... | collective-permute-start | bytes 147464 | tf_op jit(solution)/shard_map/ppermute | solution.py:351
  144.7 10.3 %collective-permute-start.1 = (s16[16,16,2176]{2,1,0:T(8,128)(2,1)}, s16[16,16,2176]{2,1,0:T(8,128)(2,1)S(1)}, u32[]{:S(2)}, u32[]{:S(2)}) collective-permute-start(s16[16,16,2176]{2,1,0:T(8,128)(2,1)} %get-tuple-element.38), channel_id=1, source_target_pairs={{0,32},{32,0},{1,33},{33,1},{2,34},{34,2},{3,35},{35,3},{4,36},{36... | collective-permute-start | bytes 3342344 | tf_op jit(solution)/shard_map/ppermute | solution.py:390
Sparse Core Ops, SparseCore 0:
  33.3 96.8 all-gather.1

commit v10 on v9

--- a/solution.py
+++ b/solution.py
@@ -263,10 +263,6 @@
     here, z_size = low_ref.shape[0], low_ref.shape[0] * pl.num_programs(0)
     lane = lax.broadcasted_iota(jnp.int32, (1, slots_ref.shape[1]), 1)
     base = HALVES * shallow
-    beyond = jnp.int32(0)
-    for owner in range(slots_ref.shape[0]):
-        beyond += jnp.maximum(counts_ref[owner] - shallow, 0)
-    crowded = jnp.where(beyond > EXTRA, 1.0, 0.0)
     for r in range(here):
         z = step * here + r
         docs, ids = [], []
@@ -276,7 +272,7 @@
             doc = lax.shift_right_logical(slots, blocks.bit_length() - 1) - first_ref[0]
             docs.append(doc.astype(jnp.float32))
             ids.append(jnp.where(lane < counts_ref[owner], slots & (blocks - 1), DEAD).astype(jnp.float32))
-        rest = jnp.full((TILE - 2, o_ref.shape[2]), crowded)
+        rest = jnp.zeros((TILE - 2, o_ref.shape[2]), jnp.float32)
         meta = jnp.concatenate([jnp.concatenate(docs, axis=1), jnp.concatenate(ids, axis=1), rest], axis=0)
         o_ref[r, :shallow, :] = low_ref[r, :shallow, :]
         o_ref[r, shallow:base, :] = high_ref[r, :shallow, :]
@@ -366,8 +362,9 @@
     packed = jnp.sum(jnp.where(taken, packed[:, SHALLOW:].reshape(1, owners * depth), 0), axis=1)
     code = jnp.maximum(packed - 1, 0)
     target = jnp.where(packed > 0, code // (span * blocks), DEAD)
-    far = jnp.stack([code % (span * blocks) // blocks, code % blocks, target]).astype(jnp.bfloat16)
-    far = jnp.pad(far, ((0, 16 - 3), (SHALLOW, LANES - SHALLOW - EXTRA)))
+    crowded = jnp.broadcast_to((jnp.sum(beyond) > EXTRA).astype(jnp.int32), (EXTRA,))
+    far = jnp.stack([code % (span * blocks) // blocks, code % blocks, target, crowded]).astype(jnp.bfloat16)
+    far = jnp.pad(far, ((0, 16 - 4), (SHALLOW, LANES - SHALLOW - EXTRA)))
     beside = jnp.concatenate([deep[g : g + 16] for g in range(0, EXTRA, 16)] + [far], axis=1)
     downward = [list(range(z_size - 1, -1, -1))]
     beside = lax.all_gather(beside, "z", axis=0, tiled=True, axis_index_groups=downward)
@@ -385,7 +382,7 @@
         rows = lax.all_to_all(sent, "z", split_axis=0, concat_axis=0, tiled=True)
         return partial_tiles(place, queries, rows, cap=cap, span=span, blocks=blocks)
 
-    flags = rows[:, HALVES * SHALLOW + TILE - 1, 0].astype(jnp.float32)
+    flags = beside[:, -LANES:].reshape(z_size, 16, LANES)[:, 3, SHALLOW].astype(jnp.float32)
     keep, give = lax.cond(jnp.max(flags) > 0.5, full, lean, home, queries, beside, rows, row_values)
     got = lax.ppermute(give, "core", [(0, 1), (1, 0)])
     coded = merged(keep, got, blocks=blocks)

time: 190 us -> 188 us (0.989)
  transfers between devices with their start and end apart: 4 -> 4, of which waited for: 3 -> 2; matrix products, arithmetic and copies ran while one was open for 1% -> 2% of each run, Pallas kernels for 0% -> 0%
where the time goes in v10:
time: 188 us
  blocking collectives  117 us (62%)
  starting transfers between devices  29.3 us (16%)
  Pallas kernels  19 us (10%)
  between operations  14.8 us (8%)
  waiting for transfers between devices  4.1 us (2%)
  other arithmetic  2.81 us (1%)
    all_gather x1, blocking collectives, per_device(): lax.all_gather(beside, 'z', axis=0, tiled=True, axis_index_groups=downward)  93.6 us
    all_to_all x1, blocking collectives, per_device(): lax.all_to_all(coded, ('chip', 'y'), split_axis=0, concat_axis=0, tiled=T...  23.4 us
    all_to_all x1, starting transfers between devices, per_device(): rows = lax.all_to_all(sent, 'z', split_axis=0, concat_axis=0, tiled=True)  15.9 us
    pallas_call x1, Pallas kernels, lean_tiles(): pl.pallas_call(functools.partial(lean_kernel, cap=cap, span=span, per_ste...  12.5 us
    ppermute x1, starting transfers between devices, per_device(): got = lax.ppermute(give, 'core', [(0, 1), (1, 0)])  8.48 us
    ppermute x1, starting transfers between devices, per_device(): mirror = lax.ppermute(theirs, 'y', [(0, 1), (1, 0)])  4.82 us
  transfers between devices with their start and end apart: 4, of which 2 were waited for; matrix products, arithmetic and copies ran while one was open for 2% of the time, Pallas kernels for 0%

profile of v10, /device:TPU:1, one launch (start us, length us, event | category | flops | bytes accessed | tf_op | source)
XLA Modules:
  0.0 188.1 jit_solution(7485002239480494513)
XLA Ops:
  6.5 0.7 copy-done
  7.2 2.9 %payload.1 = bf16[16,200,256]{2,1,0:T(8,128)(2,1)} custom-call(s32[32]{0:T(128)S(1)} %bitcast.53, s32[1]{0:T(128)} %bitcast.16.first_ref, s32[32,128]{1,0:T(8,128)} %bitcast.58, bf16[32,128,256]{2,1,0:T(8,128)(2,1)} %bitcast.55, bf16[32,128,256]{2,1,0:T(8,128)(2,1)} %bitcast.56), custom_call_target="tpu_custom_call" | custom-call | bytes 4194304 | tf_op jit(solution)/shard_map/payload/pallas_call | solution.py:297
  10.1 15.9 %all-to-all-start.1 = ((bf16[16,200,256]{2,1,0:T(8,128)(2,1)}), bf16[16,200,256]{2,1,0:T(8,128)(2,1)}, u32[]{:S(2)}, u32[]{:S(2)}) async-start(bf16[16,200,256]{2,1,0:T(8,128)(2,1)} %payload.1), calls=%async_computation.1 | async-start | bytes 3276800 | tf_op jit(solution)/shard_map/all_to_all | solution.py:342
  26.1 4.8 %collective-permute-start = (bf16[8,3072]{1,0:T(8,128)(2,1)S(1)}, bf16[8,3072]{1,0:T(8,128)(2,1)S(1)}, u32[]{:S(2)}, u32[]{:S(2)}) collective-permute-start(bf16[8,3072]{1,0:T(8,128)(2,1)S(1)} %get-tuple-element.42), channel_id=1, source_target_pairs={{0,16},{16,0},{1,17},{17,1},{2,18},{18,2},{3,19},{19,3},{4,20},{20... | collective-permute-start | bytes 147464 | tf_op jit(solution)/shard_map/ppermute | solution.py:347
  31.0 1.5 collective-permute-done
  32.5 0.6 pad_maximum_fusion.1
  33.2 0.7 fusion.17
  34.5 0.1 select_reduce_fusion.1
  34.7 0.1 add_select_fusion.3
  34.8 0.1 eq.21
  34.9 0.1 fusion.10
  35.2 0.1 select_reduce_fusion
  35.4 0.2 convolution_convert_fusion
  35.6 0.1 fusion.7
  35.7 93.6 %all_gather.6 = bf16[256,640]{1,0:T(8,128)(2,1)S(1)} all-gather(bf16[16,640]{1,0:T(8,128)(2,1)S(1)} %fusion.7), channel_id=1, replica_groups={{15,14,13,12,11,10,9,8,7,6,5,4,3,2,1,0},{31,30,29,28,27,26,25,24,23,22,..., dimensions={0}, use_global_device_ids=true | all-gather | bytes 348160 | tf_op jit(solution)/shard_map/all_gather | solution.py:370
  129.2 0.7 slice_reduce_fusion
  130.6 0.1 pad_add_fusion
  130.7 12.5 %conditional.1 = ((f32[16,16,2048]{2,1,0:T(8,128)S(1)}, s16[16,16,2176]{2,1,0:T(8,128)(2,1)})) conditional(s32[]{:T(128)} %convert_element_type.17, (s32[4]{0:T(128)S(1)}, bf16[256,3072]{1,0:T(8,128)(2,1)}, bf16[256,640]{1,0:T(8,128)(2,1)S(1)}, bf16[16,200,256]{2,1,0:T(8,128)(2,1)}) %tuple.11, (bf16[1,1,32,128,256]{4,3,2,1,0:T(8,128)(2,1)S(1)}, ...), branch_computations={%region_4.5_spmd, %region_5.6_spmd} | conditional | flops 4303708160 | bytes 22941732 | solution.py:386
  130.7 12.5 %lean_tiles.1 = (f32[16,16,2048]{2,1,0:T(8,128)S(1)}, s16[16,16,2176]{2,1,0:T(8,128)(2,1)}) custom-call(s32[4]{0:T(128)S(1)} %get-tuple-element.25.place_ref, bf16[256,3072]{1,0:T(8,128)(2,1)} %get-tuple-element.26.q_ref, bf16[256,640]{1,0:T(8,128)(2,1)S(1)} %get-tuple-element.27.deep_ref.far_ref, bf16[256,640]{1,0:T(8,128)(2,1)S(1)} %get-tuple-element.27.deep_ref.far_ref, ...), custom_call_target="tpu_custom_call" | custom-call | flops 4294967296 | bytes 3211264 | tf_op jit(solution)/shard_map/cond/branch_0_fun/lean_tiles/pallas_call | solution.py:168
  143.1 8.5 %collective-permute-start.1 = (s16[16,16,2176]{2,1,0:T(8,128)(2,1)}, s16[16,16,2176]{2,1,0:T(8,128)(2,1)S(1)}, u32[]{:S(2)}, u32[]{:S(2)}) collective-permute-start(s16[16,16,2176]{2,1,0:T(8,128)(2,1)} %get-tuple-element.38), channel_id=1, source_target_pairs={{0,32},{32,0},{1,33},{33,1},{2,34},{34,2},{3,35},{35,3},{4,36},{36... | collective-permute-start | bytes 3342344 | tf_op jit(solution)/shard_map/ppermute | solution.py:387
  151.6 2.6 %collective-permute-done.1.got_ref = s16[16,16,2176]{2,1,0:T(8,128)(2,1)S(1)} collective-permute-done((s16[16,16,2176]{2,1,0:T(8,128)(2,1)}, s16[16,16,2176]{2,1,0:T(8,128)(2,1)S(1)}, u32[]{:S(2)}, u32[]{:S(2)}) %collective-permute-start.1) | collective-permute-done | bytes 1114144 | tf_op jit(solution)/shard_map/ppermute | solution.py:387
  154.2 2.6 %merge.1 = s16[16,16,2176]{2,1,0:T(8,128)(2,1)S(1)} custom-call(f32[16,16,2048]{2,1,0:T(8,128)S(1)} %get-tuple-element.37.keep_ref, s16[16,16,2176]{2,1,0:T(8,128)(2,1)S(1)} %collective-permute-done.1.got_ref), custom_call_target="tpu_custom_call" | custom-call | tf_op jit(solution)/shard_map/merge/pallas_call | solution.py:75
  156.8 23.4 %all_to_all.15.p_ref = s16[16,16,2176]{2,1,0:T(8,128)(2,1)S(1)} all-to-all(s16[16,16,2176]{2,1,0:T(8,128)(2,1)S(1)} %merge.1), channel_id=1, replica_groups=mesh['chip'=8,'core'=2,'y'=2,'z'=16] {'chip','y'}, dimensions={0} | all-to-all | bytes 2228224 | tf_op jit(solution)/shard_map/all_to_all | solution.py:389
  180.2 1.0 sum_parts.1
  (25 shorter events, 0.5 us)
Async XLA Ops:
  6.5 0.7 copy-start
  10.1 16.0 %copy-start.4 = (bf16[8,6144]{1,0:T(8,128)(2,1)S(1)}, bf16[8,6144]{1,0:T(8,128)(2,1)}, u32[]{:S(2)}) copy-start(bf16[8,6144]{1,0:T(8,128)(2,1)} %param.6) | copy-start | bytes 294916
  10.1 23.1 %copy-start.1 = (s32[1,1,32]{2,1,0:T(1,128)S(1)}, s32[1,1,32]{2,1,0:T(1,128)}, u32[]{:S(2)}) copy-start(s32[1,1,32]{2,1,0:T(1,128)} %param.9) | copy-start | bytes 388
  10.1 23.7 %copy-start.2 = (bf16[1,1,32,128,256]{4,3,2,1,0:T(8,128)(2,1)S(1)}, bf16[1,1,32,128,256]{4,3,2,1,0:T(8,128)(2,1)}, u32[]{:S(2)}) copy-start(bf16[1,1,32,128,256]{4,3,2,1,0:T(8,128)(2,1)} %param.7) | copy-start | bytes 6291460
  10.1 24.8 %copy-start.3 = (s32[1,1,32,128]{3,2,1,0:T(8,128)S(1)}, s32[1,1,32,128]{3,2,1,0:T(8,128)}, u32[]{:S(2)}) copy-start(s32[1,1,32,128]{3,2,1,0:T(8,128)} %param.8) | copy-start | bytes 49156
  10.1 120.6 %all-to-all-start.1 = ((bf16[16,200,256]{2,1,0:T(8,128)(2,1)}), bf16[16,200,256]{2,1,0:T(8,128)(2,1)}, u32[]{:S(2)}, u32[]{:S(2)}) async-start(bf16[16,200,256]{2,1,0:T(8,128)(2,1)} %payload.1), calls=%async_computation.1 | async-start | bytes 3276800 | tf_op jit(solution)/shard_map/all_to_all | solution.py:342
  26.1 104.6 %all-gather.2.cloned.1.call-start = ((), (), s32[]{:S(2)}) async-start(), calls=%async_computation.3 | async-start | bytes 1671168 | tf_op jit(solution)/shard_map/all_gather | solution.py:348
  26.1 6.3 %collective-permute-start = (bf16[8,3072]{1,0:T(8,128)(2,1)S(1)}, bf16[8,3072]{1,0:T(8,128)(2,1)S(1)}, u32[]{:S(2)}, u32[]{:S(2)}) collective-permute-start(bf16[8,3072]{1,0:T(8,128)(2,1)S(1)} %get-tuple-element.42), channel_id=1, source_target_pairs={{0,16},{16,0},{1,17},{17,1},{2,18},{18,2},{3,19},{19,3},{4,20},{20... | collective-permute-start | bytes 147464 | tf_op jit(solution)/shard_map/ppermute | solution.py:347
  143.1 11.1 %collective-permute-start.1 = (s16[16,16,2176]{2,1,0:T(8,128)(2,1)}, s16[16,16,2176]{2,1,0:T(8,128)(2,1)S(1)}, u32[]{:S(2)}, u32[]{:S(2)}) collective-permute-start(s16[16,16,2176]{2,1,0:T(8,128)(2,1)} %get-tuple-element.38), channel_id=1, source_target_pairs={{0,32},{32,0},{1,33},{33,1},{2,34},{34,2},{3,35},{35,3},{4,36},{36... | collective-permute-start | bytes 3342344 | tf_op jit(solution)/shard_map/ppermute | solution.py:387
Sparse Core Ops, SparseCore 0:
  33.3 96.9 all-gather.1
